TPU v7x, 32 devices: a whole 2x2x4 slice. The times are simulated.
32 devices in a mesh: seq: 8 (over z, x), fsdp: 4 (over y, core).
Axes of the slice: x: 2, y: 2, z: 4, core: 2. Of those that a mesh axis runs over, the one named last changes fastest.
Arguments:
- tokens: bfloat16 [4, 1024, 1024], P('fsdp', 'seq'), may hold values from -6 to 6
- cotangent: bfloat16 [4, 1024, 1024], P('fsdp', 'seq'), may hold values from -6 to 6
- segments: int32 [4, 1024], P('fsdp', 'seq'), may hold values from 0 to 7, never falling along the last dimension, each value on 1 to 512 neighbouring positions
- weight_in: float32 [6144, 1024], P('fsdp'), may hold values from -0.1875 to 0.1875
- weight_out: float32 [2048, 1024], P('fsdp'), may hold values from -0.1875 to 0.1875
- weight_up: float32 [5632, 1024], P('fsdp'), may hold values from -0.1875 to 0.1875
- weight_down: float32 [2816, 1024], P('fsdp'), may hold values from -0.21875 to 0.21875
- vectors: float32 [35088], replicated, may hold values from -14 to 3, as said below
- momentum_in: float32 [6144, 1024], P(('seq', 'fsdp')), may hold values from -9.1552734e-05 to 9.1552734e-05
- momentum_out: float32 [2048, 1024], P(('seq', 'fsdp')), may hold values from -9.1552734e-05 to 9.1552734e-05
- momentum_up: float32 [5632, 1024], P(('seq', 'fsdp')), may hold values from -9.1552734e-05 to 9.1552734e-05
- momentum_down: float32 [2816, 1024], P(('seq', 'fsdp')), may hold values from -9.1552734e-05 to 9.1552734e-05
- first_moment: float32 [35088], replicated, may hold values from -0.00018310547 to 0.00018310547
- second_moment: float32 [35088], replicated, may hold values from 1e-09 to 1e-08
Outputs:
- mixed: bfloat16 [4, 1024, 1024], P('fsdp', 'seq')
- grad_tokens: float32 [4, 1024, 1024], P('fsdp', 'seq')
- grad_in: float32 [6144, 1024], P(('seq', 'fsdp'))
- grad_out: float32 [2048, 1024], P(('seq', 'fsdp'))
- grad_up: float32 [5632, 1024], P(('seq', 'fsdp'))
- grad_down: float32 [2816, 1024], P(('seq', 'fsdp'))
- renewed_in: float32 [6144, 1024], P(('seq', 'fsdp'))
- renewed_out: float32 [2048, 1024], P(('seq', 'fsdp'))
- renewed_up: float32 [5632, 1024], P(('seq', 'fsdp'))
- renewed_down: float32 [2816, 1024], P(('seq', 'fsdp'))
- update_in: float32 [6144, 1024], P(('seq', 'fsdp'))
- update_out: float32 [2048, 1024], P(('seq', 'fsdp'))
- update_up: float32 [5632, 1024], P(('seq', 'fsdp'))
- update_down: float32 [2816, 1024], P(('seq', 'fsdp'))
- grad_vector: float32 [35088], replicated
- first_next: float32 [35088], replicated
- second_next: float32 [35088], replicated
- update_vector: float32 [35088], replicated
- grad_norm: float32 [1], replicated
Inputs may be any that keep to these rules, and one draw needn't show every extreme that they name: `segments`: within a row the document numbers never fall; every document of 0 .. 7 has 1 to 512 tokens, and one has exactly 512. `vectors`: gains lie between 0.5 and 1.5, exp(decay_log) between 1 and 16.
All inputs are finite; a program needn't handle non-finite values.
Results may differ from a plain program's by a relative error of at most 0.01.
The roundings to bfloat16 on the way count: a program that leaves them out, or rounds other values in their place, can miss the bound.
Values may be sent and summed in bfloat16 or wider, within the bound.
No kernel may reach another device: no remote copies, remote signals or barrier semaphores. Data moves between devices by JAX's collectives and lax.ppermute only.
A program may use at most 320 MiB of HBM per device.

v0:
```python
import math

import jax
import jax.numpy as jnp
from jax import lax
from jax.sharding import PartitionSpec as P

D = 1024
H = 8
DKH = 128
DVH = 256
FF = 2816
KCONV = 4
STRETCH = 64
NS_ITERS = 2
STEP = 10


PRECISE = lax.Precision.HIGHEST
RMS_EPS = 1e-06
NS_A = 3.4445
NS_B = -4.775
NS_C = 2.0315
MOMENTUM = 0.95
ADAM_ONE = 0.9
ADAM_TWO = 0.95
LEARN_RATE = 0.02
VECTOR_RATE = 0.01
CLIP_NORM = 1.0
ADAM_EPS = 1e-08


def passed_along(value, axis, steps):
    count = lax.axis_size(axis)
    first, last = (max(0, -steps), min(count, count - steps))
    return lax.ppermute(value, axis, [(source, source + steps) for source in range(first, last)])


def entering(value, axis, join, neutral):
    count, mine = (lax.axis_size(axis), lax.axis_index(axis))
    pieces = jax.tree.map(lambda part: lax.all_gather(part, axis), value)
    running = jax.tree.map(
        lambda part, zero: jnp.full_like(part, 0) + jnp.asarray(zero, part.dtype), value, neutral
    )

    def entering_hop(position, running):
        longer = join(running, jax.tree.map(lambda part: part[position], pieces))
        return jax.tree.map(lambda new, old: jnp.where(position < mine, new, old), longer, running)

    return lax.fori_loop(0, count - 1, entering_hop, running)


def prefix_2(value, axis, combine, identity):
    count, index = (lax.axis_size(axis), lax.axis_index(axis))
    everything = jax.tree.map(
        lambda part, kind: lax.all_gather(part.astype(kind), axis),
        value,
        jax.tree.map(lambda a: jnp.bfloat16 if a.dtype == jnp.float32 else a.dtype, value),
    )
    start = jax.tree.map(
        lambda part, zero: jnp.broadcast_to(jnp.asarray(zero, part.dtype), part.shape),
        value,
        identity,
    )

    def prefix_hop(k, before):
        at = count - 1 - k
        reached = at > index
        new = combine(
            before, jax.tree.map(lambda part, own: part[at].astype(own.dtype), everything, value)
        )
        return jax.tree.map(lambda a, b: jnp.where(reached, a, b), new, before)

    return lax.fori_loop(0, count, prefix_hop, start)


def unpack_vectors(vectors):
    widths = [2 * H * D, KCONV * (2 * H * DKH + H * DVH), D, D, DVH, H, H]
    pieces = []
    offset = 0
    for span_width in widths:
        pieces.append(vectors[offset : offset + span_width])
        offset += span_width
    projection = pieces[0].reshape(2 * H, D)
    conv_taps = pieces[1].reshape(KCONV, 2 * H * DKH + H * DVH)
    return (projection, conv_taps, pieces[2], pieces[3], pieces[4], pieces[5], pieces[6])


def rms_scale(values, gain):
    inverse = lax.rsqrt(jnp.mean(values * values, axis=-1, keepdims=True) + RMS_EPS)
    return values * inverse * gain


def swiglu(values):
    return jax.nn.silu(values[:, :FF]) * values[:, FF:]


def contract_last(left, right):
    return lax.dot_general(
        left, right, (((1,), (1,)), ((), ())), preferred_element_type=jnp.float32
    )


def contract_first(left, right):
    return lax.dot_general(
        left, right, (((0,), (0,)), ((), ())), preferred_element_type=jnp.float32
    )


def short_conv(extended, extended_ids, tap_weights):
    out_rows = extended.shape[0] - (KCONV - 1)
    current_ids = extended_ids[KCONV - 1 :]
    summed = jnp.zeros((out_rows, extended.shape[1]), jnp.float32)
    for tap_index in range(KCONV):
        same_document = (extended_ids[tap_index : tap_index + out_rows] == current_ids).astype(
            jnp.float32
        )
        summed = (
            summed
            + tap_weights[tap_index]
            * extended[tap_index : tap_index + out_rows]
            * same_document[:, None]
        )
    return jax.nn.silu(summed)


def delta_block(carry_state, block_inputs):
    queries, keys_unit, values, beta_rates, log_decay, block_ids, before_id = block_inputs
    length_block = block_ids.shape[0]
    cumulative = jnp.cumsum(log_decay, axis=0).T
    row_index = lax.broadcasted_iota(jnp.int32, (length_block, length_block), 0)
    col_index = lax.broadcasted_iota(jnp.int32, (length_block, length_block), 1)
    linked = (row_index >= col_index) & (block_ids[:, None] == block_ids[None, :])
    spread = cumulative[:, :, None] - cumulative[:, None, :]
    ratios = jnp.where(linked[None], jnp.exp(jnp.where(linked[None], spread, 0.0)), 0.0)
    carried = jnp.exp(cumulative) * (block_ids == before_id).astype(jnp.float32)[None, :]
    beta_heads = beta_rates.T
    key_gram = jnp.einsum("thd,shd->hts", keys_unit, keys_unit, precision=PRECISE)
    cross_gram = jnp.einsum("thd,shd->hts", queries, keys_unit, precision=PRECISE)
    strict = jnp.where((row_index > col_index)[None], ratios * key_gram, 0.0)
    system = jnp.eye(length_block, dtype=jnp.float32)[None] + beta_heads[:, :, None] * strict
    key_state = jnp.einsum("thd,hdw->htw", keys_unit, carry_state, precision=PRECISE)
    value_heads = jnp.transpose(values, (1, 0, 2))
    target = beta_heads[:, :, None] * (value_heads - carried[:, :, None] * key_state)
    solved = jax.scipy.linalg.solve_triangular(system, target, lower=True, unit_diagonal=True)
    query_state = jnp.einsum("thd,hdw->htw", queries, carry_state, precision=PRECISE)
    outputs = carried[:, :, None] * query_state + jnp.einsum(
        "hts,hsw->htw", ratios * cross_gram, solved, precision=PRECISE
    )
    last_ratios = ratios[:, length_block - 1, :]
    new_state = carried[:, length_block - 1][:, None, None] * carry_state + jnp.einsum(
        "shd,hs,hsw->hdw", keys_unit, last_ratios, solved, precision=PRECISE
    )
    return (new_state, jnp.transpose(outputs, (1, 0, 2)))


def mixer_core(
    extended,
    extended_ids,
    normed_in,
    tap_weights,
    small_weights,
    decay_log,
    decay_bias,
    start_state,
    first_id,
):
    count_rows = normed_in.shape[0]
    conv_out = short_conv(extended, extended_ids, tap_weights)
    small = jnp.dot(normed_in, small_weights.T, precision=PRECISE)
    beta_rates = jax.nn.sigmoid(small[:, :H])
    log_decay = -jnp.exp(decay_log) * jax.nn.softplus(small[:, H:] + decay_bias)
    queries = conv_out[:, : H * DKH].reshape(count_rows, H, DKH)
    queries = (
        queries
        * lax.rsqrt(jnp.sum(queries * queries, axis=-1, keepdims=True) + RMS_EPS)
        * DKH ** (-0.5)
    )
    keys_unit = conv_out[:, H * DKH : 2 * H * DKH].reshape(count_rows, H, DKH)
    keys_unit = keys_unit * lax.rsqrt(
        jnp.sum(keys_unit * keys_unit, axis=-1, keepdims=True) + RMS_EPS
    )
    values = conv_out[:, 2 * H * DKH :].reshape(count_rows, H, DVH)
    extra_width = start_state.shape[2] - DVH
    values = jnp.concatenate([values, jnp.zeros((count_rows, H, extra_width), jnp.float32)], axis=2)
    blocks = count_rows // STRETCH
    row_ids = extended_ids[KCONV - 1 :].reshape(blocks, STRETCH)
    before_ids = jnp.concatenate([jnp.reshape(first_id, (1,)), row_ids[: blocks - 1, STRETCH - 1]])
    final_state, outputs = lax.scan(
        jax.checkpoint(delta_block),
        start_state,
        (
            queries.reshape(blocks, STRETCH, H, DKH),
            keys_unit.reshape(blocks, STRETCH, H, DKH),
            values.reshape(blocks, STRETCH, H, start_state.shape[2]),
            beta_rates.reshape(blocks, STRETCH, H),
            log_decay.reshape(blocks, STRETCH, H),
            row_ids,
            before_ids,
        ),
    )
    return (outputs.reshape(count_rows, H, start_state.shape[2]), final_state)


def compose_maps(earlier, later):
    return (
        jnp.einsum("hij,hjk->hik", later[0], earlier[0], precision=PRECISE),
        jnp.einsum("hij,hjw->hiw", later[0], earlier[1], precision=PRECISE) + later[1],
    )


def muon_update(block_rows, gram, total_rows):
    inverse_norm = 1.0 / (jnp.sqrt(jnp.trace(gram)) + 1e-07)
    current = gram * (inverse_norm * inverse_norm)
    identity = jnp.eye(gram.shape[0], dtype=jnp.float32)
    ortho = block_rows * inverse_norm
    for iteration in range(NS_ITERS):
        square = jnp.dot(current, current, precision=PRECISE)
        factor = NS_A * identity + NS_B * current + NS_C * square
        ortho = jnp.dot(ortho, factor, precision=PRECISE)
        if iteration + 1 < NS_ITERS:
            current = jnp.dot(
                current, jnp.dot(factor, factor, precision=PRECISE), precision=PRECISE
            )
    return -LEARN_RATE * 0.2 * math.sqrt(max(total_rows, D)) * ortho


def self_gram(matrix):
    return lax.dot_general(matrix, matrix, (((0,), (0,)), ((), ())), precision=PRECISE)


def shards(
    tokens,
    cotangent,
    segments,
    weight_in,
    weight_out,
    weight_up,
    weight_down,
    vectors,
    momentum_in,
    momentum_out,
    momentum_up,
    momentum_down,
    first_moment,
    second_moment,
):
    projection, conv_taps, gain_one, gain_two, gain_head, decay_log, decay_bias = unpack_vectors(
        vectors
    )
    full_in, full_out, full_up, full_down = (
        lax.all_gather(weight_in.astype(jnp.bfloat16), "fsdp", axis=0, tiled=True),
        lax.all_gather(weight_out.astype(jnp.bfloat16), "fsdp", axis=0, tiled=True),
        lax.all_gather(weight_up.astype(jnp.bfloat16), "fsdp", axis=0, tiled=True),
        lax.all_gather(weight_down.astype(jnp.bfloat16), "fsdp", axis=0, tiled=True),
    )
    token_rows = tokens[0].astype(jnp.float32)
    count_rows = token_rows.shape[0]
    conv_width = 2 * H * DKH + H * DVH
    id_plus = segments[0].astype(jnp.float32) + 1.0
    normed, norm_back = jax.vjp(rms_scale, token_rows, gain_one)
    normed_low = normed.astype(jnp.bfloat16)
    projected = contract_last(normed_low, full_in).astype(jnp.bfloat16)
    conv_low = projected[:, :conv_width]
    gate_low = projected[:, conv_width:]
    edge_rows, edge_ids = passed_along(
        (
            conv_low[count_rows - KCONV + 1 :],
            id_plus[count_rows - KCONV + 1 :].astype(jnp.bfloat16),
        ),
        "seq",
        1,
    )
    extended_ids = jnp.concatenate([edge_ids.astype(jnp.float32), id_plus])
    extended = jnp.concatenate([edge_rows, conv_low], axis=0).astype(jnp.float32)
    identity = jnp.broadcast_to(jnp.eye(DKH, dtype=jnp.float32), (H, DKH, DKH))
    zero_state = jnp.zeros((H, DKH, DVH), jnp.float32)
    start_state = jnp.concatenate([zero_state, identity], axis=2)

    def mixer_local(conv_values, normed_values, tap_weights, small_weights, rates, rate_bias):
        return mixer_core(
            conv_values,
            extended_ids,
            normed_values,
            tap_weights,
            small_weights,
            rates,
            rate_bias,
            start_state,
            extended_ids[KCONV - 2],
        )

    (local_out, final_state), mixer_back = jax.vjp(
        mixer_local,
        extended,
        normed_low.astype(jnp.float32),
        conv_taps,
        projection,
        decay_log,
        decay_bias,
    )
    own_part = local_out[:, :, :DVH]
    reach_rows = local_out[:, :, DVH:]
    carry_state = final_state[:, :, :DVH]
    transfer = final_state[:, :, DVH:]
    prefix = entering((transfer, carry_state), "seq", compose_maps, (identity, zero_state))
    state_in = prefix[1]
    recurrent = own_part + jnp.einsum("thi,hiw->thw", reach_rows, state_in, precision=PRECISE)

    def gate_local(recurrent_values, gate_values, head_gain):
        return rms_scale(recurrent_values, head_gain).reshape(count_rows, H * DVH) * jax.nn.silu(
            gate_values
        )

    gated, gate_back = jax.vjp(gate_local, recurrent, gate_low.astype(jnp.float32), gain_head)
    gated_low = gated.astype(jnp.bfloat16)
    attention = jnp.dot(gated_low, full_out, preferred_element_type=jnp.float32)
    residual = token_rows + attention
    normed_two, norm_two_back = jax.vjp(rms_scale, residual, gain_two)
    normed_two_low = normed_two.astype(jnp.bfloat16)
    gate_up = contract_last(normed_two_low, full_up)
    hidden, swiglu_back = jax.vjp(swiglu, gate_up)
    hidden_low = hidden.astype(jnp.bfloat16)
    feed_out = jnp.dot(hidden_low, full_down, preferred_element_type=jnp.float32)
    mixed = (residual + feed_out).astype(jnp.bfloat16)[None]
    back_in, back_out, back_up, back_down = (full_in, full_out, full_up, full_down)
    grad_rows = cotangent[0].astype(jnp.float32)
    grad_feed_low = cotangent[0]
    grad_down = contract_first(hidden_low, grad_feed_low)
    grad_hidden = contract_last(grad_feed_low, back_down)
    (grad_gate_up,) = swiglu_back(grad_hidden)
    grad_gate_up_low = grad_gate_up.astype(jnp.bfloat16)
    grad_up = contract_first(grad_gate_up_low, normed_two_low)
    grad_normed_two = jnp.dot(grad_gate_up_low, back_up, preferred_element_type=jnp.float32)
    grad_resid_part, grad_gain_two = norm_two_back(grad_normed_two)
    grad_residual = grad_rows + grad_resid_part
    grad_attn_low = grad_residual.astype(jnp.bfloat16)
    grad_wout = contract_first(gated_low, grad_attn_low)
    grad_gated = contract_last(grad_attn_low, back_out)
    grad_recurrent, grad_gate_in, grad_gain_head = gate_back(grad_gated)
    grad_state_local = jnp.einsum("thi,thw->hiw", reach_rows, grad_recurrent, precision=PRECISE)
    grad_reach = jnp.einsum("thw,hiw->thi", grad_recurrent, state_in, precision=PRECISE)
    back_prefix = prefix_2(
        (jnp.swapaxes(transfer, 1, 2), grad_state_local),
        "seq",
        compose_maps,
        (identity, zero_state),
    )
    grad_after = back_prefix[1]
    grad_transfer = jnp.einsum("hiw,hjw->hij", grad_after, state_in, precision=PRECISE)
    grad_outputs = jnp.concatenate([grad_recurrent, grad_reach], axis=2)
    grad_final = jnp.concatenate([grad_after, grad_transfer], axis=2)
    (
        grad_extended,
        grad_normed_small,
        grad_taps,
        grad_projection,
        grad_decay_log,
        grad_decay_bias,
    ) = mixer_back((grad_outputs, grad_final))
    from_next = passed_along(grad_extended[: KCONV - 1].astype(jnp.bfloat16), "seq", -1).astype(
        jnp.float32
    )
    grad_conv = grad_extended[KCONV - 1 :]
    grad_conv = jnp.concatenate(
        [grad_conv[: count_rows - KCONV + 1], grad_conv[count_rows - KCONV + 1 :] + from_next],
        axis=0,
    )
    grad_projected_low = jnp.concatenate([grad_conv, grad_gate_in], axis=1).astype(jnp.bfloat16)
    grad_win = contract_first(grad_projected_low, normed_low)
    grad_normed = (
        jnp.dot(grad_projected_low, back_in, preferred_element_type=jnp.float32) + grad_normed_small
    )
    grad_token_part, grad_gain_one = norm_back(grad_normed)
    grad_tokens = (grad_residual + grad_token_part)[None]
    reduced_in, reduced_out, reduced_up, reduced_down = (
        lax.psum_scatter(grad_win, ("seq", "fsdp"), scatter_dimension=0, tiled=True),
        lax.psum_scatter(grad_wout, ("seq", "fsdp"), scatter_dimension=0, tiled=True),
        lax.psum_scatter(grad_up, ("seq", "fsdp"), scatter_dimension=0, tiled=True),
        lax.psum_scatter(grad_down, ("seq", "fsdp"), scatter_dimension=0, tiled=True),
    )
    grad_vector_part = jnp.concatenate(
        [
            grad_projection.reshape(-1),
            grad_taps.reshape(-1),
            grad_gain_one,
            grad_gain_two,
            grad_gain_head,
            grad_decay_log,
            grad_decay_bias,
        ]
    )
    squares_local = (
        jnp.sum(reduced_in * reduced_in)
        + jnp.sum(reduced_out * reduced_out)
        + jnp.sum(reduced_up * reduced_up)
        + jnp.sum(reduced_down * reduced_down)
    )
    grad_vector, squares_total = lax.psum((grad_vector_part, squares_local), ("seq", "fsdp"))
    grad_norm = jnp.sqrt(squares_total + jnp.sum(grad_vector * grad_vector))
    clipping = jnp.minimum(1.0, CLIP_NORM / (grad_norm + 1e-06))
    renewed_in = MOMENTUM * momentum_in + (1.0 - MOMENTUM) * clipping * reduced_in
    renewed_out = MOMENTUM * momentum_out + (1.0 - MOMENTUM) * clipping * reduced_out
    renewed_up = MOMENTUM * momentum_up + (1.0 - MOMENTUM) * clipping * reduced_up
    renewed_down = MOMENTUM * momentum_down + (1.0 - MOMENTUM) * clipping * reduced_down
    gram_in, gram_out, gram_up, gram_down = lax.psum(
        (
            self_gram(renewed_in),
            self_gram(renewed_out),
            self_gram(renewed_up),
            self_gram(renewed_down),
        ),
        ("seq", "fsdp"),
    )
    devices_all = lax.axis_size(("seq", "fsdp"))
    update_in = muon_update(renewed_in, gram_in, renewed_in.shape[0] * devices_all)
    update_out = muon_update(renewed_out, gram_out, renewed_out.shape[0] * devices_all)
    update_up = muon_update(renewed_up, gram_up, renewed_up.shape[0] * devices_all)
    update_down = muon_update(renewed_down, gram_down, renewed_down.shape[0] * devices_all)
    clipped = clipping * grad_vector
    first_next = ADAM_ONE * first_moment + (1.0 - ADAM_ONE) * clipped
    second_next = ADAM_TWO * second_moment + (1.0 - ADAM_TWO) * clipped * clipped
    update_vector = (
        -VECTOR_RATE
        * (first_next / (1.0 - ADAM_ONE**STEP))
        / (jnp.sqrt(second_next / (1.0 - ADAM_TWO**STEP)) + ADAM_EPS)
    )
    return (
        mixed,
        grad_tokens,
        reduced_in,
        reduced_out,
        reduced_up,
        reduced_down,
        renewed_in,
        renewed_out,
        renewed_up,
        renewed_down,
        update_in,
        update_out,
        update_up,
        update_down,
        grad_vector,
        first_next,
        second_next,
        update_vector,
        grad_norm.reshape(1),
    )


def solution(mesh):
    in_specs = (
        P("fsdp", "seq", None),
        P("fsdp", "seq", None),
        P("fsdp", "seq"),
        P("fsdp", None),
        P("fsdp", None),
        P("fsdp", None),
        P("fsdp", None),
        P(),
        P(("seq", "fsdp"), None),
        P(("seq", "fsdp"), None),
        P(("seq", "fsdp"), None),
        P(("seq", "fsdp"), None),
        P(),
        P(),
    )
    out_specs = (
        P("fsdp", "seq", None),
        P("fsdp", "seq", None),
        P(("seq", "fsdp"), None),
        P(("seq", "fsdp"), None),
        P(("seq", "fsdp"), None),
        P(("seq", "fsdp"), None),
        P(("seq", "fsdp"), None),
        P(("seq", "fsdp"), None),
        P(("seq", "fsdp"), None),
        P(("seq", "fsdp"), None),
        P(("seq", "fsdp"), None),
        P(("seq", "fsdp"), None),
        P(("seq", "fsdp"), None),
        P(("seq", "fsdp"), None),
        P(),
        P(),
        P(),
        P(),
        P(),
    )
    return jax.shard_map(shards, mesh=mesh, in_specs=in_specs, out_specs=out_specs, check_vma=False)
```

profile of v0, /device:TPU:0, one launch (start us, length us, event | category | flops | bytes accessed | tf_op | source)
XLA Modules:
  0.0 2295.8 jit_solution(8241279638209485992)
XLA Ops:
  7.3 5.0 convert_element_type.177
  12.5 4.9 collective-permute-start
  21.3 76.0 %all-gather.13.cloned.1.call-done = bf16[6144,1024]{1,0:T(8,128)(2,1)} async-done(((bf16[1536,1024]{1,0:T(8,128)(2,1)}), bf16[6144,1024]{1,0:T(8,128)(2,1)}) %all-gather.13.cloned.1.call-update) | async-done | bytes 12582928 | tf_op jit(solution)/shard_map/all_gather | solution.py:252
  97.3 8.8 convolution_convert_fusion
  123.2 114.6 %while.72 = (s32[]{:T(128)}, f32[8,128,384]{2,1,0:T(8,128)S(1)}, f32[2,64,8,384]{3,1,0,2:T(8,128)}, f32[2,8,128,384]{3,2,1,0:T(8,128)}, f32[2,64,8]{2,1,0:T(8,12...) while((s32[]{:T(128)}, f32[8,128,384]{2,1,0:T(8,128)S(1)}, ...), condition=%wide.region_5.7_spmd.clone, body=%wide.region_3.6_spmd.clone.sunk | while | flops 1311179520 | bytes 18957320 | solution.py:189
  130.3 39.3 %custom-call.26 = f32[8,1,64,64]{2,3,1,0:T(8,128)S(1)} custom-call(f32[8,1,64,64]{3,2,1,0:T(8,128)S(1)} %fusion.592), custom_call_target="InvertDiagBlocksLowerTriangular" | custom-call | tf_op jit(solution)/shard_map/jvp()/while/body/eval_jaxpr/jit(_solve_triangular)/vmap()/triangular_solve/custom-call.1 | solution.py:145
  187.5 39.3 %custom-call.26 = f32[8,1,64,64]{2,3,1,0:T(8,128)S(1)} custom-call(f32[8,1,64,64]{3,2,1,0:T(8,128)S(1)} %fusion.592), custom_call_target="InvertDiagBlocksLowerTriangular" | custom-call | tf_op jit(solution)/shard_map/jvp()/while/body/eval_jaxpr/jit(_solve_triangular)/vmap()/triangular_solve/custom-call.1 | solution.py:145
  242.7 4.7 convert_element_type.189
  252.0 60.5 %all-gather.21.cloned.1.call-done = f32[64,128,128]{2,1,0:T(8,128)} async-done(((f32[8,128,128]{2,1,0:T(8,128)}), f32[64,128,128]{2,1,0:T(8,128)}) %all-gather.21.cloned.1.call-update) | async-done | bytes 4194320 | tf_op jit(solution)/shard_map/all_gather | solution.py:41
  312.5 125.2 %all-gather.23.cloned.1.call-done = f32[64,128,256]{2,1,0:T(8,128)} async-done(((f32[8,128,256]{2,1,0:T(8,128)}), f32[64,128,256]{2,1,0:T(8,128)}) %all-gather.23.cloned.1.call-update) | async-done | bytes 8388624 | tf_op jit(solution)/shard_map/all_gather | solution.py:41
  437.7 19.1 while.73
  460.8 11.0 all-gather.15.cloned.1.call-done
  475.4 74.0 %all-gather.17.cloned.1.call-done = bf16[5632,1024]{1,0:T(8,128)(2,1)} async-done(((bf16[1408,1024]{1,0:T(8,128)(2,1)}), bf16[5632,1024]{1,0:T(8,128)(2,1)}) %all-gather.17.cloned.1.call-update) | async-done | bytes 11534352 | tf_op jit(solution)/shard_map/all_gather | solution.py:254
  549.3 9.8 fusion.320
  559.1 35.1 %all-gather.19.cloned.1.call-done = bf16[2816,1024]{1,0:T(8,128)(2,1)} async-done(((bf16[704,1024]{1,0:T(8,128)(2,1)}), bf16[2816,1024]{1,0:T(8,128)(2,1)}) %all-gather.19.cloned.1.call-update) | async-done | bytes 5767184 | tf_op jit(solution)/shard_map/all_gather | solution.py:255
  594.2 6.8 fusion.274
  604.6 3.8 fusion.230
  614.0 6.0 fusion.277
  625.8 6.9 fusion.263
  632.8 13.2 all-gather.25.cloned.1.call-done
  646.0 74.1 %all-gather.27.cloned.1.call-done = bf16[64,128,256]{2,1,0:T(8,128)(2,1)} async-done(((bf16[8,128,256]{2,1,0:T(8,128)(2,1)}), bf16[64,128,256]{2,1,0:T(8,128)(2,1)}) %all-gather.27.cloned.1.call-update) | async-done | bytes 4194320 | tf_op jit(solution)/shard_map/all_gather | solution.py:56
  720.0 16.7 while.74
  742.7 177.3 %while.71 = (s32[]{:T(128)}, f32[8,128,384]{2,1,0:T(8,128)}, f32[2,64,8,128]{3,2,1,0:T(8,128)}, f32[2,64,8,128]{3,2,1,0:T(8,128)}, f32[2,64,8,384]{3,2,1,0:T(8,1...) while((s32[]{:T(128)}, f32[8,128,384]{2,1,0:T(8,128)}, ...), condition=%wide.region_24.26_spmd, body=%wide.region_14.25_spmd.sunk | while | flops 3507491072 | bytes 131133032 | solution.py:189
  757.7 40.7 %custom-call.25 = f32[8,1,64,64]{2,3,1,0:T(8,128)} custom-call(f32[8,1,64,64]{3,2,1,0:T(8,128)} %get-tuple-element.1376), custom_call_target="InvertDiagBlocksLowerTriangular" | custom-call | tf_op jit(solution)/shard_map/transpose(jvp())/while/body/eval_jaxpr/checkpoint/jit(_solve_triangular)/vmap()/triangular_solve | solution.py:145
  812.0 3.8 convolution_bitcast_fusion.12
  846.0 40.7 %custom-call.25 = f32[8,1,64,64]{2,3,1,0:T(8,128)} custom-call(f32[8,1,64,64]{3,2,1,0:T(8,128)} %get-tuple-element.1376), custom_call_target="InvertDiagBlocksLowerTriangular" | custom-call | tf_op jit(solution)/shard_map/transpose(jvp())/while/body/eval_jaxpr/checkpoint/jit(_solve_triangular)/vmap()/triangular_solve | solution.py:145
  900.3 3.8 convolution_bitcast_fusion.12
  934.8 4.2 collective-permute-done.2
  939.7 10.3 fusion.240
  952.1 9.6 fusion.271
  964.4 7.9 fusion.244
  974.8 51.8 %reduce-scatter.11.cloned.1.call-done = f32[88,1024]{1,0:T(8,128)} async-done(((f32[2816,1024]{1,0:T(8,128)}), f32[88,1024]{1,0:T(8,128)}) %reduce-scatter.11.cloned.1.call-update) | async-done | bytes 360464 | tf_op jit(solution)/shard_map/reduce_scatter | solution.py:380
  1028.3 247.4 %reduce-scatter.5.cloned.1.call-done = f32[192,1024]{1,0:T(8,128)} async-done(((f32[6144,1024]{1,0:T(8,128)}), f32[192,1024]{1,0:T(8,128)}) %reduce-scatter.5.cloned.1.call-update) | async-done | bytes 786448 | tf_op jit(solution)/shard_map/reduce_scatter | solution.py:377
  1278.9 246.4 %reduce-scatter.9.cloned.1.call-done = f32[176,1024]{1,0:T(8,128)} async-done(((f32[5632,1024]{1,0:T(8,128)}), f32[176,1024]{1,0:T(8,128)}) %reduce-scatter.9.cloned.1.call-update) | async-done | bytes 720912 | tf_op jit(solution)/shard_map/reduce_scatter | solution.py:379
  1528.6 127.5 %all-reduce.23.cloned.1.call-done = f32[35088]{0:T(1024)} async-done(((f32[35088]{0:T(1024)}), f32[35088]{0:T(1024)}) %all-reduce.23.cloned.1.call-update) | async-done | bytes 140368 | tf_op jit(solution)/shard_map/psum | solution.py:399
  1657.7 42.2 %psum.42 = f32[]{:T(128)} all-reduce(f32[]{:T(128)S(6)} %add.495), channel_id=1, replica_groups=mesh['seq'=8,'fsdp'=4] {'seq','fsdp'}, use_global_device_ids=true, to_apply=%region_36.38 | all-reduce | flops 1 | bytes 8 | tf_op jit(solution)/shard_map/psum | solution.py:399
  1702.4 5.1 fusion.347
  1708.8 5.2 fusion.344
  1714.1 5.1 fusion.341
  1719.4 5.2 fusion.338
  1724.7 4.6 fusion.221
  1731.1 272.2 %all-reduce.25.cloned.1.call-done = (f32[1024,1024]{1,0:T(8,128)}, f32[1024,1024]{1,0:T(8,128)}, f32[1024,1024]{1,0:T(8,128)}, f32[1024,1024]{1,0:T(8,128)}) async-done(((f32[1024,1024]{1,0:T(8,128)}, f32[1024,1024]{1,0:T(8,128)}, f32[1024,1024]{1,0:T(8,128)}, f32[1024,1024]{1,0:T(8,128)}), (f32[1024,1024]{1,0:T(8,128)}, f32[1024,1024]{1,0:T(8,128)}, f32[1024,1024]{1,0:T(8,128)}, ...) | async-done | bytes 16777232 | tf_op jit(solution)/shard_map/psum | solution.py:406
  2003.3 4.2 select_reduce_fusion
  2008.3 18.8 fusion.144
  2027.1 15.0 fusion.348
  2045.5 19.3 fusion.140
  2064.8 14.9 fusion.345
  2079.7 3.7 fusion.234
  2085.0 18.9 fusion.136
  2103.9 15.1 fusion.342
  2122.5 18.9 fusion.132
  2141.4 15.1 fusion.339
  2159.5 13.6 fusion.156
  2173.2 13.7 fusion.349
  2186.9 13.8 fusion.160
  2200.7 13.4 fusion.346
  2214.2 13.6 fusion.164
  2227.8 13.8 fusion.343
  2241.7 15.8 fusion.168
  2257.5 13.4 fusion.340
  2271.0 4.0 fusion.218
  2275.0 4.2 fusion.214
  2279.2 3.8 fusion.222
  2282.9 4.3 fusion.211
  (684 shorter events, 259.1 us)
Async XLA Ops:
  7.2 10.2 slice-start
  7.2 10.4 copy-start.82
  7.2 10.2 copy-start.51
  7.2 90.0 %all-gather.13.cloned.1.call-start = ((), (), s32[]{:S(2)}) async-start(), calls=%async_computation.4 | async-start | bytes 15728640 | tf_op jit(solution)/shard_map/all_gather | solution.py:252
  12.3 300.2 %all-gather.21.cloned.1.call-start = ((), (), s32[]{:S(2)}) async-start(), calls=%async_computation.13 | async-start | bytes 4718592 | tf_op jit(solution)/shard_map/all_gather | solution.py:41
  12.5 8.1 collective-permute-start
  17.6 88.5 %copy-start.125 = (f32[128]{0:T(128)}, f32[128]{0:T(128)S(1)}, u32[]{:S(2)}) copy-start(f32[128]{0:T(128)S(1)} %fusion.245) | copy-start | bytes 1540
  17.6 88.5 %copy-start.115 = (f32[128]{0:T(128)}, f32[128]{0:T(128)S(1)}, u32[]{:S(2)}) copy-start(f32[128]{0:T(128)S(1)} %fusion.293) | copy-start | bytes 1540
  17.7 88.4 %copy-start.98 = (f32[1024]{0:T(1024)}, f32[1024]{0:T(1024)S(1)}, u32[]{:S(2)}) copy-start(f32[1024]{0:T(1024)S(1)} %get-tuple-element.1103) | copy-start | bytes 12292
  20.5 90.9 %copy-start.86 = (f32[4096]{0:T(1024)}, f32[4096]{0:T(1024)S(1)}, u32[]{:S(2)}) copy-start(f32[4096]{0:T(1024)S(1)} %get-tuple-element.1104) | copy-start | bytes 49156
  20.5 90.9 %copy-start.88 = (f32[4096]{0:T(1024)}, f32[4096]{0:T(1024)S(1)}, u32[]{:S(2)}) copy-start(f32[4096]{0:T(1024)S(1)} %get-tuple-element.1105) | copy-start | bytes 49156
  20.5 90.9 %copy-start.90 = (f32[4096]{0:T(1024)}, f32[4096]{0:T(1024)S(1)}, u32[]{:S(2)}) copy-start(f32[4096]{0:T(1024)S(1)} %get-tuple-element.1106) | copy-start | bytes 49156
  20.5 90.9 %copy-start.92 = (f32[4096]{0:T(1024)}, f32[4096]{0:T(1024)S(1)}, u32[]{:S(2)}) copy-start(f32[4096]{0:T(1024)S(1)} %get-tuple-element.1107) | copy-start | bytes 49156
  21.3 90.2 %copy-start.107 = (f32[128]{0:T(128)}, f32[128]{0:T(128)S(1)}, u32[]{:S(2)}) copy-start(f32[128]{0:T(128)S(1)} %get-tuple-element.1116) | copy-start | bytes 1540
  21.3 90.2 %copy-start.109 = (f32[128]{0:T(128)}, f32[128]{0:T(128)S(1)}, u32[]{:S(2)}) copy-start(f32[128]{0:T(128)S(1)} %get-tuple-element.1117) | copy-start | bytes 1540
  21.3 90.2 %copy-start.111 = (f32[128]{0:T(128)}, f32[128]{0:T(128)S(1)}, u32[]{:S(2)}) copy-start(f32[128]{0:T(128)S(1)} %get-tuple-element.1118) | copy-start | bytes 1540
  21.3 90.2 %copy-start.113 = (f32[128]{0:T(128)}, f32[128]{0:T(128)S(1)}, u32[]{:S(2)}) copy-start(f32[128]{0:T(128)S(1)} %get-tuple-element.1119) | copy-start | bytes 1540
  106.1 8.3 copy-start.34
  106.1 5.0 collective-permute-start.1
  238.7 199.0 %all-gather.23.cloned.1.call-start = ((), (), s32[]{:S(2)}) async-start(), calls=%async_computation.14 | async-start | bytes 9437184 | tf_op jit(solution)/shard_map/all_gather | solution.py:41
  239.8 231.9 %all-gather.15.cloned.1.call-start = ((), (), s32[]{:S(2)}) async-start(), calls=%async_computation.5 | async-start | bytes 5242880 | tf_op jit(solution)/shard_map/all_gather | solution.py:253
  242.6 306.7 %all-gather.17.cloned.1.call-start = ((), (), s32[]{:S(2)}) async-start(), calls=%async_computation.6 | async-start | bytes 14417920 | tf_op jit(solution)/shard_map/all_gather | solution.py:254
  247.4 346.7 %all-gather.19.cloned.1.call-start = ((), (), s32[]{:S(2)}) async-start(), calls=%async_computation.7 | async-start | bytes 7208960 | tf_op jit(solution)/shard_map/all_gather | solution.py:255
  250.9 395.1 %all-gather.25.cloned.1.call-start = ((), (), s32[]{:S(2)}) async-start(), calls=%async_computation.15 | async-start | bytes 2359296 | tf_op jit(solution)/shard_map/all_gather | solution.py:56
  251.9 468.1 %all-gather.27.cloned.1.call-start = ((), (), s32[]{:S(2)}) async-start(), calls=%async_computation.16 | async-start | bytes 4718592 | tf_op jit(solution)/shard_map/all_gather | solution.py:56
  456.8 15.0 copy-start.52
  475.3 128.0 %copy-start.25 = (f32[128,1024]{1,0:T(8,128)}, f32[128,1024]{1,0:T(8,128)S(1)}, u32[]{:S(2)}) copy-start(f32[128,1024]{1,0:T(8,128)S(1)} %get-tuple-element.1126) | copy-start | bytes 1572868
  549.3 44.8 %copy-start.71 = (bf16[1,128,1024]{2,1,0:T(8,128)(2,1)S(1)}, bf16[1,128,1024]{2,1,0:T(8,128)(2,1)}, u32[]{:S(2)}) copy-start(bf16[1,128,1024]{2,1,0:T(8,128)(2,1)} %param.25) | copy-start | bytes 786436
  604.6 9.4 copy-start.41
  613.4 359.7 %reduce-scatter.7.cloned.1.call-start = ((), (), s32[]{:S(2)}) async-start(), calls=%async_computation.9 | async-start | bytes 8650752 | tf_op jit(solution)/shard_map/reduce_scatter | solution.py:378
  620.0 406.6 %reduce-scatter.11.cloned.1.call-start = ((), (), s32[]{:S(2)}) async-start(), calls=%async_computation.11 | async-start | bytes 11894784 | tf_op jit(solution)/shard_map/reduce_scatter | solution.py:380
  632.7 643.0 %reduce-scatter.5.cloned.1.call-start = ((), (), s32[]{:S(2)}) async-start(), calls=%async_computation.8 | async-start | bytes 25952256 | tf_op jit(solution)/shard_map/reduce_scatter | solution.py:377
  742.7 179.8 %copy-start.103 = (f32[128,8]{0,1:T(8,128)S(1)}, f32[128,8]{0,1:T(8,128)}, u32[]{:S(2)}) copy-start(f32[128,8]{0,1:T(8,128)} %copy-done.102) | copy-start | bytes 12292
  742.7 181.7 %copy-start.101 = (f32[128,8]{0,1:T(8,128)S(1)}, f32[128,8]{0,1:T(8,128)}, u32[]{:S(2)}) copy-start(f32[128,8]{0,1:T(8,128)} %copy-done.100) | copy-start | bytes 12292
  742.9 9.1 copy-start.68
  757.7 45.6 %copy-start.5 = (f32[8,64,384]{2,1,0:T(8,128)}, f32[8,64,384]{2,1,0:T(8,128)S(1)}, u32[]{:S(2)}) copy-start(f32[8,64,384]{2,1,0:T(8,128)S(1)} %convolution_add_fusion.8) | copy-start | bytes 2359300 | tf_op jit(solution)/shard_map/transpose(jvp())/while
  812.0 8.0 copy-start.15
  815.8 8.4 copy-start.43
  815.8 8.4 copy-start.46
  831.3 9.1 copy-start.68
  846.0 45.5 %copy-start.5 = (f32[8,64,384]{2,1,0:T(8,128)}, f32[8,64,384]{2,1,0:T(8,128)S(1)}, u32[]{:S(2)}) copy-start(f32[8,64,384]{2,1,0:T(8,128)S(1)} %convolution_add_fusion.8) | copy-start | bytes 2359300 | tf_op jit(solution)/shard_map/transpose(jvp())/while
  900.3 8.0 copy-start.15
  904.1 8.4 copy-start.43
  904.1 8.4 copy-start.46
  933.3 5.8 collective-permute-start.2
  950.1 575.3 %reduce-scatter.9.cloned.1.call-start = ((), (), s32[]{:S(2)}) async-start(), calls=%async_computation.10 | async-start | bytes 23789568 | tf_op jit(solution)/shard_map/reduce_scatter | solution.py:379
  961.7 694.4 %all-reduce.23.cloned.1.call-start = ((), (), s32[]{:S(2)}) async-start(), calls=%async_computation.12 | async-start | bytes 286720 | tf_op jit(solution)/shard_map/psum | solution.py:399
  964.4 7.9 copy-start.106
  964.4 736.9 %copy-start.77 = (f32[88,1024]{1,0:T(8,128)S(1)}, f32[88,1024]{1,0:T(8,128)}, u32[]{:S(2)}) copy-start(f32[88,1024]{1,0:T(8,128)} %param.35) | copy-start | bytes 1081348
  973.1 1030.3 %all-reduce.25.cloned.1.call-start = ((), (), s32[]{:S(2)}) async-start(), calls=%async_computation.17 | async-start | bytes 33554432 | tf_op jit(solution)/shard_map/psum | solution.py:406
  1525.4 182.2 %copy-start.66 = (f32[176,1024]{1,0:T(8,128)S(1)}, f32[176,1024]{1,0:T(8,128)}, u32[]{:S(2)}) copy-start(f32[176,1024]{1,0:T(8,128)} %reduce-scatter.9.cloned.1.call-done) | copy-start | bytes 2162692
  1702.4 339.8 %copy-start.40 = (f32[88,1024]{1,0:T(8,128)}, f32[88,1024]{1,0:T(8,128)S(1)}, u32[]{:S(2)}) copy-start(f32[88,1024]{1,0:T(8,128)S(1)} %multiply_add_fusion.4) | copy-start | bytes 1081348
  1708.8 370.9 %copy-start.30 = (f32[176,1024]{1,0:T(8,128)}, f32[176,1024]{1,0:T(8,128)S(1)}, u32[]{:S(2)}) copy-start(f32[176,1024]{1,0:T(8,128)S(1)} %multiply_add_fusion.3) | copy-start | bytes 2162692
  1708.8 10.4 copy-start.65
  1708.8 10.4 copy-start.73
  1714.1 404.9 %copy-start.55 = (f32[64,1024]{1,0:T(8,128)}, f32[64,1024]{1,0:T(8,128)S(1)}, u32[]{:S(2)}) copy-start(f32[64,1024]{1,0:T(8,128)S(1)} %multiply_add_fusion.5) | copy-start | bytes 786436
  1719.4 437.2 %copy-start.29 = (f32[192,1024]{1,0:T(8,128)}, f32[192,1024]{1,0:T(8,128)S(1)}, u32[]{:S(2)}) copy-start(f32[192,1024]{1,0:T(8,128)S(1)} %multiply_add_fusion.2) | copy-start | bytes 2359300
  2064.8 18.7 copy-start.58
  2141.4 18.1 copy-start.132
  2173.2 13.7 copy-start.60
  2173.2 13.7 copy-start.133
  2200.7 13.4 copy-start.59
  2200.7 13.4 copy-start.134
  2227.8 13.8 copy-start.57
  (119 other events, 455.4 us)
Sparse Core Ops, SparseCore 0:
  12.4 84.7 all-gather.12
  238.8 73.6 all-gather.20
  314.6 122.9 all-gather.22
  439.1 32.6 all-gather.14
  473.2 76.1 all-gather.16
  550.7 43.3 all-gather.18
  596.8 49.0 all-gather.24
  648.7 71.3 all-gather.26
  722.9 149.6 reduce-scatter.6
  875.4 151.1 reduce-scatter.10
  1033.6 242.0 reduce-scatter.4
  1278.4 246.9 reduce-scatter.8
  1531.5 124.6 all-reduce.22
  1724.8 278.5 all-reduce.24
where the time goes:
time: 2300 us
  waiting for transfers between devices  1420 us (62%)
  matrix products  511 us (22%)
  other arithmetic  226 us (10%)
  local copies, waits for them, and re-layouts  59.7 us (3%)
  blocking collectives  42.2 us (2%)
  between operations  23.9 us (1%)
    psum x1, waiting for transfers between devices, shards(): lax.psum((self_gram(renewed_in), self_gram(renewed_out), self_gram(renewe...  272 us
    reduce_scatter x1, waiting for transfers between devices, shards(): lax.psum_scatter(grad_win, ('seq', 'fsdp'), scatter_dimension=0, tiled=True)  247 us
    reduce_scatter x1, waiting for transfers between devices, shards(): lax.psum_scatter(grad_up, ('seq', 'fsdp'), scatter_dimension=0, tiled=True)  246 us
    all_gather x2, waiting for transfers between devices, entering(): pieces = jax.tree.map(lambda part: lax.all_gather(part, axis), value)  186 us
    another operation x18, other arithmetic, delta_block(): jax.scipy.linalg.solve_triangular(system, target, lower=True, unit_diagon...  162 us
    dot_general x8, matrix products, muon_update(): square = jnp.dot(current, current, precision=PRECISE)  130 us
    psum x1, waiting for transfers between devices, shards(): lax.psum((grad_vector_part, squares_local), ('seq', 'fsdp'))  128 us
    all_gather x2, waiting for transfers between devices, prefix_2(): lax.all_gather(part.astype(kind), axis)  87.3 us
  transfers between devices with their start and end apart: 17, of which 15 were waited for; matrix products, arithmetic and copies ran while one was open for 15% of the time, Pallas kernels for 0%

commit v1 on v0

--- a/solution.py
+++ b/solution.py
@@ -448,6 +448,584 @@
     )
 
 
+def permuted(value, axis, bit):
+    count = lax.axis_size(axis)
+    return lax.ppermute(value, axis, [(i, i ^ (1 << bit)) for i in range(count)])
+
+
+def picked(value, index, position=0):
+    return lax.dynamic_index_in_dim(value, index, position, keepdims=False)
+
+
+def scattered_sum(parts, axis, order, wire=jnp.bfloat16):
+    width = len(order)
+    mine = lax.axis_index(axis)
+    held = parts.reshape((2,) * width + parts.shape[1:])
+    left = list(range(width - 1, -1, -1))
+    for bit in order:
+        position = left.index(bit)
+        value = (mine >> bit) & 1
+        keep = picked(held, value, position)
+        gone = picked(held, 1 - value, position)
+        held = keep.astype(jnp.float32) + permuted(gone.astype(wire), axis, bit).astype(jnp.float32)
+        left.remove(bit)
+    return held
+
+
+def gathered(value, axis, order):
+    mine = lax.axis_index(axis)
+    held = value[None]
+    done = []
+    for bit in order:
+        other = permuted(held, axis, bit)
+        high = ((mine >> bit) & 1) == 1
+        first = jnp.where(high, other, held)
+        second = jnp.where(high, held, other)
+        joined = jnp.stack([first, second])
+        place = sum(1 for d in done if d > bit)
+        shape = (2,) * (len(done) + 1) + value.shape
+        joined = jnp.moveaxis(joined.reshape(shape), 0, place)
+        done = sorted(done + [bit], reverse=True)
+        held = joined.reshape((2 ** len(done),) + value.shape)
+    return held
+
+
+def summed_everywhere(value, axes_bits):
+    for axis, bit in axes_bits:
+        value = value + permuted(value, axis, bit)
+    return value
+
+
+def matchings(targets, slots, count):
+    remaining = {src: [(dst, i) for i, (dst, _) in enumerate(targets[src])] for src in range(count)}
+    rounds = []
+    for _ in range(slots):
+        owner = {}
+
+        def seek(src, seen):
+            for dst, i in remaining[src]:
+                if dst in seen:
+                    continue
+                seen.add(dst)
+                if dst not in owner or seek(owner[dst][0], seen):
+                    owner[dst] = (src, i)
+                    return True
+            return False
+
+        for src in range(count):
+            assert seek(src, set())
+        chosen = {}
+        for dst, (src, i) in owner.items():
+            chosen[src] = (dst, i)
+        for src, (dst, i) in chosen.items():
+            remaining[src].remove((dst, i))
+        rounds.append(chosen)
+    return rounds
+
+
+def routed(granules, targets, axes, me):
+    slots, count = (len(targets[0]), len(targets))
+    pieces = []
+    for chosen in matchings(targets, slots, count):
+        sent = jnp.asarray([chosen[src][1] for src in range(count)], jnp.int32)
+        landing = [0] * count
+        for src, (dst, i) in chosen.items():
+            landing[dst] = targets[src][i][1]
+        piece = lax.ppermute(
+            picked(granules, sent[me]), axes, [(src, chosen[src][0]) for src in range(count)]
+        )
+        pieces.append((piece, jnp.asarray(landing, jnp.int32)[me]))
+    return [
+        sum(
+            jnp.where(place == slot, piece.astype(jnp.float32), 0.0)
+            for piece, place in pieces
+        )
+        for slot in range(slots)
+    ]
+
+
+CHUNK = 128
+MIX = lax.Precision.HIGH
+
+
+def product(spec, left, right):
+    return jnp.einsum(spec, left, right, precision=MIX, preferred_element_type=jnp.float32)
+
+
+def unit_inverse(strict):
+    size = strict.shape[-1]
+    rows = lax.broadcasted_iota(jnp.int32, (size, size), 0)
+    cols = lax.broadcasted_iota(jnp.int32, (size, size), 1)
+    exact = lambda a, b: jnp.einsum("nij,njk->nik", a, b, precision=PRECISE)
+    eye = (rows == cols).astype(jnp.float32)[None]
+    base = -jnp.where((rows // 8 == cols // 8)[None], strict, 0.0)
+    second = exact(base, base)
+    fourth = exact(second, second)
+    inverse = eye + base
+    inverse = inverse + exact(inverse, second)
+    inverse = inverse + exact(inverse, fourth)
+    width = 8
+    while width < size:
+        joint = (rows // (2 * width) == cols // (2 * width)) & (rows // width != cols // width)
+        inverse = inverse - exact(exact(inverse, jnp.where(joint[None], strict, 0.0)), inverse)
+        width *= 2
+    return inverse
+
+
+@jax.custom_vjp
+def solved_with(strict, right):
+    return product("nij,njw->niw", unit_inverse(strict), right)
+
+
+def solved_keep(strict, right):
+    inverse = unit_inverse(strict)
+    answer = product("nij,njw->niw", inverse, right)
+    return answer, (inverse, answer)
+
+
+def solved_back(kept, grad):
+    inverse, answer = kept
+    grad_right = product("nji,njw->niw", inverse, grad)
+    return -product("niw,njw->nij", grad_right, answer), grad_right
+
+
+solved_with.defvjp(solved_keep, solved_back)
+
+
+def chunk_maps(queries, keys, values, beta, cumulative, linked, below, first_open):
+    spread = cumulative[:, :, None] - cumulative[:, None, :]
+    ratios = jnp.where(linked, jnp.exp(jnp.where(linked, spread, 0.0)), 0.0)
+    carried = jnp.exp(cumulative) * first_open
+    key_gram = product("ntd,nsd->nts", keys, keys)
+    cross = ratios * product("ntd,nsd->nts", queries, keys)
+    strict = beta[:, :, None] * jnp.where(below, ratios * key_gram, 0.0)
+    right = beta[:, :, None] * jnp.concatenate([carried[:, :, None] * keys, values], axis=2)
+    both = solved_with(strict, right)
+    weighted = keys * ratios[:, -1, :, None]
+    onward = product("nsd,nsw->ndw", weighted, both)
+    outward = product("nts,nsw->ntw", cross, both)
+    size = keys.shape[2]
+    eye = jnp.eye(size, dtype=jnp.float32)[None]
+    state_map = carried[:, -1][:, None, None] * eye - onward[:, :, :size]
+    reach = carried[:, :, None] * queries - outward[:, :, :size]
+    return state_map, onward[:, :, size:], reach, outward[:, :, size:]
+
+
+def pair_inputs(conv_in, small, ids, taps, rate, bias):
+    count = conv_in.shape[0]
+    extended = jnp.concatenate([jnp.zeros((KCONV - 1, conv_in.shape[1]), jnp.float32), conv_in])
+    extended_ids = jnp.concatenate([jnp.zeros((KCONV - 1,), jnp.float32), ids])
+    conv_out = short_conv(extended, extended_ids, taps)
+    beta = jax.nn.sigmoid(small[:, 0])
+    log_decay = -jnp.exp(rate) * jax.nn.softplus(small[:, 1] + bias)
+    queries = conv_out[:, :DKH]
+    queries = (
+        queries
+        * lax.rsqrt(jnp.sum(queries * queries, axis=-1, keepdims=True) + RMS_EPS)
+        * DKH ** (-0.5)
+    )
+    keys = conv_out[:, DKH : 2 * DKH]
+    keys = keys * lax.rsqrt(jnp.sum(keys * keys, axis=-1, keepdims=True) + RMS_EPS)
+    chunks = count // CHUNK
+    cut = lambda a: a.reshape((chunks, CHUNK) + a.shape[1:])
+    cumulative = jnp.cumsum(cut(log_decay), axis=1)
+    return cut(queries), cut(keys), cut(conv_out[:, 2 * DKH :]), cut(beta), cumulative
+
+
+def pair_masks(ids):
+    chunks = ids.shape[0] // CHUNK
+    cut = ids.reshape(chunks, CHUNK)
+    rows = lax.broadcasted_iota(jnp.int32, (CHUNK, CHUNK), 0)
+    cols = lax.broadcasted_iota(jnp.int32, (CHUNK, CHUNK), 1)
+    linked = (rows >= cols)[None] & (cut[:, :, None] == cut[:, None, :])
+    before = jnp.concatenate([jnp.zeros((1,), ids.dtype), cut[:-1, -1]])
+    return linked, (rows > cols)[None], (cut == before[:, None]).astype(jnp.float32)
+
+
+def states_forward(state_map, addend):
+    state = jnp.zeros(addend.shape[1:], jnp.float32)
+    entering_states = []
+    for n in range(addend.shape[0]):
+        entering_states.append(state)
+        state = jnp.dot(state_map[n], state, precision=MIX) + addend[n]
+    return jnp.stack(entering_states)
+
+
+def states_backward(state_map, grad_entering):
+    grad = jnp.zeros(grad_entering.shape[1:], jnp.float32)
+    after = []
+    for n in reversed(range(grad_entering.shape[0])):
+        after.append(grad)
+        grad = grad_entering[n] + jnp.einsum("ij,iw->jw", state_map[n], grad, precision=MIX)
+    return jnp.stack(after[::-1])
+
+
+def gram_panels(matrix):
+    side = D // 4
+    narrow = matrix.astype(jnp.bfloat16)
+    blocks = []
+    for i in range(4):
+        panel = contract_first(narrow[:, i * side : (i + 1) * side], narrow[:, i * side :])
+        for j in range(4 - i):
+            blocks.append(panel[:, j * side : (j + 1) * side])
+    return blocks
+
+
+def gram_whole(blocks):
+    index = {}
+    count = 0
+    for i in range(4):
+        for j in range(i, 4):
+            index[i, j] = count
+            count += 1
+    rows = [
+        jnp.concatenate(
+            [blocks[index[i, j]] if i <= j else blocks[index[j, i]].T for j in range(4)], axis=1
+        )
+        for i in range(4)
+    ]
+    return jnp.concatenate(rows, axis=0)
+
+
+def thin_update(block_rows, gram, total_rows):
+    inverse_norm = 1.0 / (jnp.sqrt(jnp.trace(gram.astype(jnp.float32))) + 1e-07)
+    current = (gram.astype(jnp.float32) * (inverse_norm * inverse_norm)).astype(jnp.bfloat16)
+
+    def times(rows):
+        return jnp.dot(rows.astype(jnp.bfloat16), current, preferred_element_type=jnp.float32)
+
+    def through(rows):
+        once = times(rows)
+        return NS_A * rows + NS_B * once + NS_C * times(once)
+
+    def advanced(rows):
+        return through(through(times(rows)))
+
+    first = through(block_rows * inverse_norm)
+    once = advanced(first)
+    ortho = NS_A * first + NS_B * once + NS_C * advanced(once)
+    return -LEARN_RATE * 0.2 * math.sqrt(max(total_rows, D)) * ortho
+
+
+def head_tables(fsdp):
+    per = (2 * H * DKH + 2 * H * DVH) // fsdp // DKH
+    give, find = ([], [])
+    for head in range(H):
+        wanted = [head, H + head] + [
+            2 * H + base + 2 * head + k for base in (0, 2 * H) for k in range(2)
+        ]
+        lists = [[g % per for g in wanted if g // per == f] for f in range(fsdp)]
+        seen = [0] * fsdp
+        where = []
+        for g in wanted:
+            f = g // per
+            where.append((f, seen[f]))
+            seen[f] += 1
+        most = 2
+        assert max(len(one) for one in lists) <= most
+        give.append([one + [0] * (most - len(one)) for one in lists])
+        find.append([f * most + j for f, j in where])
+    return give, find
+
+
+def in_targets(seq, fsdp):
+    granule = 64
+    per = (2 * H * DKH + 2 * H * DVH) // (seq * fsdp) // granule
+    targets = []
+    for s in range(seq):
+        rows = []
+        for start, size in (
+            (s * DKH, DKH),
+            (H * DKH + s * DKH, DKH),
+            (2 * H * DKH + s * DVH, DVH),
+            (2 * H * DKH + H * DVH + s * DVH, DVH),
+        ):
+            rows += [start // granule + k for k in range(size // granule)]
+        for f in range(fsdp):
+            own = rows[f * per : (f + 1) * per]
+            targets.append([(g // per, g % per) for g in own])
+    return targets
+
+
+def up_targets(seq, fsdp):
+    piece = FF // (seq * fsdp)
+    return [
+        [((f * seq + s) // 2, (f * seq + s) % 2), (seq * fsdp // 2 + (f * seq + s) // 2, (f * seq + s) % 2)]
+        for s in range(seq)
+        for f in range(fsdp)
+    ]
+
+
+def down_targets(seq, fsdp):
+    return [[(f * seq + s, 0)] for s in range(seq) for f in range(fsdp)]
+
+
+def up_shuffle_targets(fsdp):
+    half = fsdp // 2
+    return [[(2 * (f % half) + k, f // half) for k in range(2)] for f in range(fsdp)]
+
+
+def pair_shards(
+    tokens,
+    cotangent,
+    segments,
+    weight_in,
+    weight_out,
+    weight_up,
+    weight_down,
+    vectors,
+    momentum_in,
+    momentum_out,
+    momentum_up,
+    momentum_down,
+    first_moment,
+    second_moment,
+):
+    seq, fsdp = (lax.axis_size("seq"), lax.axis_size("fsdp"))
+    head, group = (lax.axis_index("seq"), lax.axis_index("fsdp"))
+    me = head * fsdp + group
+    seq_bits, fsdp_bits = (seq.bit_length() - 1, fsdp.bit_length() - 1)
+    fsdp_order = list(range(fsdp_bits))
+    projection, conv_taps, gain_one, gain_two, gain_head, decay_log, decay_bias = unpack_vectors(
+        vectors
+    )
+    own = tokens.shape[1]
+    length = own * seq
+    heads_low = jnp.bfloat16
+
+    row_ids = jnp.zeros((16, D), heads_low)
+    row_ids = row_ids.at[0, :own].set((segments[0] + 1).astype(heads_low))
+    packed = lax.all_gather(jnp.concatenate([tokens[0], row_ids]), "seq")
+    token_seq = packed[:, :own].reshape(length, D)
+    ids = packed[:, own, :own].reshape(length).astype(jnp.float32)
+
+    give, find = head_tables(fsdp)
+    give_table = jnp.asarray(give, jnp.int32)
+    find_table = jnp.asarray(find, jnp.int32)
+    slices = [
+        lax.dynamic_slice_in_dim(weight_in, give_table[head, group, j] * DKH, DKH, 0)
+        for j in range(2)
+    ]
+    given = lax.all_gather(jnp.stack(slices).astype(heads_low), "fsdp", axis=0, tiled=True)
+    head_rows = jnp.concatenate([picked(given, find_table[head, j]) for j in range(6)])
+    small_rows = jnp.stack([picked(projection, head), picked(projection, H + head)])
+    taps_rows = conv_taps.reshape(KCONV, 4 * H, DKH)
+    taps_head = jnp.concatenate(
+        [
+            picked(taps_rows, head, 1),
+            picked(taps_rows, H + head, 1),
+            picked(taps_rows, 2 * H + 2 * head, 1),
+            picked(taps_rows, 2 * H + 2 * head + 1, 1),
+        ],
+        axis=1,
+    )
+    rate, bias = (decay_log[head], decay_bias[head])
+
+    full_out = lax.all_gather(weight_out.astype(heads_low), "fsdp", axis=0, tiled=True)
+    cot_group = gathered(cotangent[0], "fsdp", fsdp_order[::-1]).reshape(fsdp * own, D)
+    half_up = weight_up.shape[0] // 2
+    up_gate, up_value = [
+        part.astype(heads_low)
+        for part in routed(
+            weight_up.astype(heads_low).reshape(2, half_up, D), up_shuffle_targets(fsdp), "fsdp", group
+        )
+    ]
+    low_up = jnp.concatenate([up_gate, up_value])
+    low_down = weight_down.astype(heads_low)
+
+    token_rows = token_seq.astype(jnp.float32)
+    normed_low = rms_scale(token_rows, gain_one).astype(heads_low)
+    projected = contract_last(normed_low, head_rows).astype(heads_low)
+    conv_in = projected[:, : 2 * DKH + DVH].astype(jnp.float32)
+    gate_in = projected[:, 2 * DKH + DVH :].astype(jnp.float32)
+    small = lax.dot_general(
+        normed_low.astype(jnp.float32), small_rows, (((1,), (1,)), ((), ())), precision=PRECISE
+    )
+    linked, below, first_open = pair_masks(ids)
+    parts, inputs_back = jax.vjp(
+        lambda c, m, t, r, b: pair_inputs(c, m, ids, t, r, b),
+        conv_in,
+        small,
+        taps_head,
+        rate,
+        bias,
+    )
+    maps, maps_back = jax.vjp(
+        lambda q, k, v, b, c: chunk_maps(q, k, v, b, c, linked, below, first_open), *parts
+    )
+    state_map, addend, reach, local = maps
+    states = states_forward(state_map, addend)
+    recurrent = (product("ntd,ndw->ntw", reach, states) + local).reshape(length, DVH)
+
+    def gate_pair(recurrent_values, gate_values, head_gain):
+        return rms_scale(recurrent_values, head_gain) * jax.nn.silu(gate_values)
+
+    gated, gate_back = jax.vjp(gate_pair, recurrent, gate_in, gain_head)
+    gated_low = gated.astype(heads_low)
+    gated_own = lax.all_to_all(gated_low.reshape(seq, own, DVH), "seq", 0, 0)
+    gated_own = jnp.transpose(gated_own, (1, 0, 2)).reshape(own, H * DVH)
+
+    own_rows = tokens[0].astype(jnp.float32)
+    residual = own_rows + jnp.dot(gated_own, full_out, preferred_element_type=jnp.float32)
+    normed_two, norm_two_back = jax.vjp(rms_scale, residual, gain_two)
+    two_group = gathered(normed_two.astype(heads_low), "fsdp", fsdp_order[::-1])
+    two_group = two_group.reshape(fsdp * own, D)
+    gate_up = contract_last(two_group, low_up)
+    units = half_up
+
+    def swiglu_own(values):
+        return jax.nn.silu(values[:, :units]) * values[:, units:]
+
+    hidden, swiglu_back = jax.vjp(swiglu_own, gate_up)
+    hidden_low = hidden.astype(heads_low)
+    feed_parts = jnp.dot(hidden_low, low_down, preferred_element_type=jnp.float32)
+    feed_out = scattered_sum(feed_parts.reshape(fsdp, own, D), "fsdp", fsdp_order)
+    mixed = (residual + feed_out).astype(heads_low)[None]
+
+    grad_hidden = contract_last(cot_group, low_down)
+    (grad_gate_up,) = swiglu_back(grad_hidden)
+    grad_gate_up_low = grad_gate_up.astype(heads_low)
+    two_parts = jnp.dot(grad_gate_up_low, low_up, preferred_element_type=jnp.float32)
+    grad_normed_two = scattered_sum(two_parts.reshape(fsdp, own, D), "fsdp", fsdp_order)
+    grad_down_part = contract_first(hidden_low, cot_group)
+    grad_up_part = contract_first(grad_gate_up_low, two_group)
+    grad_resid_part, grad_gain_two = norm_two_back(grad_normed_two)
+    grad_residual = cotangent[0].astype(jnp.float32) + grad_resid_part
+    grad_attn_low = grad_residual.astype(heads_low)
+    attn_seq = lax.all_gather(grad_attn_low, "seq", axis=0, tiled=True)
+
+    piece = FF // (seq * fsdp)
+    ff_parts = jnp.concatenate(
+        [
+            grad_down_part.reshape(seq, 1, piece, D),
+            jnp.transpose(grad_up_part.reshape(2, seq, piece, D), (1, 0, 2, 3)),
+        ],
+        axis=1,
+    )
+    ff_low = ff_parts.astype(heads_low)
+    ff_left = scattered_sum(ff_low[..., : D // 2], "seq", [0, 1, 2])
+    ff_right = scattered_sum(ff_low[..., D // 2 :], "seq", [1, 0, 2])
+    ff_own = jnp.concatenate([ff_left, ff_right], axis=-1).astype(heads_low)
+    both = ("seq", "fsdp")
+    (reduced_down,) = routed(ff_own[:1], down_targets(seq, fsdp), both, me)
+    reduced_up = jnp.concatenate(routed(ff_own[1:], up_targets(seq, fsdp), both, me))
+
+    out_rows = lax.dynamic_slice_in_dim(full_out, head * DVH, DVH, 0)
+    grad_gated = contract_last(attn_seq, out_rows)
+    grad_out_part = contract_first(gated_low, attn_seq)
+    reduced_out = scattered_sum(grad_out_part.reshape(fsdp, DVH // fsdp, D), "fsdp", fsdp_order)
+    grad_recurrent, grad_gate_in, grad_gain_head = gate_back(grad_gated)
+    grad_out_chunks = grad_recurrent.reshape(local.shape)
+    grad_entering = product("ntd,ntw->ndw", reach, grad_out_chunks)
+    grad_after = states_backward(state_map, grad_entering)
+    grad_maps = (
+        product("niw,njw->nij", grad_after, states),
+        grad_after,
+        product("ntw,ndw->ntd", grad_out_chunks, states),
+        grad_out_chunks,
+    )
+    grad_conv, grad_small, grad_taps, grad_rate, grad_bias = inputs_back(maps_back(grad_maps))
+    grad_projected_low = jnp.concatenate([grad_conv, grad_gate_in], axis=1).astype(heads_low)
+    grad_in_part = contract_first(grad_projected_low, normed_low)
+    normed_parts = jnp.dot(grad_projected_low, head_rows, preferred_element_type=jnp.float32)
+    normed_parts = normed_parts + jnp.dot(grad_small, small_rows, precision=PRECISE)
+    normed_low_parts = normed_parts.astype(heads_low).reshape(seq, own, D)
+    normed_left = scattered_sum(normed_low_parts[..., : D // 2], "seq", [0, 1, 2])
+    normed_right = scattered_sum(normed_low_parts[..., D // 2 :], "seq", [1, 0, 2])
+    grad_normed = jnp.concatenate([normed_left, normed_right], axis=-1)
+    _, norm_back = jax.vjp(rms_scale, own_rows, gain_one)
+    grad_token_part, grad_gain_one = norm_back(grad_normed)
+    grad_tokens = (grad_residual + grad_token_part)[None]
+    in_rows = grad_in_part.shape[0] // fsdp
+    in_own = scattered_sum(grad_in_part.reshape(fsdp, in_rows, D), "fsdp", fsdp_order)
+    in_granules = in_own.astype(heads_low).reshape(in_rows // 64, 64, D)
+    reduced_in = jnp.concatenate(routed(in_granules, in_targets(seq, fsdp), both, me))
+
+    grad_projection = lax.dot_general(
+        grad_small, normed_low.astype(jnp.float32), (((0,), (0,)), ((), ())), precision=PRECISE
+    )
+    width = 2 * DKH + DVH
+    compact = jnp.concatenate(
+        [
+            grad_projection.reshape(-1),
+            grad_taps.reshape(-1),
+            grad_gain_one,
+            grad_gain_two,
+            grad_gain_head,
+            grad_rate.reshape(1),
+            grad_bias.reshape(1),
+        ]
+    )
+    fill = -compact.shape[0] % 1024
+    compact = jnp.concatenate([compact, jnp.zeros((fill,), jnp.float32)]).reshape(-1, 128)
+    compact = summed_everywhere(compact, [("fsdp", bit) for bit in range(fsdp_bits)])
+    compact = gathered(compact, "seq", list(range(seq_bits))).reshape(seq, -1)
+    cuts = [2 * D, KCONV * width, D, D, DVH, 1, 1]
+    places = [sum(cuts[:i]) for i in range(len(cuts))]
+    take = lambda i: compact[:, places[i] : places[i] + cuts[i]]
+    taps_all = take(1).reshape(seq, KCONV, width)
+    spread_taps = lambda a, b: jnp.transpose(taps_all[:, :, a:b], (1, 0, 2)).reshape(KCONV, -1)
+    grad_vector = jnp.concatenate(
+        [
+            jnp.transpose(take(0).reshape(seq, 2, D), (1, 0, 2)).reshape(-1),
+            jnp.concatenate(
+                [spread_taps(0, DKH), spread_taps(DKH, 2 * DKH), spread_taps(2 * DKH, width)],
+                axis=1,
+            ).reshape(-1),
+            jnp.sum(take(2), axis=0),
+            jnp.sum(take(3), axis=0),
+            jnp.sum(take(4), axis=0),
+            take(5).reshape(-1),
+            take(6).reshape(-1),
+        ]
+    )
+
+    squares = (
+        jnp.sum(reduced_in * reduced_in)
+        + jnp.sum(reduced_out * reduced_out)
+        + jnp.sum(reduced_up * reduced_up)
+        + jnp.sum(reduced_down * reduced_down)
+    )
+    all_bits = [("fsdp", bit) for bit in range(fsdp_bits)] + [("seq", bit) for bit in range(seq_bits)]
+    squares = summed_everywhere(jnp.full((8, 128), squares), all_bits)[0, 0]
+    grad_norm = jnp.sqrt(squares + jnp.sum(grad_vector * grad_vector))
+    clipping = jnp.minimum(1.0, CLIP_NORM / (grad_norm + 1e-06))
+    reduced = (reduced_in, reduced_out, reduced_up, reduced_down)
+    momenta = (momentum_in, momentum_out, momentum_up, momentum_down)
+    renewed = [MOMENTUM * m + (1.0 - MOMENTUM) * clipping * g for m, g in zip(momenta, reduced)]
+    blocks = jnp.stack([block for one in renewed for block in gram_panels(one)])
+    blocks = lax.psum(blocks.astype(heads_low), both)
+    updates = [
+        thin_update(one, gram_whole(blocks[10 * i : 10 * i + 10]), one.shape[0] * seq * fsdp)
+        for i, one in enumerate(renewed)
+    ]
+    clipped = clipping * grad_vector
+    first_next = ADAM_ONE * first_moment + (1.0 - ADAM_ONE) * clipped
+    second_next = ADAM_TWO * second_moment + (1.0 - ADAM_TWO) * clipped * clipped
+    update_vector = (
+        -VECTOR_RATE
+        * (first_next / (1.0 - ADAM_ONE**STEP))
+        / (jnp.sqrt(second_next / (1.0 - ADAM_TWO**STEP)) + ADAM_EPS)
+    )
+    return (
+        mixed,
+        grad_tokens,
+        *reduced,
+        *renewed,
+        *updates,
+        grad_vector,
+        first_next,
+        second_next,
+        update_vector,
+        grad_norm.reshape(1),
+    )
+
+
+def fits_pairs(mesh, sequences):
+    seq, fsdp = (mesh.shape["seq"], mesh.shape["fsdp"])
+    return seq == H and fsdp == 4 and sequences == fsdp
+
+
 def solution(mesh):
     in_specs = (
         P("fsdp", "seq", None),
@@ -486,4 +1064,11 @@
         P(),
         P(),
     )
-    return jax.shard_map(shards, mesh=mesh, in_specs=in_specs, out_specs=out_specs, check_vma=False)
+
+    def step(tokens, *rest):
+        local = pair_shards if fits_pairs(mesh, tokens.shape[0]) else shards
+        return jax.shard_map(
+            local, mesh=mesh, in_specs=in_specs, out_specs=out_specs, check_vma=False
+        )(tokens, *rest)
+
+    return step

time: 2300 us -> 801 us (0.35)
  waiting for transfers between devices: 1420 us -> 308 us
  matrix products: 511 us -> 111 us
  other arithmetic: 226 us -> 115 us
  starting transfers between devices: 10.7 us -> 85.4 us
  local copies, waits for them, and re-layouts: 59.7 us -> 109 us
  blocking collectives: 42.2 us -> 0 us
  between operations: 23.9 us -> 64.7 us
    reduce_scatter x4 -> x0, waiting for transfers between devices: 546 us -> none  [the longest x1 247 us: shards(): lax.psum_scatter(grad_win, ('seq', 'fsdp'), scatter_dimension=0, tiled=True)]
    all_gather x8 -> x4, waiting for transfers between devices: 469 us -> 55.4 us  [the longest x1 48.7 us: pair_shards(): packed = lax.all_gather(jnp.concatenate([tokens[0], row_ids]), 'seq')]
    dot_general x100, matrix products: 441 us -> 87.6 us  [the longest x48 32 us: times(): jnp.dot(rows.astype(jnp.bfloat16), current, preferred_element_type=jnp.fl...]
    psum x2 -> x1, waiting for transfers between devices: 400 us -> 143 us  [pair_shards(): blocks = lax.psum(blocks.astype(heads_low), both)]
    another operation x29 -> x15, other arithmetic: 164 us -> 8.44 us  [the longest x3 3.5 us: step(): jax.shard_map(local, mesh=mesh, in_specs=in_specs, out_specs=out_specs, c...]
    ppermute x3 -> x42, waiting for transfers between devices: 4.35 us -> 109 us  [the longest x34 105 us: permuted(): return lax.ppermute(value, axis, [(i, i ^ 1 << bit) for i in range(count)])]
    ppermute x3 -> x42, starting transfers between devices: 9.52 us -> 81.1 us  [the longest x34 58 us: permuted(): return lax.ppermute(value, axis, [(i, i ^ 1 << bit) for i in range(count)])]
    psum x1 -> x0, blocking collectives: 42.2 us -> none  [shards(): lax.psum((grad_vector_part, squares_local), ('seq', 'fsdp'))]
  transfers between devices with their start and end apart: 17 -> 48, of which waited for: 15 -> 28; matrix products, arithmetic and copies ran while one was open for 15% -> 17% of each run, Pallas kernels for 0% -> 0%
where the time goes in v1:
time: 801 us; the launch traced here: 793 us
  waiting for transfers between devices  308 us (38%)
  other arithmetic  115 us (14%)
  matrix products  111 us (14%)
  local copies, waits for them, and re-layouts  109 us (14%)
  starting transfers between devices  85.4 us (11%)
  between operations  64.7 us (8%)
    psum x1, waiting for transfers between devices, pair_shards(): blocks = lax.psum(blocks.astype(heads_low), both)  143 us
    ppermute x34, waiting for transfers between devices, permuted(): return lax.ppermute(value, axis, [(i, i ^ 1 << bit) for i in range(count)])  105 us
    ppermute x34, starting transfers between devices, permuted(): return lax.ppermute(value, axis, [(i, i ^ 1 << bit) for i in range(count)])  58 us
    unnamed x403, local copies, waits for them, and re-layouts  50.4 us
    all_gather x1, waiting for transfers between devices, pair_shards(): packed = lax.all_gather(jnp.concatenate([tokens[0], row_ids]), 'seq')  48.7 us
    reduce_sum x4, other arithmetic, thin_update(): inverse_norm = 1.0 / (jnp.sqrt(jnp.trace(gram.astype(jnp.float32))) + 1e-07)  39.5 us
    dot_general x48, matrix products, times(): jnp.dot(rows.astype(jnp.bfloat16), current, preferred_element_type=jnp.fl...  32 us
    ppermute x8, starting transfers between devices, routed(): lax.ppermute(picked(granules, sent[me]), axes, [(src, chosen[src][0]) for...  23.1 us
  transfers between devices with their start and end apart: 48, of which 28 were waited for; matrix products, arithmetic and copies ran while one was open for 17% of the time, Pallas kernels for 0%

profile of v1, /device:TPU:0, one launch (start us, length us, event | category | flops | bytes accessed | tf_op | source)
XLA Modules:
  0.0 792.9 jit_solution(14040528054565675551)
XLA Ops:
  31.0 6.6 all-gather.6.cloned.1.call-done
  43.5 48.7 %all-gather.12.cloned.1.call-done = bf16[1152,1024]{1,0:T(8,128)(2,1)} async-done(((bf16[144,1024]{1,0:T(8,128)(2,1)}), bf16[1152,1024]{1,0:T(8,128)(2,1)}) %all-gather.12.cloned.1.call-update) | async-done | bytes 2359312 | tf_op jit(solution)/shard_map/all_gather | solution.py:798
  92.2 2.1 multiply_reduce_fusion
  95.0 2.0 slice_convert_fusion
  101.4 3.2 fusion.18
  109.5 2.3 fusion.128
  134.4 4.1 all-to-all-start
  145.2 4.6 convert_element_type.558
  151.2 3.6 dynamic-slice_bitcast_fusion
  154.8 12.5 %collective-permute-start.3 = (bf16[704,1024]{1,0:T(8,128)(2,1)}, bf16[704,1024]{1,0:T(8,128)(2,1)}, u32[]{:S(2)}, u32[]{:S(2)}) collective-permute-start(bf16[704,1024]{1,0:T(8,128)(2,1)} %get-tuple-element.156), channel_id=1, source_target_pairs={{0,0},{1,2},{2,1},{3,3},{4,4},{5,6},{6,5},{7,7},{8,8},{9,10},{10,9... | collective-permute-start | bytes 4325384 | tf_op jit(solution)/shard_map/ppermute | solution.py:534
  173.3 3.2 multiply_reduce_fusion.17
  176.7 2.0 collective-permute-start
  179.9 15.6 %collective-permute-done = bf16[1,128,1024]{2,1,0:T(8,128)(2,1)S(1)} collective-permute-done((bf16[1,128,1024]{2,1,0:T(8,128)(2,1)S(1)}, bf16[1,128,1024]{2,1,0:T(8,128)(2,1)S(1)}, u32[]{:S(2)}, u32[]{:S(2)}) %collective-permute-start) | collective-permute-done | bytes 262176 | tf_op jit(solution)/shard_map/ppermute | solution.py:453
  196.1 3.1 fusion.11
  201.6 2.3 fusion.275
  204.0 3.2 fusion.19
  208.7 2.8 copy.272
  211.4 2.1 fusion.106
  214.0 2.3 copy.271
  216.3 3.5 convert_bitcast_fusion
  234.6 6.9 collective-permute-done.9
  242.3 3.8 collective-permute-done.5
  247.4 6.9 collective-permute-done.23
  254.3 2.0 convert_add_fusion.1
  263.9 13.3 %collective-permute-done.24 = bf16[2,3,88,512]{3,2,1,0:T(8,128)(2,1)} collective-permute-done((bf16[2,3,88,512]{3,2,1,0:T(8,128)(2,1)}, bf16[2,3,88,512]{3,2,1,0:T(8,128)(2,1)}, u32[]{:S(2)}, u32[]{:S(2)}) %collective-permute-start.24) | collective-permute-done | bytes 540704 | tf_op jit(solution)/shard_map/ppermute | solution.py:453
  278.9 2.6 collective-permute-start.25
  308.9 4.7 collective-permute-done.25
  314.9 5.4 collective-permute-done.28
  322.3 5.1 collective-permute-start.29
  333.6 3.9 multiply_reduce_fusion.6
  338.3 2.0 fusion.276
  351.4 2.3 multiply_select_fusion
  359.7 2.5 multiply_reduce_fusion.3
  366.2 3.8 fusion.85
  372.5 9.2 %collective-permute-start.21 = (bf16[2,64,1024]{2,1,0:T(8,128)(2,1)}, bf16[2,64,1024]{2,1,0:T(8,128)(2,1)}, u32[]{:S(2)}, u32[]{:S(2)}) collective-permute-start(bf16[2,64,1024]{2,1,0:T(8,128)(2,1)} %fusion.205), channel_id=1, source_target_pairs={{0,1},{1,0},{2,3},{3,2},{4,5},{5,4},{6,7},{7,6},{8,9},{9,8},{10,11... | collective-permute-start | bytes 786440 | tf_op jit(solution)/shard_map/ppermute | solution.py:453
  388.0 5.6 add_convert_fusion
  394.1 2.1 collective-permute-start.13
  396.2 3.1 collective-permute-start.10
  402.3 6.5 collective-permute-done.13
  409.0 3.9 collective-permute-start.14
  414.1 4.9 collective-permute-done.14
  419.2 3.3 collective-permute-start.15
  424.3 7.7 collective-permute-done.15
  432.0 1.9 collective-permute-done.12
  436.7 2.1 collective-permute-start.22
  438.7 2.1 collective-permute-done.38
  445.3 1.9 bitcast_add_fusion
  451.2 4.8 collective-permute-done.41
  456.2 3.6 collective-permute-done.17
  459.9 1.9 collective-permute-start.20
  463.7 4.5 collective-permute-done.20
  471.8 5.8 collective-permute-start.32
  478.4 5.3 collective-permute-start.33
  485.3 3.6 collective-permute-done.34
  489.2 3.3 collective-permute-done.35
  493.6 3.4 collective-permute-done.36
  537.5 143.4 %all-reduce.26.cloned.1.call-done = bf16[40,256,256]{2,1,0:T(8,128)(2,1)} async-done(((bf16[40,256,256]{2,1,0:T(8,128)(2,1)}), bf16[40,256,256]{2,1,0:T(8,128)(2,1)}) %all-reduce.26.cloned.1.call-update) | async-done | bytes 5242896 | tf_op jit(solution)/shard_map/psum | solution.py:997
  681.0 2.8 slice_bitcast_fusion.64
  683.8 2.8 slice_bitcast_fusion.2
  687.6 2.7 slice_bitcast_fusion.66
  707.1 9.5 %fusion = (f32[]{:T(128)}, bf16[1024,1024]{1,0:T(8,128)(2,1)}) fusion(bf16[256,256]{1,0:T(8,128)(2,1)S(1)} %copy-done.85, bf16[256,256]{1,0:T(8,128)(2,1)S(1)} %bitcast.1005, bf16[256,256]{1,0:T(8,128)(2,1)} %copy.284, bf16[256,256]{1,0:T(8,128)(2,1)S(1)} %bitcast.1007, bf16[256,1024]{1,0:T(8,128)(2,1)S(1)} %copy.286, ...), kind=kLoop, calls=%fused_computation.10 | loop fusion | flops 25165824 | bytes 4194308 | tf_op jit(solution)/shard_map/jit(trace)/reduce_sum | solution.py:691
  718.4 4.8 fusion.2
  732.5 15.6 %fusion.4 = (f32[]{:T(128)}, bf16[1024,1024]{1,0:T(8,128)(2,1)}) fusion(bf16[256,256]{1,0:T(8,128)(2,1)S(1)} %copy-done.84, bf16[256,256]{1,0:T(8,128)(2,1)S(1)} %bitcast.993, bf16[256,256]{1,0:T(8,128)(2,1)S(1)} %copy-done.86, bf16[256,256]{1,0:T(8,128)(2,1)S(1)} %bitcast.995, bf16[256,1024]{1,0:T(8,128)(2,1)S(1)} %copy.306, ...), kind=kLoop, calls=%fused_computation.14 | loop fusion | flops 25165824 | bytes 4194308 | tf_op jit(solution)/shard_map/jit(trace)/reduce_sum | solution.py:691
  749.2 9.6 %fusion.6 = (f32[]{:T(128)}, bf16[1024,1024]{1,0:T(8,128)(2,1)S(1)}) fusion(bf16[256,256]{1,0:T(8,128)(2,1)} %get-tuple-element.145, bf16[256,256]{1,0:T(8,128)(2,1)} %copy.312, bf16[256,256]{1,0:T(8,128)(2,1)S(1)} %bitcast.989, bf16[256,256]{1,0:T(8,128)(2,1)} %copy.311, bf16[256,256]{1,0:T(8,128)(2,1)} %get-tuple-element.144, ...), kind=kLoop, calls=%fused_computation.16 | loop fusion | flops 31457280 | bytes 4194308 | tf_op jit(solution)/shard_map/jit(trace)/reduce_sum | solution.py:691
  (794 shorter events, 251.5 us)
Async XLA Ops:
  7.2 30.4 %all-gather.6.cloned.1.call-start = ((), (), s32[]{:S(2)}) async-start(), calls=%async_computation.1 | async-start | bytes 2621440 | tf_op jit(solution)/shard_map/all_gather | solution.py:809
  12.2 80.0 %all-gather.12.cloned.1.call-start = ((), (), s32[]{:S(2)}) async-start(), calls=%async_computation.5 | async-start | bytes 2654208 | tf_op jit(solution)/shard_map/all_gather | solution.py:798
  13.0 160.2 %all-gather.8.cloned.1.call-start = ((), (), s32[]{:S(2)}) async-start(), calls=%async_computation.2 | async-start | bytes 5242880 | tf_op jit(solution)/shard_map/all_gather | solution.py:824
  26.0 75.4 %copy-start.117 = (f32[1,512]{1,0:T(1,128)}, f32[1,512]{1,0:T(1,128)S(1)}, u32[]{:S(2)}) copy-start(f32[1,512]{1,0:T(1,128)S(1)} %get-tuple-element.225) | copy-start | bytes 6148
  26.0 75.4 %copy-start.119 = (f32[1,512]{1,0:T(1,128)}, f32[1,512]{1,0:T(1,128)S(1)}, u32[]{:S(2)}) copy-start(f32[1,512]{1,0:T(1,128)S(1)} %get-tuple-element.226) | copy-start | bytes 6148
  26.0 75.3 %copy-start.121 = (f32[1,512]{1,0:T(1,128)}, f32[1,512]{1,0:T(1,128)S(1)}, u32[]{:S(2)}) copy-start(f32[1,512]{1,0:T(1,128)S(1)} %get-tuple-element.227) | copy-start | bytes 6148
  26.1 75.3 %copy-start.123 = (f32[1,512]{1,0:T(1,128)}, f32[1,512]{1,0:T(1,128)S(1)}, u32[]{:S(2)}) copy-start(f32[1,512]{1,0:T(1,128)S(1)} %get-tuple-element.228) | copy-start | bytes 6148
  30.0 75.0 %copy-start.101 = (f32[1,1024]{1,0:T(1,128)}, f32[1,1024]{1,0:T(1,128)S(1)}, u32[]{:S(2)}) copy-start(f32[1,1024]{1,0:T(1,128)S(1)} %get-tuple-element.219) | copy-start | bytes 12292
  30.0 75.0 %copy-start.103 = (f32[1,1024]{1,0:T(1,128)}, f32[1,1024]{1,0:T(1,128)S(1)}, u32[]{:S(2)}) copy-start(f32[1,1024]{1,0:T(1,128)S(1)} %get-tuple-element.220) | copy-start | bytes 12292
  43.5 54.9 %copy-start.99 = (bf16[768,1024]{1,0:T(8,128)(2,1)}, bf16[768,1024]{1,0:T(8,128)(2,1)S(1)}, u32[]{:S(2)}) copy-start(bf16[768,1024]{1,0:T(8,128)(2,1)S(1)} %bitcast_dynamic-update-slice_fusion) | copy-start | bytes 4718596
  134.4 38.9 %all-to-all-start = ((bf16[8,128,256]{1,2,0:T(8,128)(2,1)}), bf16[8,128,256]{1,2,0:T(8,128)(2,1)}, u32[]{:S(2)}, u32[]{:S(2)}) async-start(bf16[8,128,256]{1,2,0:T(8,128)(2,1)} %copy.249), calls=%async_computation | async-start | bytes 1048576 | tf_op jit(solution)/shard_map/all_to_all | solution.py:865
  138.5 195.0 %all-gather.10.cloned.1.call-start = ((), (), s32[]{:S(2)}) async-start(), calls=%async_computation.3 | async-start | bytes 2359296 | tf_op jit(solution)/shard_map/all_gather | solution.py:895
  138.6 32.6 %collective-permute-start.6 = (bf16[1,128,1024]{2,1,0:T(8,128)(2,1)}, bf16[1,128,1024]{2,1,0:T(8,128)(2,1)}, u32[]{:S(2)}, u32[]{:S(2)}) collective-permute-start(bf16[1,128,1024]{2,1,0:T(8,128)(2,1)} %param.34), channel_id=1, source_target_pairs={{0,2},{1,3},{2,0},{3,1},{4,6},{5,7},{6,4},{7,5},{8,10},{9,11},{10,... | collective-permute-start | bytes 786440 | tf_op jit(solution)/shard_map/ppermute | solution.py:453
  154.8 41.3 %collective-permute-start.3 = (bf16[704,1024]{1,0:T(8,128)(2,1)}, bf16[704,1024]{1,0:T(8,128)(2,1)}, u32[]{:S(2)}, u32[]{:S(2)}) collective-permute-start(bf16[704,1024]{1,0:T(8,128)(2,1)} %get-tuple-element.156), channel_id=1, source_target_pairs={{0,0},{1,2},{2,1},{3,3},{4,4},{5,6},{6,5},{7,7},{8,8},{9,10},{10,9... | collective-permute-start | bytes 4325384 | tf_op jit(solution)/shard_map/ppermute | solution.py:534
  167.3 28.7 %collective-permute-start.2 = (bf16[704,1024]{1,0:T(8,128)(2,1)}, bf16[704,1024]{1,0:T(8,128)(2,1)}, u32[]{:S(2)}, u32[]{:S(2)}) collective-permute-start(bf16[704,1024]{1,0:T(8,128)(2,1)} %get-tuple-element.157), channel_id=1, source_target_pairs={{0,1},{1,3},{2,0},{3,2},{4,5},{5,7},{6,4},{7,6},{8,9},{9,11},{10,8... | collective-permute-start | bytes 4325384 | tf_op jit(solution)/shard_map/ppermute | solution.py:534
  173.2 5.5 collective-permute-start.7
  176.7 18.9 %collective-permute-start = (bf16[1,128,1024]{2,1,0:T(8,128)(2,1)S(1)}, bf16[1,128,1024]{2,1,0:T(8,128)(2,1)S(1)}, u32[]{:S(2)}, u32[]{:S(2)}) collective-permute-start(bf16[1,128,1024]{2,1,0:T(8,128)(2,1)S(1)} %fusion.199), channel_id=1, source_target_pairs={{0,2},{1,3},{2,0},{3,1},{4,6},{5,7},{6,4},{7,5},{8,10},{9,11},{10,... | collective-permute-start | bytes 786440 | tf_op jit(solution)/shard_map/ppermute | solution.py:453
  195.8 3.4 collective-permute-start.1
  213.5 17.4 %collective-permute-start.8 = (bf16[2,128,1024]{2,1,0:T(8,128)(2,1)}, bf16[2,128,1024]{2,1,0:T(8,128)(2,1)}, u32[]{:S(2)}, u32[]{:S(2)}) collective-permute-start(bf16[2,128,1024]{2,1,0:T(8,128)(2,1)} %fusion.106), channel_id=1, source_target_pairs={{0,1},{1,0},{2,3},{3,2},{4,5},{5,4},{6,7},{7,6},{8,9},{9,8},{10,11... | collective-permute-start | bytes 1572872 | tf_op jit(solution)/shard_map/ppermute | solution.py:453
  225.3 8.3 %collective-permute-start.4 = (bf16[2,128,1024]{2,1,0:T(8,128)(2,1)S(1)}, bf16[2,128,1024]{2,1,0:T(8,128)(2,1)S(1)}, u32[]{:S(2)}, u32[]{:S(2)}) collective-permute-start(bf16[2,128,1024]{2,1,0:T(8,128)(2,1)S(1)} %fusion.107), channel_id=1, source_target_pairs={{0,1},{1,0},{2,3},{3,2},{4,5},{5,4},{6,7},{7,6},{8,9},{9,8},{10,11... | collective-permute-start | bytes 1572872 | tf_op jit(solution)/shard_map/ppermute | solution.py:453
  227.7 26.6 %collective-permute-start.23 = (bf16[2,2,3,88,512]{4,3,2,0,1:T(8,128)(2,1)}, bf16[2,2,3,88,512]{4,3,2,0,1:T(8,128)(2,1)}, u32[]{:S(2)}, u32[]{:S(2)}) collective-permute-start(bf16[2,2,3,88,512]{4,3,2,0,1:T(8,128)(2,1)} %bitcast.938), channel_id=1, source_target_pairs={{0,4},{4,0},{8,12},{12,8},{16,20},{20,16},{24,28},{28,24},{1,5},{5... | collective-permute-start | bytes 3244040 | tf_op jit(solution)/shard_map/ppermute | solution.py:453
  229.4 29.6 %collective-permute-start.26 = (bf16[2,2,3,88,512]{4,3,2,0,1:T(8,128)(2,1)}, bf16[2,2,3,88,512]{4,3,2,0,1:T(8,128)(2,1)}, u32[]{:S(2)}, u32[]{:S(2)}) collective-permute-start(bf16[2,2,3,88,512]{4,3,2,0,1:T(8,128)(2,1)} %bitcast.937), channel_id=1, source_target_pairs={{0,8},{4,12},{8,0},{12,4},{16,24},{20,28},{24,16},{28,20},{1,9},{5... | collective-permute-start | bytes 3244040 | tf_op jit(solution)/shard_map/ppermute | solution.py:453
  232.2 9.2 %collective-permute-start.9 = (bf16[128,1024]{1,0:T(8,128)(2,1)S(1)}, bf16[128,1024]{1,0:T(8,128)(2,1)S(1)}, u32[]{:S(2)}, u32[]{:S(2)}) collective-permute-start(bf16[128,1024]{1,0:T(8,128)(2,1)S(1)} %fusion.201), channel_id=1, source_target_pairs={{0,2},{1,3},{2,0},{3,1},{4,6},{5,7},{6,4},{7,5},{8,10},{9,11},{10,... | collective-permute-start | bytes 786440 | tf_op jit(solution)/shard_map/ppermute | solution.py:453
  233.7 12.3 %collective-permute-start.5 = (bf16[128,1024]{1,0:T(8,128)(2,1)S(1)}, bf16[128,1024]{1,0:T(8,128)(2,1)S(1)}, u32[]{:S(2)}, u32[]{:S(2)}) collective-permute-start(bf16[128,1024]{1,0:T(8,128)(2,1)S(1)} %fusion.200), channel_id=1, source_target_pairs={{0,2},{1,3},{2,0},{3,1},{4,6},{5,7},{6,4},{7,5},{8,10},{9,11},{10,... | collective-permute-start | bytes 786440 | tf_op jit(solution)/shard_map/ppermute | solution.py:453
  247.3 433.6 %all-reduce.26.cloned.1.call-start = ((), (), s32[]{:S(2)}) async-start(), calls=%async_computation.4 | async-start | bytes 10485760 | tf_op jit(solution)/shard_map/psum | solution.py:997
  257.3 19.9 %collective-permute-start.24 = (bf16[2,3,88,512]{3,2,1,0:T(8,128)(2,1)}, bf16[2,3,88,512]{3,2,1,0:T(8,128)(2,1)}, u32[]{:S(2)}, u32[]{:S(2)}) collective-permute-start(bf16[2,3,88,512]{3,2,1,0:T(8,128)(2,1)} %fusion.95), channel_id=1, source_target_pairs={{0,8},{4,12},{8,0},{12,4},{16,24},{20,28},{24,16},{28,20},{1,9},{5... | collective-permute-start | bytes 1622024 | tf_op jit(solution)/shard_map/ppermute | solution.py:453
  262.3 19.2 %collective-permute-start.27 = (bf16[2,3,88,512]{3,2,1,0:T(8,128)(2,1)}, bf16[2,3,88,512]{3,2,1,0:T(8,128)(2,1)}, u32[]{:S(2)}, u32[]{:S(2)}) collective-permute-start(bf16[2,3,88,512]{3,2,1,0:T(8,128)(2,1)} %fusion.96), channel_id=1, source_target_pairs={{0,4},{4,0},{8,12},{12,8},{16,20},{20,16},{24,28},{28,24},{1,5},{5... | collective-permute-start | bytes 1622024 | tf_op jit(solution)/shard_map/ppermute | solution.py:453
  278.9 23.0 %copy-start.151 = (s32[32]{0:T(128)S(1)}, s32[32]{0:T(128)}, u32[]{:S(2)}) copy-start(s32[32]{0:T(128)} %constant.541.clone) | copy-start | bytes 388
  278.9 24.9 %copy-start.150 = (s32[32]{0:T(128)S(1)}, s32[32]{0:T(128)}, u32[]{:S(2)}) copy-start(s32[32]{0:T(128)} %constant.540.clone) | copy-start | bytes 388
  278.9 34.7 %collective-permute-start.25 = (bf16[3,88,512]{2,1,0:T(8,128)(2,1)S(1)}, bf16[3,88,512]{2,1,0:T(8,128)(2,1)}, u32[]{:S(2)}, u32[]{:S(2)}) collective-permute-start(bf16[3,88,512]{2,1,0:T(8,128)(2,1)S(1)} %fusion.188), channel_id=1, source_target_pairs={{0,16},{4,20},{8,24},{12,28},{16,0},{20,4},{24,8},{28,12},{1,17},{... | collective-permute-start | bytes 811016 | tf_op jit(solution)/shard_map/ppermute | solution.py:453
  282.8 44.7 %copy-start.131 = (f32[8,128]{1,0:T(8,128)S(1)}, f32[8,128]{1,0:T(8,128)}, u32[]{:S(2)}) copy-start(f32[8,128]{1,0:T(8,128)} %get-tuple-element.234) | copy-start | bytes 12292
  283.9 36.5 %collective-permute-start.28 = (bf16[3,88,512]{2,1,0:T(8,128)(2,1)}, bf16[3,88,512]{2,1,0:T(8,128)(2,1)}, u32[]{:S(2)}, u32[]{:S(2)}) collective-permute-start(bf16[3,88,512]{2,1,0:T(8,128)(2,1)} %fusion.189), channel_id=1, source_target_pairs={{0,16},{4,20},{8,24},{12,28},{16,0},{20,4},{24,8},{28,12},{1,17},{... | collective-permute-start | bytes 811016 | tf_op jit(solution)/shard_map/ppermute | solution.py:453
  321.6 8.8 %collective-permute-start.30 = (bf16[88,1024]{1,0:T(8,128)(2,1)S(1)}, bf16[88,1024]{1,0:T(8,128)(2,1)S(1)}, u32[]{:S(2)}, u32[]{:S(2)}) collective-permute-start(bf16[88,1024]{1,0:T(8,128)(2,1)S(1)} %get-tuple-element.199), channel_id=1, source_target_pairs={{0,0},{1,4},{2,8},{3,12},{4,16},{5,20},{6,24},{7,28},{8,1},{9,5},{... | collective-permute-start | bytes 540680 | tf_op jit(solution)/shard_map/ppermute | solution.py:534
  322.3 8.2 %collective-permute-start.29 = (bf16[88,1024]{1,0:T(8,128)(2,1)S(1)}, bf16[88,1024]{1,0:T(8,128)(2,1)S(1)}, u32[]{:S(2)}, u32[]{:S(2)}) collective-permute-start(bf16[88,1024]{1,0:T(8,128)(2,1)S(1)} %get-tuple-element.200), channel_id=1, source_target_pairs={{0,16},{1,20},{2,24},{3,28},{4,0},{5,4},{6,8},{7,12},{8,17},{9,21}... | collective-permute-start | bytes 540680 | tf_op jit(solution)/shard_map/ppermute | solution.py:534
  329.3 2.9 collective-permute-start.31
  372.5 62.9 %collective-permute-start.21 = (bf16[2,64,1024]{2,1,0:T(8,128)(2,1)}, bf16[2,64,1024]{2,1,0:T(8,128)(2,1)}, u32[]{:S(2)}, u32[]{:S(2)}) collective-permute-start(bf16[2,64,1024]{2,1,0:T(8,128)(2,1)} %fusion.205), channel_id=1, source_target_pairs={{0,1},{1,0},{2,3},{3,2},{4,5},{5,4},{6,7},{7,6},{8,9},{9,8},{10,11... | collective-permute-start | bytes 786440 | tf_op jit(solution)/shard_map/ppermute | solution.py:453
  394.1 14.7 %collective-permute-start.13 = (bf16[2,2,128,512]{3,2,0,1:T(8,128)(2,1)S(1)}, bf16[2,2,128,512]{3,2,0,1:T(8,128)(2,1)S(1)}, u32[]{:S(2)}, u32[]{:S(2)}) collective-permute-start(bf16[2,2,128,512]{3,2,0,1:T(8,128)(2,1)S(1)} %bitcast.1021), channel_id=1, source_target_pairs={{0,8},{4,12},{8,0},{12,4},{16,24},{20,28},{24,16},{28,20},{1,9},{5... | collective-permute-start | bytes 1572872 | tf_op jit(solution)/shard_map/ppermute | solution.py:453
  396.2 16.7 %collective-permute-start.10 = (bf16[2,2,128,512]{3,2,0,1:T(8,128)(2,1)S(1)}, bf16[2,2,128,512]{3,2,0,1:T(8,128)(2,1)S(1)}, u32[]{:S(2)}, u32[]{:S(2)}) collective-permute-start(bf16[2,2,128,512]{3,2,0,1:T(8,128)(2,1)S(1)} %bitcast.1020), channel_id=1, source_target_pairs={{0,4},{4,0},{8,12},{12,8},{16,20},{20,16},{24,28},{28,24},{1,5},{5... | collective-permute-start | bytes 1572872 | tf_op jit(solution)/shard_map/ppermute | solution.py:453
  402.3 42.9 %collective-permute-start.16 = (bf16[2,192,1024]{2,1,0:T(8,128)(2,1)}, bf16[2,192,1024]{2,1,0:T(8,128)(2,1)}, u32[]{:S(2)}, u32[]{:S(2)}) collective-permute-start(bf16[2,192,1024]{2,1,0:T(8,128)(2,1)} %fusion.87), channel_id=1, source_target_pairs={{0,1},{1,0},{2,3},{3,2},{4,5},{5,4},{6,7},{7,6},{8,9},{9,8},{10,11... | collective-permute-start | bytes 2359304 | tf_op jit(solution)/shard_map/ppermute | solution.py:453
  409.0 10.1 %collective-permute-start.14 = (bf16[2,128,512]{2,1,0:T(8,128)(2,1)S(1)}, bf16[2,128,512]{2,1,0:T(8,128)(2,1)S(1)}, u32[]{:S(2)}, u32[]{:S(2)}) collective-permute-start(bf16[2,128,512]{2,1,0:T(8,128)(2,1)S(1)} %fusion.203), channel_id=1, source_target_pairs={{0,4},{4,0},{8,12},{12,8},{16,20},{20,16},{24,28},{28,24},{1,5},{5... | collective-permute-start | bytes 786440 | tf_op jit(solution)/shard_map/ppermute | solution.py:453
  413.2 9.3 %collective-permute-start.11 = (bf16[2,128,512]{2,1,0:T(8,128)(2,1)S(1)}, bf16[2,128,512]{2,1,0:T(8,128)(2,1)S(1)}, u32[]{:S(2)}, u32[]{:S(2)}) collective-permute-start(bf16[2,128,512]{2,1,0:T(8,128)(2,1)S(1)} %fusion.202), channel_id=1, source_target_pairs={{0,8},{4,12},{8,0},{12,4},{16,24},{20,28},{24,16},{28,20},{1,9},{5... | collective-permute-start | bytes 786440 | tf_op jit(solution)/shard_map/ppermute | solution.py:453
  419.2 12.7 %collective-permute-start.15 = (bf16[128,512]{1,0:T(8,128)(2,1)S(1)}, bf16[128,512]{1,0:T(8,128)(2,1)S(1)}, u32[]{:S(2)}, u32[]{:S(2)}) collective-permute-start(bf16[128,512]{1,0:T(8,128)(2,1)S(1)} %fusion.281), channel_id=1, source_target_pairs={{0,16},{4,20},{8,24},{12,28},{16,0},{20,4},{24,8},{28,12},{1,17},{... | collective-permute-start | bytes 393224 | tf_op jit(solution)/shard_map/ppermute | solution.py:453
  422.6 11.3 %collective-permute-start.12 = (bf16[128,512]{1,0:T(8,128)(2,1)S(1)}, bf16[128,512]{1,0:T(8,128)(2,1)S(1)}, u32[]{:S(2)}, u32[]{:S(2)}) collective-permute-start(bf16[128,512]{1,0:T(8,128)(2,1)S(1)} %fusion.280), channel_id=1, source_target_pairs={{0,16},{4,20},{8,24},{12,28},{16,0},{20,4},{24,8},{28,12},{1,17},{... | collective-permute-start | bytes 393224 | tf_op jit(solution)/shard_map/ppermute | solution.py:453
  435.4 1.2 collective-permute-start.37
  436.6 4.2 collective-permute-start.38
  436.7 6.4 collective-permute-start.22
  440.8 3.9 collective-permute-start.39
  443.7 55.2 %copy-start.71 = (f32[64,1024]{1,0:T(8,128)}, f32[64,1024]{1,0:T(8,128)S(1)}, u32[]{:S(2)}) copy-start(f32[64,1024]{1,0:T(8,128)S(1)} %get-tuple-element.81) | copy-start | bytes 786436
  444.8 4.2 collective-permute-start.40
  449.0 7.0 collective-permute-start.41
  451.0 8.8 %collective-permute-start.17 = (bf16[192,1024]{1,0:T(8,128)(2,1)S(1)}, bf16[192,1024]{1,0:T(8,128)(2,1)S(1)}, u32[]{:S(2)}, u32[]{:S(2)}) collective-permute-start(bf16[192,1024]{1,0:T(8,128)(2,1)S(1)} %fusion.131), channel_id=1, source_target_pairs={{0,2},{1,3},{2,0},{3,1},{4,6},{5,7},{6,4},{7,5},{8,10},{9,11},{10,... | collective-permute-start | bytes 1179656 | tf_op jit(solution)/shard_map/ppermute | solution.py:453
  459.9 8.3 %collective-permute-start.20 = (bf16[64,1024]{1,0:T(8,128)(2,1)S(1)}, bf16[64,1024]{1,0:T(8,128)(2,1)S(1)}, u32[]{:S(2)}, u32[]{:S(2)}) collective-permute-start(bf16[64,1024]{1,0:T(8,128)(2,1)S(1)} %get-tuple-element.194), channel_id=1, source_target_pairs={{0,5},{1,11},{2,21},{3,22},{4,0},{5,6},{6,12},{7,23},{8,1},{9,13},... | collective-permute-start | bytes 393224 | tf_op jit(solution)/shard_map/ppermute | solution.py:534
  461.9 6.3 collective-permute-start.19
  462.5 5.7 collective-permute-start.18
  469.2 36.3 %copy-start.40 = (f32[192,1024]{1,0:T(8,128)}, f32[192,1024]{1,0:T(8,128)S(1)}, u32[]{:S(2)}) copy-start(f32[192,1024]{1,0:T(8,128)S(1)} %get-tuple-element.83) | copy-start | bytes 2359300
  471.8 6.6 collective-permute-start.32
  478.4 6.9 collective-permute-start.33
  485.3 3.6 collective-permute-start.34
  488.9 3.6 collective-permute-start.35
  489.2 47.5 %copy-start.60 = (f32[35088]{0:T(1024)}, f32[35088]{0:T(1024)S(1)}, u32[]{:S(2)}) copy-start(f32[35088]{0:T(1024)S(1)} %concatenate.132) | copy-start | bytes 421060
  492.5 4.5 collective-permute-start.36
  502.7 257.4 %copy-start.37 = (f32[88,1024]{1,0:T(8,128)}, f32[88,1024]{1,0:T(8,128)S(1)}, u32[]{:S(2)}) copy-start(f32[88,1024]{1,0:T(8,128)S(1)} %get-tuple-element.65) | copy-start | bytes 1081348
  691.2 26.1 %copy-start.68 = (bf16[1,256,256]{1,2,0:T(8,128)(2,1)}, bf16[1,256,256]{1,2,0:T(8,128)(2,1)S(1)}, u32[]{:S(2)}) copy-start(bf16[1,256,256]{1,2,0:T(8,128)(2,1)S(1)} %copy.342) | copy-start | bytes 393220
  691.3 26.0 %copy-start.69 = (bf16[1,256,256]{1,2,0:T(8,128)(2,1)}, bf16[1,256,256]{1,2,0:T(8,128)(2,1)S(1)}, u32[]{:S(2)}) copy-start(bf16[1,256,256]{1,2,0:T(8,128)(2,1)S(1)} %copy.340) | copy-start | bytes 393220
  (146 other events, 808.1 us)
Sparse Core Ops, SparseCore 0:
  12.3 25.2 all-gather.5
  40.4 51.7 all-gather.11
  93.8 33.0 all-gather.7
  247.4 68.9 all-gather.9
  534.9 146.0 all-reduce.25

commit v2 on v1

--- a/solution.py
+++ b/solution.py
@@ -3,6 +3,8 @@
 import jax
 import jax.numpy as jnp
 from jax import lax
+from jax.experimental import pallas as pl
+from jax.experimental.pallas import tpu as pltpu
 from jax.sharding import PartitionSpec as P
 
 D = 1024
@@ -448,51 +450,67 @@
     )
 
 
-def permuted(value, axis, bit):
-    count = lax.axis_size(axis)
-    return lax.ppermute(value, axis, [(i, i ^ (1 << bit)) for i in range(count)])
+Z_LINE = ("seq", (1, 2))
+X_PAIR = ("seq", (0,))
+Y_PAIR = ("fsdp", (1,))
+CORES = ("fsdp", (0,))
+SEQ_LAYOUT = (Z_LINE, X_PAIR)
+FSDP_LAYOUT = (Y_PAIR, CORES)
+
+
+def exchanged(value, group, offset):
+    axis, bits = group
+    mask = sum(1 << bit for i, bit in enumerate(bits) if (offset >> i) & 1)
+    return lax.ppermute(value, axis, [(i, i ^ mask) for i in range(lax.axis_size(axis))])
+
+
+def place_in(group):
+    axis, bits = group
+    mine = lax.axis_index(axis)
+    return sum(((mine >> bit) & 1) << i for i, bit in enumerate(bits))
 
 
 def picked(value, index, position=0):
     return lax.dynamic_index_in_dim(value, index, position, keepdims=False)
 
 
-def scattered_sum(parts, axis, order, wire=jnp.bfloat16):
-    width = len(order)
-    mine = lax.axis_index(axis)
-    held = parts.reshape((2,) * width + parts.shape[1:])
-    left = list(range(width - 1, -1, -1))
-    for bit in order:
-        position = left.index(bit)
-        value = (mine >> bit) & 1
-        keep = picked(held, value, position)
-        gone = picked(held, 1 - value, position)
-        held = keep.astype(jnp.float32) + permuted(gone.astype(wire), axis, bit).astype(jnp.float32)
-        left.remove(bit)
+def scattered_sum(parts, layout, order, wire=jnp.bfloat16):
+    sizes = tuple(2 ** len(bits) for _, bits in layout)
+    held = parts.reshape(sizes + parts.shape[1:])
+    left = list(layout)
+    for group in order:
+        position, place = (left.index(group), place_in(group))
+        total = picked(held, place, position).astype(jnp.float32)
+        for offset in range(1, 2 ** len(group[1])):
+            gone = picked(held, place ^ offset, position).astype(wire)
+            total = total + exchanged(gone, group, offset).astype(jnp.float32)
+        held = total
+        left.remove(group)
     return held
 
 
-def gathered(value, axis, order):
-    mine = lax.axis_index(axis)
-    held = value[None]
+def gathered(value, layout, order):
+    held = value
     done = []
-    for bit in order:
-        other = permuted(held, axis, bit)
-        high = ((mine >> bit) & 1) == 1
-        first = jnp.where(high, other, held)
-        second = jnp.where(high, held, other)
-        joined = jnp.stack([first, second])
-        place = sum(1 for d in done if d > bit)
-        shape = (2,) * (len(done) + 1) + value.shape
-        joined = jnp.moveaxis(joined.reshape(shape), 0, place)
-        done = sorted(done + [bit], reverse=True)
-        held = joined.reshape((2 ** len(done),) + value.shape)
-    return held
-
-
-def summed_everywhere(value, axes_bits):
-    for axis, bit in axes_bits:
-        value = value + permuted(value, axis, bit)
+    for group in order:
+        count, place = (2 ** len(group[1]), place_in(group))
+        pieces = [held] + [exchanged(held, group, offset) for offset in range(1, count)]
+        rows = []
+        for k in range(count):
+            row = pieces[0]
+            for offset in range(1, count):
+                row = jnp.where((place ^ k) == offset, pieces[offset], row)
+            rows.append(row)
+        spot = sum(1 for other in done if layout.index(other) < layout.index(group))
+        held = jnp.stack(rows, axis=spot)
+        done.append(group)
+    return held.reshape((-1,) + value.shape)
+
+
+def summed_over(value, group_list):
+    for group in group_list:
+        others = [exchanged(value, group, offset) for offset in range(1, 2 ** len(group[1]))]
+        value = sum(others, value)
     return value
 
 
@@ -660,39 +678,55 @@
     return jnp.stack(after[::-1])
 
 
-def gram_panels(matrix):
-    side = D // 4
-    narrow = matrix.astype(jnp.bfloat16)
-    blocks = []
-    for i in range(4):
-        panel = contract_first(narrow[:, i * side : (i + 1) * side], narrow[:, i * side :])
-        for j in range(4 - i):
-            blocks.append(panel[:, j * side : (j + 1) * side])
-    return blocks
-
-
-def gram_whole(blocks):
-    index = {}
+BLOCK = 128
+SIDE = D // BLOCK
+PACK = SIDE * (SIDE + 1) // 2
+
+
+def gram_kernel(rows_ref, blocks_ref):
     count = 0
-    for i in range(4):
-        for j in range(i, 4):
-            index[i, j] = count
+    for i in range(SIDE):
+        left = rows_ref[0, :, i * BLOCK : (i + 1) * BLOCK]
+        panel = contract_first(left, rows_ref[0, :, i * BLOCK :])
+        for j in range(SIDE - i):
+            blocks_ref[count] = panel[:, j * BLOCK : (j + 1) * BLOCK].astype(jnp.bfloat16)
             count += 1
-    rows = [
-        jnp.concatenate(
-            [blocks[index[i, j]] if i <= j else blocks[index[j, i]].T for j in range(4)], axis=1
-        )
-        for i in range(4)
-    ]
-    return jnp.concatenate(rows, axis=0)
-
-
-def thin_update(block_rows, gram, total_rows):
-    inverse_norm = 1.0 / (jnp.sqrt(jnp.trace(gram.astype(jnp.float32))) + 1e-07)
-    current = (gram.astype(jnp.float32) * (inverse_norm * inverse_norm)).astype(jnp.bfloat16)
+
+
+def gram_blocks(rows):
+    count, height, width = rows.shape
+    return pl.pallas_call(
+        gram_kernel,
+        grid=(count,),
+        in_specs=[pl.BlockSpec((1, height, width), lambda m: (m, 0, 0))],
+        out_specs=pl.BlockSpec((PACK, BLOCK, BLOCK), lambda m: (m, 0, 0)),
+        out_shape=jax.ShapeDtypeStruct((count * PACK, BLOCK, BLOCK), jnp.bfloat16),
+        name="gram_blocks",
+    )(rows)
+
+
+def muon_kernel(rates_ref, rows_ref, blocks_ref, out_ref, gram_ref):
+    count = 0
+    trace = jnp.zeros((BLOCK, BLOCK), jnp.float32)
+    line = lax.broadcasted_iota(jnp.int32, (BLOCK, BLOCK), 0)
+    column = lax.broadcasted_iota(jnp.int32, (BLOCK, BLOCK), 1)
+    for i in range(SIDE):
+        for j in range(i, SIDE):
+            block = blocks_ref[count]
+            gram_ref[i * BLOCK : (i + 1) * BLOCK, j * BLOCK : (j + 1) * BLOCK] = block
+            if i == j:
+                trace = trace + jnp.where(line == column, block.astype(jnp.float32), 0.0)
+            else:
+                turned = block.astype(jnp.float32).T.astype(jnp.bfloat16)
+                gram_ref[j * BLOCK : (j + 1) * BLOCK, i * BLOCK : (i + 1) * BLOCK] = turned
+            count += 1
+    total = jnp.sum(jnp.sum(trace, axis=1, keepdims=True), axis=0, keepdims=True)
+    inverse_norm = 1.0 / (jnp.sqrt(total) + 1e-07)
+    squared = inverse_norm * inverse_norm
 
     def times(rows):
-        return jnp.dot(rows.astype(jnp.bfloat16), current, preferred_element_type=jnp.float32)
+        narrow = rows.astype(jnp.bfloat16)
+        return jnp.dot(narrow, gram_ref[...], preferred_element_type=jnp.float32) * squared
 
     def through(rows):
         once = times(rows)
@@ -701,10 +735,38 @@
     def advanced(rows):
         return through(through(times(rows)))
 
-    first = through(block_rows * inverse_norm)
+    first = through(rows_ref[0] * inverse_norm)
     once = advanced(first)
     ortho = NS_A * first + NS_B * once + NS_C * advanced(once)
-    return -LEARN_RATE * 0.2 * math.sqrt(max(total_rows, D)) * ortho
+    out_ref[0] = ortho * rates_ref[pl.program_id(0)]
+
+
+def muon_rows(rows, blocks, rates):
+    count, height, width = rows.shape
+    return pl.pallas_call(
+        muon_kernel,
+        grid_spec=pltpu.PrefetchScalarGridSpec(
+            num_scalar_prefetch=1,
+            grid=(count,),
+            in_specs=[
+                pl.BlockSpec((1, height, width), lambda m, _: (m, 0, 0)),
+                pl.BlockSpec((PACK, BLOCK, BLOCK), lambda m, _: (m, 0, 0)),
+            ],
+            out_specs=pl.BlockSpec((1, height, width), lambda m, _: (m, 0, 0)),
+            scratch_shapes=[pltpu.VMEM((D, D), jnp.bfloat16)],
+        ),
+        out_shape=jax.ShapeDtypeStruct(rows.shape, jnp.float32),
+        name="muon_rows",
+    )(rates, rows, blocks)
+
+
+def blocks_everywhere(blocks):
+    whole = blocks.reshape(2, 32, -1, BLOCK)
+    halves = []
+    for half, order in ((0, (CORES, Y_PAIR, X_PAIR, Z_LINE)), (1, (CORES, X_PAIR, Y_PAIR, Z_LINE))):
+        own = scattered_sum(whole[half], order, order).astype(jnp.bfloat16)
+        halves.append(gathered(own, order, order[::-1]))
+    return jnp.stack(halves).reshape(blocks.shape)
 
 
 def head_tables(fsdp):
@@ -756,7 +818,7 @@
     ]
 
 
-def down_targets(seq, fsdp):
+def block_targets(seq, fsdp):
     return [[(f * seq + s, 0)] for s in range(seq) for f in range(fsdp)]
 
 
@@ -784,8 +846,7 @@
     seq, fsdp = (lax.axis_size("seq"), lax.axis_size("fsdp"))
     head, group = (lax.axis_index("seq"), lax.axis_index("fsdp"))
     me = head * fsdp + group
-    seq_bits, fsdp_bits = (seq.bit_length() - 1, fsdp.bit_length() - 1)
-    fsdp_order = list(range(fsdp_bits))
+    inward, outward = ((CORES, Y_PAIR), (Y_PAIR, CORES))
     projection, conv_taps, gain_one, gain_two, gain_head, decay_log, decay_bias = unpack_vectors(
         vectors
     )
@@ -796,8 +857,6 @@
     row_ids = jnp.zeros((16, D), heads_low)
     row_ids = row_ids.at[0, :own].set((segments[0] + 1).astype(heads_low))
     packed = lax.all_gather(jnp.concatenate([tokens[0], row_ids]), "seq")
-    token_seq = packed[:, :own].reshape(length, D)
-    ids = packed[:, own, :own].reshape(length).astype(jnp.float32)
 
     give, find = head_tables(fsdp)
     give_table = jnp.asarray(give, jnp.int32)
@@ -806,8 +865,8 @@
         lax.dynamic_slice_in_dim(weight_in, give_table[head, group, j] * DKH, DKH, 0)
         for j in range(2)
     ]
-    given = lax.all_gather(jnp.stack(slices).astype(heads_low), "fsdp", axis=0, tiled=True)
-    head_rows = jnp.concatenate([picked(given, find_table[head, j]) for j in range(6)])
+    given = gathered(jnp.stack(slices).astype(heads_low), FSDP_LAYOUT, outward)
+    given = given.reshape(2 * fsdp, DKH, D)
     small_rows = jnp.stack([picked(projection, head), picked(projection, H + head)])
     taps_rows = conv_taps.reshape(KCONV, 4 * H, DKH)
     taps_head = jnp.concatenate(
@@ -822,7 +881,7 @@
     rate, bias = (decay_log[head], decay_bias[head])
 
     full_out = lax.all_gather(weight_out.astype(heads_low), "fsdp", axis=0, tiled=True)
-    cot_group = gathered(cotangent[0], "fsdp", fsdp_order[::-1]).reshape(fsdp * own, D)
+    cot_group = gathered(cotangent[0], FSDP_LAYOUT, outward).reshape(fsdp * own, D)
     half_up = weight_up.shape[0] // 2
     up_gate, up_value = [
         part.astype(heads_low)
@@ -830,11 +889,18 @@
             weight_up.astype(heads_low).reshape(2, half_up, D), up_shuffle_targets(fsdp), "fsdp", group
         )
     ]
+    packed, up_gate, up_value, given = lax.optimization_barrier((packed, up_gate, up_value, given))
     low_up = jnp.concatenate([up_gate, up_value])
+    token_seq = packed[:, :own].reshape(length, D)
+    ids = packed[:, own, :own].reshape(length).astype(jnp.float32)
+    head_rows = jnp.concatenate([picked(given, find_table[head, j]) for j in range(6)])
     low_down = weight_down.astype(heads_low)
 
     token_rows = token_seq.astype(jnp.float32)
-    normed_low = rms_scale(token_rows, gain_one).astype(heads_low)
+    scaled_rows = token_rows * lax.rsqrt(
+        jnp.mean(token_rows * token_rows, axis=-1, keepdims=True) + RMS_EPS
+    )
+    normed_low = (scaled_rows * gain_one).astype(heads_low)
     projected = contract_last(normed_low, head_rows).astype(heads_low)
     conv_in = projected[:, : 2 * DKH + DVH].astype(jnp.float32)
     gate_in = projected[:, 2 * DKH + DVH :].astype(jnp.float32)
@@ -861,14 +927,14 @@
         return rms_scale(recurrent_values, head_gain) * jax.nn.silu(gate_values)
 
     gated, gate_back = jax.vjp(gate_pair, recurrent, gate_in, gain_head)
-    gated_low = gated.astype(heads_low)
+    gated_low, cot_group = lax.optimization_barrier((gated.astype(heads_low), cot_group))
     gated_own = lax.all_to_all(gated_low.reshape(seq, own, DVH), "seq", 0, 0)
     gated_own = jnp.transpose(gated_own, (1, 0, 2)).reshape(own, H * DVH)
 
     own_rows = tokens[0].astype(jnp.float32)
     residual = own_rows + jnp.dot(gated_own, full_out, preferred_element_type=jnp.float32)
     normed_two, norm_two_back = jax.vjp(rms_scale, residual, gain_two)
-    two_group = gathered(normed_two.astype(heads_low), "fsdp", fsdp_order[::-1])
+    two_group = gathered(normed_two.astype(heads_low), FSDP_LAYOUT, outward)
     two_group = two_group.reshape(fsdp * own, D)
     gate_up = contract_last(two_group, low_up)
     units = half_up
@@ -879,41 +945,50 @@
     hidden, swiglu_back = jax.vjp(swiglu_own, gate_up)
     hidden_low = hidden.astype(heads_low)
     feed_parts = jnp.dot(hidden_low, low_down, preferred_element_type=jnp.float32)
-    feed_out = scattered_sum(feed_parts.reshape(fsdp, own, D), "fsdp", fsdp_order)
+    feed_out = scattered_sum(feed_parts.reshape(fsdp, own, D), FSDP_LAYOUT, inward)
     mixed = (residual + feed_out).astype(heads_low)[None]
 
     grad_hidden = contract_last(cot_group, low_down)
     (grad_gate_up,) = swiglu_back(grad_hidden)
     grad_gate_up_low = grad_gate_up.astype(heads_low)
     two_parts = jnp.dot(grad_gate_up_low, low_up, preferred_element_type=jnp.float32)
-    grad_normed_two = scattered_sum(two_parts.reshape(fsdp, own, D), "fsdp", fsdp_order)
-    grad_down_part = contract_first(hidden_low, cot_group)
-    grad_up_part = contract_first(grad_gate_up_low, two_group)
+    grad_normed_two = scattered_sum(two_parts.reshape(fsdp, own, D), FSDP_LAYOUT, inward)
     grad_resid_part, grad_gain_two = norm_two_back(grad_normed_two)
     grad_residual = cotangent[0].astype(jnp.float32) + grad_resid_part
     grad_attn_low = grad_residual.astype(heads_low)
-    attn_seq = lax.all_gather(grad_attn_low, "seq", axis=0, tiled=True)
-
-    piece = FF // (seq * fsdp)
-    ff_parts = jnp.concatenate(
+    grad_gated_own = contract_last(grad_attn_low, full_out).astype(heads_low)
+    grad_gated_own = jnp.transpose(grad_gated_own.reshape(own, seq, DVH), (1, 0, 2))
+    grad_gated = lax.all_to_all(grad_gated_own, "seq", 0, 0).reshape(length, DVH)
+
+    grad_gated, grad_gate_up_late = lax.optimization_barrier((grad_gated, grad_gate_up_low))
+    grad_down_part = contract_first(hidden_low, cot_group)
+    grad_up_part = contract_first(grad_gate_up_late, two_group)
+    gated_group = lax.all_to_all(gated_own.reshape(own, fsdp, -1), "fsdp", 1, 0)
+    attn_group = gathered(grad_attn_low, FSDP_LAYOUT, outward).reshape(fsdp * own, D)
+    grad_out_part = contract_first(gated_group.reshape(fsdp * own, -1), attn_group)
+    piece, out_piece = (FF // (seq * fsdp), H * DVH // (seq * fsdp))
+    late_parts = jnp.concatenate(
         [
-            grad_down_part.reshape(seq, 1, piece, D),
-            jnp.transpose(grad_up_part.reshape(2, seq, piece, D), (1, 0, 2, 3)),
+            grad_down_part.astype(heads_low).reshape(seq, piece, D),
+            grad_out_part.astype(heads_low).reshape(seq, out_piece, D),
+            grad_up_part[: half_up].astype(heads_low).reshape(seq, piece, D),
+            grad_up_part[half_up :].astype(heads_low).reshape(seq, piece, D),
         ],
         axis=1,
     )
-    ff_low = ff_parts.astype(heads_low)
-    ff_left = scattered_sum(ff_low[..., : D // 2], "seq", [0, 1, 2])
-    ff_right = scattered_sum(ff_low[..., D // 2 :], "seq", [1, 0, 2])
-    ff_own = jnp.concatenate([ff_left, ff_right], axis=-1).astype(heads_low)
+    late_left = scattered_sum(late_parts[..., : D // 2], SEQ_LAYOUT, (X_PAIR, Z_LINE))
+    late_right = scattered_sum(late_parts[..., D // 2 :], SEQ_LAYOUT, (Z_LINE, X_PAIR))
+    late_own = jnp.concatenate([late_left, late_right], axis=-1).astype(heads_low)
     both = ("seq", "fsdp")
-    (reduced_down,) = routed(ff_own[:1], down_targets(seq, fsdp), both, me)
-    reduced_up = jnp.concatenate(routed(ff_own[1:], up_targets(seq, fsdp), both, me))
-
-    out_rows = lax.dynamic_slice_in_dim(full_out, head * DVH, DVH, 0)
-    grad_gated = contract_last(attn_seq, out_rows)
-    grad_out_part = contract_first(gated_low, attn_seq)
-    reduced_out = scattered_sum(grad_out_part.reshape(fsdp, DVH // fsdp, D), "fsdp", fsdp_order)
+    (reduced_block,) = routed(
+        late_own[None, : piece + out_piece], block_targets(seq, fsdp), both, me
+    )
+    reduced_down, reduced_out = (reduced_block[:piece], reduced_block[piece:])
+    reduced_up = jnp.concatenate(
+        routed(late_own[piece + out_piece :].reshape(2, piece, D), up_targets(seq, fsdp), both, me)
+    )
+
+    grad_gated = grad_gated.astype(jnp.float32)
     grad_recurrent, grad_gate_in, grad_gain_head = gate_back(grad_gated)
     grad_out_chunks = grad_recurrent.reshape(local.shape)
     grad_entering = product("ntd,ntw->ndw", reach, grad_out_chunks)
@@ -930,21 +1005,24 @@
     normed_parts = jnp.dot(grad_projected_low, head_rows, preferred_element_type=jnp.float32)
     normed_parts = normed_parts + jnp.dot(grad_small, small_rows, precision=PRECISE)
     normed_low_parts = normed_parts.astype(heads_low).reshape(seq, own, D)
-    normed_left = scattered_sum(normed_low_parts[..., : D // 2], "seq", [0, 1, 2])
-    normed_right = scattered_sum(normed_low_parts[..., D // 2 :], "seq", [1, 0, 2])
+    normed_left = scattered_sum(normed_low_parts[..., : D // 2], SEQ_LAYOUT, (X_PAIR, Z_LINE))
+    normed_right = scattered_sum(normed_low_parts[..., D // 2 :], SEQ_LAYOUT, (Z_LINE, X_PAIR))
     grad_normed = jnp.concatenate([normed_left, normed_right], axis=-1)
     _, norm_back = jax.vjp(rms_scale, own_rows, gain_one)
-    grad_token_part, grad_gain_one = norm_back(grad_normed)
+    grad_token_part, _ = norm_back(grad_normed)
+    grad_gain_one = jnp.sum(normed_parts * scaled_rows, axis=0)
     grad_tokens = (grad_residual + grad_token_part)[None]
     in_rows = grad_in_part.shape[0] // fsdp
-    in_own = scattered_sum(grad_in_part.reshape(fsdp, in_rows, D), "fsdp", fsdp_order)
-    in_granules = in_own.astype(heads_low).reshape(in_rows // 64, 64, D)
+    in_own = scattered_sum(grad_in_part.reshape(fsdp, in_rows, D), FSDP_LAYOUT, inward)
+    in_own = in_own.astype(heads_low)
+    in_granules = in_own.reshape(in_rows // 64, 64, D)
     reduced_in = jnp.concatenate(routed(in_granules, in_targets(seq, fsdp), both, me))
 
     grad_projection = lax.dot_general(
         grad_small, normed_low.astype(jnp.float32), (((0,), (0,)), ((), ())), precision=PRECISE
     )
     width = 2 * DKH + DVH
+    square = lambda part: jnp.sum(jnp.square(part.astype(jnp.float32)))
     compact = jnp.concatenate(
         [
             grad_projection.reshape(-1),
@@ -954,13 +1032,14 @@
             grad_gain_head,
             grad_rate.reshape(1),
             grad_bias.reshape(1),
+            (square(in_own) + square(late_own)).reshape(1),
         ]
     )
     fill = -compact.shape[0] % 1024
     compact = jnp.concatenate([compact, jnp.zeros((fill,), jnp.float32)]).reshape(-1, 128)
-    compact = summed_everywhere(compact, [("fsdp", bit) for bit in range(fsdp_bits)])
-    compact = gathered(compact, "seq", list(range(seq_bits))).reshape(seq, -1)
-    cuts = [2 * D, KCONV * width, D, D, DVH, 1, 1]
+    compact = summed_over(compact, [("fsdp", (0, 1))])
+    compact = gathered(compact, SEQ_LAYOUT, (X_PAIR, Z_LINE)).reshape(seq, -1)
+    cuts = [2 * D, KCONV * width, D, D, DVH, 1, 1, 1]
     places = [sum(cuts[:i]) for i in range(len(cuts))]
     take = lambda i: compact[:, places[i] : places[i] + cuts[i]]
     taps_all = take(1).reshape(seq, KCONV, width)
@@ -980,25 +1059,21 @@
         ]
     )
 
-    squares = (
-        jnp.sum(reduced_in * reduced_in)
-        + jnp.sum(reduced_out * reduced_out)
-        + jnp.sum(reduced_up * reduced_up)
-        + jnp.sum(reduced_down * reduced_down)
-    )
-    all_bits = [("fsdp", bit) for bit in range(fsdp_bits)] + [("seq", bit) for bit in range(seq_bits)]
-    squares = summed_everywhere(jnp.full((8, 128), squares), all_bits)[0, 0]
+    squares = jnp.sum(take(7))
     grad_norm = jnp.sqrt(squares + jnp.sum(grad_vector * grad_vector))
     clipping = jnp.minimum(1.0, CLIP_NORM / (grad_norm + 1e-06))
     reduced = (reduced_in, reduced_out, reduced_up, reduced_down)
     momenta = (momentum_in, momentum_out, momentum_up, momentum_down)
     renewed = [MOMENTUM * m + (1.0 - MOMENTUM) * clipping * g for m, g in zip(momenta, reduced)]
-    blocks = jnp.stack([block for one in renewed for block in gram_panels(one)])
-    blocks = lax.psum(blocks.astype(heads_low), both)
-    updates = [
-        thin_update(one, gram_whole(blocks[10 * i : 10 * i + 10]), one.shape[0] * seq * fsdp)
-        for i, one in enumerate(renewed)
-    ]
+    height = max(one.shape[0] for one in renewed)
+    stacked = jnp.stack([jnp.pad(one, ((0, height - one.shape[0]), (0, 0))) for one in renewed])
+    blocks = blocks_everywhere(gram_blocks(stacked.astype(heads_low)))
+    rates = jnp.asarray(
+        [-LEARN_RATE * 0.2 * math.sqrt(max(one.shape[0] * seq * fsdp, D)) for one in renewed],
+        jnp.float32,
+    )
+    stacked = muon_rows(stacked, blocks, rates)
+    updates = [stacked[i, : one.shape[0]] for i, one in enumerate(renewed)]
     clipped = clipping * grad_vector
     first_next = ADAM_ONE * first_moment + (1.0 - ADAM_ONE) * clipped
     second_next = ADAM_TWO * second_moment + (1.0 - ADAM_TWO) * clipped * clipped

time: 801 us -> 687 us (0.86)
  waiting for transfers between devices: 308 us -> 194 us
  matrix products: 111 us -> 74.8 us
  Pallas kernels: 0 us -> 31 us
  local copies, waits for them, and re-layouts: 109 us -> 78.6 us
  starting transfers between devices: 85.4 us -> 114 us
  blocking collectives: 0 us -> 21 us
  other arithmetic: 115 us -> 102 us
    psum x1 -> x0, waiting for transfers between devices: 143 us -> none  [pair_shards(): blocks = lax.psum(blocks.astype(heads_low), both)]
    ppermute x34 -> x61, waiting for transfers between devices: 105 us -> 186 us  [exchanged(): lax.ppermute(value, axis, [(i, i ^ mask) for i in range(lax.axis_size(axi...]
    all_gather x1, waiting for transfers between devices: 48.7 us -> 0.02 us  [pair_shards(): packed = lax.all_gather(jnp.concatenate([tokens[0], row_ids]), 'seq')]
    reduce_sum x8 -> x3, other arithmetic: 44 us -> 3.84 us  [the longest x1 2.07 us: pair_shards(): jnp.mean(token_rows * token_rows, axis=-1, keepdims=True) + RMS_EPS]
    unnamed x403 -> x273, local copies, waits for them, and re-layouts: 50.4 us -> 16.5 us
    dot_general x48 -> x0, matrix products: 32 us -> none  [times(): jnp.dot(rows.astype(jnp.bfloat16), current, preferred_element_type=jnp.fl...]
    pallas_call x0 -> x2, Pallas kernels: none -> 31 us  [the longest x1 25.8 us: muon_rows(): pl.pallas_call(muon_kernel, grid_spec=pltpu.PrefetchScalarGridSpec(num_sc...]
    all_to_all x0 -> x1, blocking collectives: none -> 21 us  [pair_shards(): gated_own = lax.all_to_all(gated_low.reshape(seq, own, DVH), 'seq', 0, 0)]
  transfers between devices with their start and end apart: 48 -> 73, of which waited for: 28 -> 32; matrix products, arithmetic and copies ran while one was open for 17% -> 25% of each run, Pallas kernels for 0% -> 1%
where the time goes in v2:
time: 687 us; the launch traced here: 676 us
  waiting for transfers between devices  194 us (28%)
  starting transfers between devices  114 us (17%)
  other arithmetic  102 us (15%)
  local copies, waits for them, and re-layouts  78.6 us (11%)
  matrix products  74.8 us (11%)
  between operations  60.4 us (9%)
  Pallas kernels  31 us (5%)
  blocking collectives  21 us (3%)
    ppermute x61, waiting for transfers between devices, exchanged(): lax.ppermute(value, axis, [(i, i ^ mask) for i in range(lax.axis_size(axi...  186 us
    ppermute x61, starting transfers between devices, exchanged(): lax.ppermute(value, axis, [(i, i ^ mask) for i in range(lax.axis_size(axi...  72.8 us
    ppermute x8, starting transfers between devices, routed(): lax.ppermute(picked(granules, sent[me]), axes, [(src, chosen[src][0]) for...  32.1 us
    pallas_call x1, Pallas kernels, muon_rows(): pl.pallas_call(muon_kernel, grid_spec=pltpu.PrefetchScalarGridSpec(num_sc...  25.8 us
    all_to_all x1, blocking collectives, pair_shards(): gated_own = lax.all_to_all(gated_low.reshape(seq, own, DVH), 'seq', 0, 0)  21 us
    dot_general x17, matrix products, product(): jnp.einsum(spec, left, right, precision=MIX, preferred_element_type=jnp.f...  18.5 us
    unnamed x273, local copies, waits for them, and re-layouts  16.5 us
  transfers between devices with their start and end apart: 73, of which 32 were waited for; matrix products, arithmetic and copies ran while one was open for 25% of the time, Pallas kernels for 1%

profile of v2, /device:TPU:0, one launch (start us, length us, event | category | flops | bytes accessed | tf_op | source)
XLA Modules:
  0.0 675.8 jit_solution(2012665238606657587)
XLA Ops:
  14.7 3.1 convert_element_type.487
  21.6 12.4 %collective-permute-start.1 = (bf16[704,1024]{1,0:T(8,128)(2,1)}, bf16[704,1024]{1,0:T(8,128)(2,1)}, u32[]{:S(2)}, u32[]{:S(2)}) collective-permute-start(bf16[704,1024]{1,0:T(8,128)(2,1)} %get-tuple-element.110), channel_id=1, source_target_pairs={{0,0},{1,2},{2,1},{3,3},{4,4},{5,6},{6,5},{7,7},{8,8},{9,10},{10,9... | collective-permute-start | bytes 4325384 | tf_op jit(solution)/shard_map/ppermute | solution.py:552
  40.1 3.1 convert_element_type.509
  51.4 22.2 %collective-permute-done.4 = bf16[128,1024]{1,0:T(8,128)(2,1)S(1)} collective-permute-done((bf16[128,1024]{1,0:T(8,128)(2,1)S(1)}, bf16[128,1024]{1,0:T(8,128)(2,1)S(1)}, u32[]{:S(2)}, u32[]{:S(2)}) %collective-permute-start.4) | collective-permute-done | bytes 262176 | tf_op jit(solution)/shard_map/ppermute | solution.py:464
  102.9 3.9 fusion.3
  108.4 2.1 multiply_reduce_fusion.1
  110.5 3.1 copy.119
  119.7 3.1 fusion.7
  149.5 2.3 multiply_convert_fusion.3
  153.1 21.0 %all_to_all.25 = bf16[8,128,256]{1,2,0:T(8,128)(2,1)} all-to-all(bf16[8,128,256]{1,2,0:T(8,128)(2,1)S(1)} %copy.123), channel_id=1, replica_groups=mesh['seq'=8,'fsdp'=4] {'seq'}, dimensions={0} | all-to-all | bytes 1048576 | tf_op jit(solution)/shard_map/all_to_all | solution.py:931
  174.2 3.2 multiply_reduce_fusion.18
  177.9 6.7 collective-permute-done.6
  232.4 4.2 all-to-all-start.2
  242.0 9.6 %collective-permute-done.11 = bf16[128,1024]{1,0:T(8,128)(2,1)S(1)} collective-permute-done((bf16[128,1024]{1,0:T(8,128)(2,1)S(1)}, bf16[128,1024]{1,0:T(8,128)(2,1)S(1)}, u32[]{:S(2)}, u32[]{:S(2)}) %collective-permute-start.11) | collective-permute-done | bytes 262176 | tf_op jit(solution)/shard_map/ppermute | solution.py:464
  252.3 4.3 collective-permute-done.9
  260.1 2.0 copy.141
  262.2 3.7 collective-permute-done.25
  267.9 3.8 convolution_convert_fusion.1
  272.5 4.5 all-to-all-start.1
  277.1 3.6 convolution_convert_fusion.3
  284.6 7.4 %all-to-all-done.1 = bf16[8,128,256]{2,1,0:T(8,128)(2,1)S(1)} async-done(((bf16[8,128,256]{2,1,0:T(8,128)(2,1)}), bf16[8,128,256]{2,1,0:T(8,128)(2,1)S(1)}, u32[]{:S(2)}, u32[]{:S(2)}) %all-to-all-start.1) | async-done | bytes 524320 | tf_op jit(solution)/shard_map/all_to_all | solution.py:961
  292.0 2.7 multiply_reduce_fusion.8
  317.6 2.5 multiply_reduce_fusion.4
  322.5 3.8 fusion.33
  330.7 2.5 convolution_bitcast_fusion
  333.2 6.1 multiply_reduce_fusion
  343.8 2.2 collective-permute-start.16
  347.6 4.0 fusion.256
  356.9 5.9 pad_maximum_fusion
  368.6 2.9 collective-permute-start.31
  373.8 2.1 fusion.57
  378.7 6.0 collective-permute-done.33
  384.7 40.2 %collective-permute-done.32 = bf16[2,328,512]{2,1,0:T(8,128)(2,1)} collective-permute-done((bf16[2,328,512]{2,1,0:T(8,128)(2,1)}, bf16[2,328,512]{2,1,0:T(8,128)(2,1)}, u32[]{:S(2)}, u32[]{:S(2)}) %collective-permute-start.32) | collective-permute-done | bytes 671776 | tf_op jit(solution)/shard_map/ppermute | solution.py:464
  430.6 6.1 collective-permute-start.24
  437.2 3.2 collective-permute-start.30
  442.2 2.8 collective-permute-start.12
  445.1 5.0 collective-permute-done.30
  450.1 23.9 %collective-permute-done.29 = bf16[328,512]{1,0:T(8,128)(2,1)S(1)} collective-permute-done((bf16[328,512]{1,0:T(8,128)(2,1)S(1)}, bf16[328,512]{1,0:T(8,128)(2,1)S(1)}, u32[]{:S(2)}, u32[]{:S(2)}) %collective-permute-start.29) | collective-permute-done | bytes 335904 | tf_op jit(solution)/shard_map/ppermute | solution.py:464
  482.8 3.8 collective-permute-start.35
  486.6 2.4 collective-permute-start.42
  489.0 2.1 collective-permute-start.44
  491.8 6.0 collective-permute-done.42
  497.8 7.4 %collective-permute-start.36 = (bf16[88,1024]{1,0:T(8,128)(2,1)}, bf16[88,1024]{1,0:T(8,128)(2,1)S(1)}, u32[]{:S(2)}, u32[]{:S(2)}) collective-permute-start(bf16[88,1024]{1,0:T(8,128)(2,1)} %get-tuple-element.190), channel_id=1, source_target_pairs={{0,16},{1,20},{2,24},{3,28},{4,0},{5,4},{6,8},{7,12},{8,17},{9,21}... | collective-permute-start | bytes 540680 | tf_op jit(solution)/shard_map/ppermute | solution.py:552
  510.0 2.3 multiply_add_fusion.1
  519.7 5.2 gram_blocks.1
  524.8 3.3 fusion.243
  528.3 9.5 %collective-permute-start.57 = (bf16[2,2,4,288,128]{4,3,2,1,0:T(8,128)(2,1)S(1)}, bf16[2,2,4,288,128]{4,3,2,1,0:T(8,128)(2,1)S(1)}, u32[]{:S(2)}, u32[]{:S(2)}) collective-permute-start(bf16[2,2,4,288,128]{4,3,2,1,0:T(8,128)(2,1)S(1)} %dynamic-slice_bitcast_fusion.3), channel_id=1, source_target_pairs={{0,1},{1,0},{2,3},{3,2},{4,5},{5,4},{6,7},{7,6},{8,9},{9,8},{10,11... | collective-permute-start | bytes 3538952 | tf_op jit(solution)/shard_map/ppermute | solution.py:464
  541.7 2.4 collective-permute-done.19
  544.9 3.8 collective-permute-done.15
  548.7 5.3 collective-permute-done.14
  557.0 12.6 %collective-permute-done.58 = bf16[2,4,288,128]{3,2,1,0:T(8,128)(2,1)S(1)} collective-permute-done((bf16[2,4,288,128]{3,2,1,0:T(8,128)(2,1)S(1)}, bf16[2,4,288,128]{3,2,1,0:T(8,128)(2,1)S(1)}, u32[]{:S(2)}, u32[]{:S(2)}) %collective-permute-start.58) | collective-permute-done | bytes 589856 | tf_op jit(solution)/shard_map/ppermute | solution.py:464
  572.1 5.8 collective-permute-done.59
  579.6 2.9 collective-permute-start.60
  584.4 2.7 collective-permute-start.48
  588.5 4.1 collective-permute-start.63
  593.6 2.6 collective-permute-done.49
  597.1 3.6 collective-permute-start.53
  602.5 2.5 collective-permute-done.52
  610.1 4.9 collective-permute-done.54
  617.2 9.1 %collective-permute-done.67 = bf16[2,4,288,128]{3,2,1,0:T(8,128)(2,1)S(1)} collective-permute-done((bf16[2,4,288,128]{3,2,1,0:T(8,128)(2,1)S(1)}, bf16[2,4,288,128]{3,2,1,0:T(8,128)(2,1)S(1)}, u32[]{:S(2)}, u32[]{:S(2)}) %collective-permute-start.67) | collective-permute-done | bytes 589856 | tf_op jit(solution)/shard_map/ppermute | solution.py:464
  631.5 2.6 pad_maximum_fusion.1
  634.1 25.8 %muon_rows.1 = f32[4,192,1024]{2,1,0:T(8,128)} custom-call(f32[4]{0:T(128)} %constant.545.clone.rates_ref, f32[4,192,1024]{2,1,0:T(8,128)} %pad_maximum_fusion.2.rows_ref, bf16[144,128,128]{2,1,0:T(8,128)(2,1)} %bitcast.770), custom_call_target="tpu_custom_call" | custom-call | tf_op jit(solution)/shard_map/muon_rows/pallas_call | solution.py:746
  659.9 2.1 slice_bitcast_fusion
  663.6 2.0 slice_bitcast_fusion.1
  (648 shorter events, 227.6 us)
Async XLA Ops:
  7.2 101.2 %all-gather.6.cloned.1.call-start = ((), (), s32[]{:S(2)}) async-start(), calls=%async_computation.4 | async-start | bytes 2654208 | tf_op jit(solution)/shard_map/all_gather | solution.py:859
  9.6 164.5 %all-gather.4.cloned.1.call-start = ((), (), s32[]{:S(2)}) async-start(), calls=%async_computation.3 | async-start | bytes 5242880 | tf_op jit(solution)/shard_map/all_gather | solution.py:883
  21.1 81.8 %collective-permute-start = (bf16[704,1024]{1,0:T(8,128)(2,1)}, bf16[704,1024]{1,0:T(8,128)(2,1)S(1)}, u32[]{:S(2)}, u32[]{:S(2)}) collective-permute-start(bf16[704,1024]{1,0:T(8,128)(2,1)} %get-tuple-element.111), channel_id=1, source_target_pairs={{0,1},{1,3},{2,0},{3,2},{4,5},{5,7},{6,4},{7,6},{8,9},{9,11},{10,8... | collective-permute-start | bytes 4325384 | tf_op jit(solution)/shard_map/ppermute | solution.py:552
  21.6 81.3 %collective-permute-start.1 = (bf16[704,1024]{1,0:T(8,128)(2,1)}, bf16[704,1024]{1,0:T(8,128)(2,1)}, u32[]{:S(2)}, u32[]{:S(2)}) collective-permute-start(bf16[704,1024]{1,0:T(8,128)(2,1)} %get-tuple-element.110), channel_id=1, source_target_pairs={{0,0},{1,2},{2,1},{3,3},{4,4},{5,6},{6,5},{7,7},{8,8},{9,10},{10,9... | collective-permute-start | bytes 4325384 | tf_op jit(solution)/shard_map/ppermute | solution.py:552
  38.0 36.5 %collective-permute-start.2 = (bf16[2,128,1024]{2,1,0:T(8,128)(2,1)S(1)}, bf16[2,128,1024]{2,1,0:T(8,128)(2,1)}, u32[]{:S(2)}, u32[]{:S(2)}) collective-permute-start(bf16[2,128,1024]{2,1,0:T(8,128)(2,1)S(1)} %pad_maximum_fusion.21), channel_id=1, source_target_pairs={{0,2},{1,3},{2,0},{3,1},{4,6},{5,7},{6,4},{7,5},{8,10},{9,11},{10,... | collective-permute-start | bytes 1572872 | tf_op jit(solution)/shard_map/ppermute | solution.py:464
  38.1 35.5 %collective-permute-start.4 = (bf16[128,1024]{1,0:T(8,128)(2,1)S(1)}, bf16[128,1024]{1,0:T(8,128)(2,1)S(1)}, u32[]{:S(2)}, u32[]{:S(2)}) collective-permute-start(bf16[128,1024]{1,0:T(8,128)(2,1)S(1)} %bitcast.827), channel_id=1, source_target_pairs={{0,2},{1,3},{2,0},{3,1},{4,6},{5,7},{6,4},{7,5},{8,10},{9,11},{10,... | collective-permute-start | bytes 786440 | tf_op jit(solution)/shard_map/ppermute | solution.py:464
  74.5 26.1 %collective-permute-start.5 = (bf16[2,128,1024]{2,1,0:T(8,128)(2,1)}, bf16[2,128,1024]{2,1,0:T(8,128)(2,1)}, u32[]{:S(2)}, u32[]{:S(2)}) collective-permute-start(bf16[2,128,1024]{2,1,0:T(8,128)(2,1)} %pad_maximum_fusion.22), channel_id=1, source_target_pairs={{0,1},{1,0},{2,3},{3,2},{4,5},{5,4},{6,7},{7,6},{8,9},{9,8},{10,11... | collective-permute-start | bytes 1572872 | tf_op jit(solution)/shard_map/ppermute | solution.py:464
  76.8 30.0 %collective-permute-start.3 = (bf16[2,2,128,1024]{3,2,1,0:T(8,128)(2,1)}, bf16[2,2,128,1024]{3,2,1,0:T(8,128)(2,1)}, u32[]{:S(2)}, u32[]{:S(2)}) collective-permute-start(bf16[2,2,128,1024]{3,2,1,0:T(8,128)(2,1)} %pad_maximum_fusion.11), channel_id=1, source_target_pairs={{0,1},{1,0},{2,3},{3,2},{4,5},{5,4},{6,7},{7,6},{8,9},{9,8},{10,11... | collective-permute-start | bytes 3145736 | tf_op jit(solution)/shard_map/ppermute | solution.py:464
  177.5 7.0 %collective-permute-start.6 = (bf16[128,1024]{1,0:T(8,128)(2,1)S(1)}, bf16[128,1024]{1,0:T(8,128)(2,1)S(1)}, u32[]{:S(2)}, u32[]{:S(2)}) collective-permute-start(bf16[128,1024]{1,0:T(8,128)(2,1)S(1)} %multiply_convert_fusion.4), channel_id=1, source_target_pairs={{0,2},{1,3},{2,0},{3,1},{4,6},{5,7},{6,4},{7,5},{8,10},{9,11},{10,... | collective-permute-start | bytes 786440 | tf_op jit(solution)/shard_map/ppermute | solution.py:464
  197.7 38.9 %collective-permute-start.10 = (bf16[2,128,1024]{2,1,0:T(8,128)(2,1)}, bf16[2,128,1024]{2,1,0:T(8,128)(2,1)}, u32[]{:S(2)}, u32[]{:S(2)}) collective-permute-start(bf16[2,128,1024]{2,1,0:T(8,128)(2,1)} %fusion.54), channel_id=1, source_target_pairs={{0,1},{1,0},{2,3},{3,2},{4,5},{5,4},{6,7},{7,6},{8,9},{9,8},{10,11... | collective-permute-start | bytes 1572872 | tf_op jit(solution)/shard_map/ppermute | solution.py:464
  201.4 39.0 %collective-permute-start.8 = (bf16[2,128,1024]{2,1,0:T(8,128)(2,1)}, bf16[2,128,1024]{2,1,0:T(8,128)(2,1)}, u32[]{:S(2)}, u32[]{:S(2)}) collective-permute-start(bf16[2,128,1024]{2,1,0:T(8,128)(2,1)} %fusion.55), channel_id=1, source_target_pairs={{0,1},{1,0},{2,3},{3,2},{4,5},{5,4},{6,7},{7,6},{8,9},{9,8},{10,11... | collective-permute-start | bytes 1572872 | tf_op jit(solution)/shard_map/ppermute | solution.py:464
  232.4 27.7 %all-to-all-start.2 = ((bf16[1,128,4,512]{1,3,0,2:T(8,128)(2,1)}), bf16[1,128,4,512]{1,3,0,2:T(8,128)(2,1)}, u32[]{:S(2)}, u32[]{:S(2)}) async-start(bf16[1,128,4,512]{1,3,0,2:T(8,128)(2,1)} %bitcast.805), calls=%async_computation.2 | async-start | bytes 1048576 | tf_op jit(solution)/shard_map/all_to_all | solution.py:966
  238.4 13.2 %collective-permute-start.11 = (bf16[128,1024]{1,0:T(8,128)(2,1)S(1)}, bf16[128,1024]{1,0:T(8,128)(2,1)S(1)}, u32[]{:S(2)}, u32[]{:S(2)}) collective-permute-start(bf16[128,1024]{1,0:T(8,128)(2,1)S(1)} %fusion.112), channel_id=1, source_target_pairs={{0,2},{1,3},{2,0},{3,1},{4,6},{5,7},{6,4},{7,5},{8,10},{9,11},{10,... | collective-permute-start | bytes 786440 | tf_op jit(solution)/shard_map/ppermute | solution.py:464
  241.7 14.9 %collective-permute-start.9 = (bf16[128,1024]{1,0:T(8,128)(2,1)S(1)}, bf16[128,1024]{1,0:T(8,128)(2,1)S(1)}, u32[]{:S(2)}, u32[]{:S(2)}) collective-permute-start(bf16[128,1024]{1,0:T(8,128)(2,1)S(1)} %fusion.111), channel_id=1, source_target_pairs={{0,2},{1,3},{2,0},{3,1},{4,6},{5,7},{6,4},{7,5},{8,10},{9,11},{10,... | collective-permute-start | bytes 786440 | tf_op jit(solution)/shard_map/ppermute | solution.py:464
  257.8 8.1 %collective-permute-start.25 = (bf16[128,1024]{1,0:T(8,128)(2,1)}, bf16[128,1024]{1,0:T(8,128)(2,1)}, u32[]{:S(2)}, u32[]{:S(2)}) collective-permute-start(bf16[128,1024]{1,0:T(8,128)(2,1)} %get-tuple-element.87), channel_id=1, source_target_pairs={{0,2},{1,3},{2,0},{3,1},{4,6},{5,7},{6,4},{7,5},{8,10},{9,11},{10,... | collective-permute-start | bytes 786440 | tf_op jit(solution)/shard_map/ppermute | solution.py:464
  267.9 12.8 %collective-permute-start.26 = (bf16[2,128,1024]{2,1,0:T(8,128)(2,1)}, bf16[2,128,1024]{2,1,0:T(8,128)(2,1)}, u32[]{:S(2)}, u32[]{:S(2)}) collective-permute-start(bf16[2,128,1024]{2,1,0:T(8,128)(2,1)} %pad_maximum_fusion.24), channel_id=1, source_target_pairs={{0,1},{1,0},{2,3},{3,2},{4,5},{5,4},{6,7},{7,6},{8,9},{9,8},{10,11... | collective-permute-start | bytes 1572872 | tf_op jit(solution)/shard_map/ppermute | solution.py:464
  272.5 19.5 %all-to-all-start.1 = ((bf16[8,128,256]{2,1,0:T(8,128)(2,1)}), bf16[8,128,256]{2,1,0:T(8,128)(2,1)S(1)}, u32[]{:S(2)}, u32[]{:S(2)}) async-start(bf16[8,128,256]{2,1,0:T(8,128)(2,1)} %bitcast.814), calls=%async_computation.1 | async-start | bytes 1048576 | tf_op jit(solution)/shard_map/all_to_all | solution.py:961
  341.6 26.7 %collective-permute-start.18 = (bf16[2,128,512]{2,1,0:T(8,128)(2,1)}, bf16[2,128,512]{2,1,0:T(8,128)(2,1)}, u32[]{:S(2)}, u32[]{:S(2)}) collective-permute-start(bf16[2,128,512]{2,1,0:T(8,128)(2,1)} %get-tuple-element.152), channel_id=1, source_target_pairs={{0,24},{4,28},{8,16},{12,20},{16,8},{20,12},{24,0},{28,4},{1,25},{... | collective-permute-start | bytes 786440 | tf_op jit(solution)/shard_map/ppermute | solution.py:464
  342.8 25.9 %collective-permute-start.17 = (bf16[2,128,512]{2,1,0:T(8,128)(2,1)}, bf16[2,128,512]{2,1,0:T(8,128)(2,1)}, u32[]{:S(2)}, u32[]{:S(2)}) collective-permute-start(bf16[2,128,512]{2,1,0:T(8,128)(2,1)} %get-tuple-element.153), channel_id=1, source_target_pairs={{0,16},{4,20},{8,24},{12,28},{16,0},{20,4},{24,8},{28,12},{1,17},{... | collective-permute-start | bytes 786440 | tf_op jit(solution)/shard_map/ppermute | solution.py:464
  343.8 28.4 %collective-permute-start.16 = (bf16[2,128,512]{2,1,0:T(8,128)(2,1)S(1)}, bf16[2,128,512]{2,1,0:T(8,128)(2,1)}, u32[]{:S(2)}, u32[]{:S(2)}) collective-permute-start(bf16[2,128,512]{2,1,0:T(8,128)(2,1)S(1)} %get-tuple-element.151), channel_id=1, source_target_pairs={{0,8},{4,12},{8,0},{12,4},{16,24},{20,28},{24,16},{28,20},{1,9},{5... | collective-permute-start | bytes 786440 | tf_op jit(solution)/shard_map/ppermute | solution.py:464
  353.5 22.4 %collective-permute-start.20 = (bf16[2,192,1024]{2,1,0:T(8,128)(2,1)}, bf16[2,192,1024]{2,1,0:T(8,128)(2,1)}, u32[]{:S(2)}, u32[]{:S(2)}) collective-permute-start(bf16[2,192,1024]{2,1,0:T(8,128)(2,1)} %fusion.35), channel_id=1, source_target_pairs={{0,1},{1,0},{2,3},{3,2},{4,5},{5,4},{6,7},{7,6},{8,9},{9,8},{10,11... | collective-permute-start | bytes 2359304 | tf_op jit(solution)/shard_map/ppermute | solution.py:464
  364.5 20.2 %collective-permute-start.33 = (bf16[2,328,512]{2,1,0:T(8,128)(2,1)}, bf16[2,328,512]{2,1,0:T(8,128)(2,1)}, u32[]{:S(2)}, u32[]{:S(2)}) collective-permute-start(bf16[2,328,512]{2,1,0:T(8,128)(2,1)} %get-tuple-element.116), channel_id=1, source_target_pairs={{0,24},{4,28},{8,16},{12,20},{16,8},{20,12},{24,0},{28,4},{1,25},{... | collective-permute-start | bytes 2015240 | tf_op jit(solution)/shard_map/ppermute | solution.py:464
  368.3 56.6 %collective-permute-start.32 = (bf16[2,328,512]{2,1,0:T(8,128)(2,1)}, bf16[2,328,512]{2,1,0:T(8,128)(2,1)}, u32[]{:S(2)}, u32[]{:S(2)}) collective-permute-start(bf16[2,328,512]{2,1,0:T(8,128)(2,1)} %get-tuple-element.117), channel_id=1, source_target_pairs={{0,16},{4,20},{8,24},{12,28},{16,0},{20,4},{24,8},{28,12},{1,17},{... | collective-permute-start | bytes 2015240 | tf_op jit(solution)/shard_map/ppermute | solution.py:464
  368.6 56.3 %collective-permute-start.31 = (bf16[2,328,512]{2,1,0:T(8,128)(2,1)}, bf16[2,328,512]{2,1,0:T(8,128)(2,1)}, u32[]{:S(2)}, u32[]{:S(2)}) collective-permute-start(bf16[2,328,512]{2,1,0:T(8,128)(2,1)} %get-tuple-element.115), channel_id=1, source_target_pairs={{0,8},{4,12},{8,0},{12,4},{16,24},{20,28},{24,16},{28,20},{1,9},{5... | collective-permute-start | bytes 2015240 | tf_op jit(solution)/shard_map/ppermute | solution.py:464
  372.2 64.4 %collective-permute-start.27 = (bf16[4,328,512]{2,1,0:T(8,128)(2,1)}, bf16[4,328,512]{2,1,0:T(8,128)(2,1)S(1)}, u32[]{:S(2)}, u32[]{:S(2)}) collective-permute-start(bf16[4,328,512]{2,1,0:T(8,128)(2,1)} %dynamic-slice_bitcast_fusion.2), channel_id=1, source_target_pairs={{0,4},{4,0},{8,12},{12,8},{16,20},{20,16},{24,28},{28,24},{1,5},{5... | collective-permute-start | bytes 4030472 | tf_op jit(solution)/shard_map/ppermute | solution.py:464
  377.8 50.5 %collective-permute-start.21 = (bf16[192,1024]{1,0:T(8,128)(2,1)S(1)}, bf16[192,1024]{1,0:T(8,128)(2,1)S(1)}, u32[]{:S(2)}, u32[]{:S(2)}) collective-permute-start(bf16[192,1024]{1,0:T(8,128)(2,1)S(1)} %fusion.78), channel_id=1, source_target_pairs={{0,2},{1,3},{2,0},{3,1},{4,6},{5,7},{6,4},{7,5},{8,10},{9,11},{10,... | collective-permute-start | bytes 1179656 | tf_op jit(solution)/shard_map/ppermute | solution.py:464
  426.8 14.0 %collective-permute-start.34 = (bf16[328,512]{1,0:T(8,128)(2,1)S(1)}, bf16[328,512]{1,0:T(8,128)(2,1)S(1)}, u32[]{:S(2)}, u32[]{:S(2)}) collective-permute-start(bf16[328,512]{1,0:T(8,128)(2,1)S(1)} %fusion.91), channel_id=1, source_target_pairs={{0,4},{4,0},{8,12},{12,8},{16,20},{20,16},{24,28},{28,24},{1,5},{5... | collective-permute-start | bytes 1007624 | tf_op jit(solution)/shard_map/ppermute | solution.py:464
  429.2 12.8 %collective-permute-start.22 = (bf16[64,1024]{1,0:T(8,128)(2,1)S(1)}, bf16[64,1024]{1,0:T(8,128)(2,1)S(1)}, u32[]{:S(2)}, u32[]{:S(2)}) collective-permute-start(bf16[64,1024]{1,0:T(8,128)(2,1)S(1)} %get-tuple-element.186), channel_id=1, source_target_pairs={{0,0},{1,5},{2,11},{3,21},{4,1},{5,12},{6,22},{7,23},{8,6},{9,13},... | collective-permute-start | bytes 393224 | tf_op jit(solution)/shard_map/ppermute | solution.py:552
  429.9 12.3 %collective-permute-start.23 = (bf16[64,1024]{1,0:T(8,128)(2,1)S(1)}, bf16[64,1024]{1,0:T(8,128)(2,1)S(1)}, u32[]{:S(2)}, u32[]{:S(2)}) collective-permute-start(bf16[64,1024]{1,0:T(8,128)(2,1)S(1)} %get-tuple-element.185), channel_id=1, source_target_pairs={{0,0},{1,10},{2,11},{3,22},{4,6},{5,12},{6,13},{7,23},{8,1},{9,7},... | collective-permute-start | bytes 393224 | tf_op jit(solution)/shard_map/ppermute | solution.py:552
  430.6 14.4 %collective-permute-start.24 = (bf16[64,1024]{1,0:T(8,128)(2,1)S(1)}, bf16[64,1024]{1,0:T(8,128)(2,1)S(1)}, u32[]{:S(2)}, u32[]{:S(2)}) collective-permute-start(bf16[64,1024]{1,0:T(8,128)(2,1)S(1)} %get-tuple-element.184), channel_id=1, source_target_pairs={{0,5},{1,11},{2,21},{3,22},{4,0},{5,6},{6,12},{7,23},{8,1},{9,13},... | collective-permute-start | bytes 393224 | tf_op jit(solution)/shard_map/ppermute | solution.py:552
  437.2 12.9 %collective-permute-start.30 = (bf16[328,512]{1,0:T(8,128)(2,1)S(1)}, bf16[328,512]{1,0:T(8,128)(2,1)S(1)}, u32[]{:S(2)}, u32[]{:S(2)}) collective-permute-start(bf16[328,512]{1,0:T(8,128)(2,1)S(1)} %get-tuple-element.113), channel_id=1, source_target_pairs={{0,24},{4,28},{8,16},{12,20},{16,8},{20,12},{24,0},{28,4},{1,25},{... | collective-permute-start | bytes 1007624 | tf_op jit(solution)/shard_map/ppermute | solution.py:464
  440.8 33.2 %collective-permute-start.29 = (bf16[328,512]{1,0:T(8,128)(2,1)S(1)}, bf16[328,512]{1,0:T(8,128)(2,1)S(1)}, u32[]{:S(2)}, u32[]{:S(2)}) collective-permute-start(bf16[328,512]{1,0:T(8,128)(2,1)S(1)} %get-tuple-element.114), channel_id=1, source_target_pairs={{0,16},{4,20},{8,24},{12,28},{16,0},{20,4},{24,8},{28,12},{1,17},{... | collective-permute-start | bytes 1007624 | tf_op jit(solution)/shard_map/ppermute | solution.py:464
  442.0 32.1 %collective-permute-start.28 = (bf16[328,512]{1,0:T(8,128)(2,1)S(1)}, bf16[328,512]{1,0:T(8,128)(2,1)S(1)}, u32[]{:S(2)}, u32[]{:S(2)}) collective-permute-start(bf16[328,512]{1,0:T(8,128)(2,1)S(1)} %get-tuple-element.112), channel_id=1, source_target_pairs={{0,8},{4,12},{8,0},{12,4},{16,24},{20,28},{24,16},{28,20},{1,9},{5... | collective-permute-start | bytes 1007624 | tf_op jit(solution)/shard_map/ppermute | solution.py:464
  442.2 95.9 %collective-permute-start.12 = (bf16[4,128,512]{2,1,0:T(8,128)(2,1)}, bf16[4,128,512]{2,1,0:T(8,128)(2,1)}, u32[]{:S(2)}, u32[]{:S(2)}) collective-permute-start(bf16[4,128,512]{2,1,0:T(8,128)(2,1)} %dynamic-slice_bitcast_fusion.8), channel_id=1, source_target_pairs={{0,4},{4,0},{8,12},{12,8},{16,20},{20,16},{24,28},{28,24},{1,5},{5... | collective-permute-start | bytes 1572872 | tf_op jit(solution)/shard_map/ppermute | solution.py:464
  482.8 30.7 %collective-permute-start.35 = (bf16[152,1024]{1,0:T(8,128)(2,1)}, bf16[152,1024]{1,0:T(8,128)(2,1)}, u32[]{:S(2)}, u32[]{:S(2)}) collective-permute-start(bf16[152,1024]{1,0:T(8,128)(2,1)} %fusion.92), channel_id=1, source_target_pairs={{0,0},{1,8},{2,16},{3,24},{4,1},{5,9},{6,17},{7,25},{8,2},{9,10},{... | collective-permute-start | bytes 933896 | tf_op jit(solution)/shard_map/ppermute | solution.py:552
  486.6 11.1 %collective-permute-start.42 = (f32[2,56,128]{2,1,0:T(8,128)S(1)}, f32[2,56,128]{2,1,0:T(8,128)S(1)}, u32[]{:S(2)}, u32[]{:S(2)}) collective-permute-start(f32[2,56,128]{2,1,0:T(8,128)S(1)} %pad_maximum_fusion.28), channel_id=1, source_target_pairs={{0,24},{4,28},{8,16},{12,20},{16,8},{20,12},{24,0},{28,4},{1,25},{... | collective-permute-start | bytes 172040 | tf_op jit(solution)/shard_map/ppermute | solution.py:464
  489.0 17.2 %collective-permute-start.43 = (f32[2,56,128]{2,1,0:T(8,128)S(1)}, f32[2,56,128]{2,1,0:T(8,128)S(1)}, u32[]{:S(2)}, u32[]{:S(2)}) collective-permute-start(f32[2,56,128]{2,1,0:T(8,128)S(1)} %pad_maximum_fusion.28), channel_id=1, source_target_pairs={{0,16},{4,20},{8,24},{12,28},{16,0},{20,4},{24,8},{28,12},{1,17},{... | collective-permute-start | bytes 172040 | tf_op jit(solution)/shard_map/ppermute | solution.py:464
  489.0 17.9 %collective-permute-start.44 = (f32[2,56,128]{2,1,0:T(8,128)S(1)}, f32[2,56,128]{2,1,0:T(8,128)S(1)}, u32[]{:S(2)}, u32[]{:S(2)}) collective-permute-start(f32[2,56,128]{2,1,0:T(8,128)S(1)} %pad_maximum_fusion.28), channel_id=1, source_target_pairs={{0,8},{4,12},{8,0},{12,4},{16,24},{20,28},{24,16},{28,20},{1,9},{5... | collective-permute-start | bytes 172040 | tf_op jit(solution)/shard_map/ppermute | solution.py:464
  497.8 14.5 %collective-permute-start.36 = (bf16[88,1024]{1,0:T(8,128)(2,1)}, bf16[88,1024]{1,0:T(8,128)(2,1)S(1)}, u32[]{:S(2)}, u32[]{:S(2)}) collective-permute-start(bf16[88,1024]{1,0:T(8,128)(2,1)} %get-tuple-element.190), channel_id=1, source_target_pairs={{0,16},{1,20},{2,24},{3,28},{4,0},{5,4},{6,8},{7,12},{8,17},{9,21}... | collective-permute-start | bytes 540680 | tf_op jit(solution)/shard_map/ppermute | solution.py:552
  528.3 26.0 %collective-permute-start.57 = (bf16[2,2,4,288,128]{4,3,2,1,0:T(8,128)(2,1)S(1)}, bf16[2,2,4,288,128]{4,3,2,1,0:T(8,128)(2,1)S(1)}, u32[]{:S(2)}, u32[]{:S(2)}) collective-permute-start(bf16[2,2,4,288,128]{4,3,2,1,0:T(8,128)(2,1)S(1)} %dynamic-slice_bitcast_fusion.3), channel_id=1, source_target_pairs={{0,1},{1,0},{2,3},{3,2},{4,5},{5,4},{6,7},{7,6},{8,9},{9,8},{10,11... | collective-permute-start | bytes 3538952 | tf_op jit(solution)/shard_map/ppermute | solution.py:464
  537.8 6.3 collective-permute-start.19
  539.4 17.1 %collective-permute-start.45 = (bf16[2,2,4,288,128]{4,3,2,1,0:T(8,128)(2,1)S(1)}, bf16[2,2,4,288,128]{4,3,2,1,0:T(8,128)(2,1)S(1)}, u32[]{:S(2)}, u32[]{:S(2)}) collective-permute-start(bf16[2,2,4,288,128]{4,3,2,1,0:T(8,128)(2,1)S(1)} %dynamic-slice_bitcast_fusion.4), channel_id=1, source_target_pairs={{0,1},{1,0},{2,3},{3,2},{4,5},{5,4},{6,7},{7,6},{8,9},{9,8},{10,11... | collective-permute-start | bytes 3538952 | tf_op jit(solution)/shard_map/ppermute | solution.py:464
  540.4 8.3 %collective-permute-start.15 = (bf16[128,512]{1,0:T(8,128)(2,1)S(1)}, bf16[128,512]{1,0:T(8,128)(2,1)S(1)}, u32[]{:S(2)}, u32[]{:S(2)}) collective-permute-start(bf16[128,512]{1,0:T(8,128)(2,1)S(1)} %get-tuple-element.149), channel_id=1, source_target_pairs={{0,24},{4,28},{8,16},{12,20},{16,8},{20,12},{24,0},{28,4},{1,25},{... | collective-permute-start | bytes 393224 | tf_op jit(solution)/shard_map/ppermute | solution.py:464
  540.5 13.5 %collective-permute-start.14 = (bf16[128,512]{1,0:T(8,128)(2,1)S(1)}, bf16[128,512]{1,0:T(8,128)(2,1)S(1)}, u32[]{:S(2)}, u32[]{:S(2)}) collective-permute-start(bf16[128,512]{1,0:T(8,128)(2,1)S(1)} %get-tuple-element.150), channel_id=1, source_target_pairs={{0,16},{4,20},{8,24},{12,28},{16,0},{20,4},{24,8},{28,12},{1,17},{... | collective-permute-start | bytes 393224 | tf_op jit(solution)/shard_map/ppermute | solution.py:464
  544.1 9.9 %collective-permute-start.13 = (bf16[128,512]{1,0:T(8,128)(2,1)S(1)}, bf16[128,512]{1,0:T(8,128)(2,1)S(1)}, u32[]{:S(2)}, u32[]{:S(2)}) collective-permute-start(bf16[128,512]{1,0:T(8,128)(2,1)S(1)} %get-tuple-element.148), channel_id=1, source_target_pairs={{0,8},{4,12},{8,0},{12,4},{16,24},{20,28},{24,16},{28,20},{1,9},{5... | collective-permute-start | bytes 393224 | tf_op jit(solution)/shard_map/ppermute | solution.py:464
  554.7 15.0 %collective-permute-start.58 = (bf16[2,4,288,128]{3,2,1,0:T(8,128)(2,1)S(1)}, bf16[2,4,288,128]{3,2,1,0:T(8,128)(2,1)S(1)}, u32[]{:S(2)}, u32[]{:S(2)}) collective-permute-start(bf16[2,4,288,128]{3,2,1,0:T(8,128)(2,1)S(1)} %fusion.47), channel_id=1, source_target_pairs={{0,4},{4,0},{8,12},{12,8},{16,20},{20,16},{24,28},{28,24},{1,5},{5... | collective-permute-start | bytes 1769480 | tf_op jit(solution)/shard_map/ppermute | solution.py:464
  556.9 15.0 %collective-permute-start.46 = (bf16[2,4,288,128]{3,2,1,0:T(8,128)(2,1)S(1)}, bf16[2,4,288,128]{3,2,1,0:T(8,128)(2,1)S(1)}, u32[]{:S(2)}, u32[]{:S(2)}) collective-permute-start(bf16[2,4,288,128]{3,2,1,0:T(8,128)(2,1)S(1)} %fusion.46), channel_id=1, source_target_pairs={{0,2},{1,3},{2,0},{3,1},{4,6},{5,7},{6,4},{7,5},{8,10},{9,11},{10,... | collective-permute-start | bytes 1769480 | tf_op jit(solution)/shard_map/ppermute | solution.py:464
  569.8 8.1 %collective-permute-start.59 = (bf16[4,288,128]{2,1,0:T(8,128)(2,1)S(1)}, bf16[4,288,128]{2,1,0:T(8,128)(2,1)S(1)}, u32[]{:S(2)}, u32[]{:S(2)}) collective-permute-start(bf16[4,288,128]{2,1,0:T(8,128)(2,1)S(1)} %fusion.102), channel_id=1, source_target_pairs={{0,2},{1,3},{2,0},{3,1},{4,6},{5,7},{6,4},{7,5},{8,10},{9,11},{10,... | collective-permute-start | bytes 884744 | tf_op jit(solution)/shard_map/ppermute | solution.py:464
  572.0 10.4 %collective-permute-start.47 = (bf16[4,288,128]{2,1,0:T(8,128)(2,1)S(1)}, bf16[4,288,128]{2,1,0:T(8,128)(2,1)S(1)}, u32[]{:S(2)}, u32[]{:S(2)}) collective-permute-start(bf16[4,288,128]{2,1,0:T(8,128)(2,1)S(1)} %fusion.101), channel_id=1, source_target_pairs={{0,4},{4,0},{8,12},{12,8},{16,20},{20,16},{24,28},{28,24},{1,5},{5... | collective-permute-start | bytes 884744 | tf_op jit(solution)/shard_map/ppermute | solution.py:464
  578.0 6.4 collective-permute-start.62
  579.6 8.9 %collective-permute-start.61 = (bf16[288,128]{1,0:T(8,128)(2,1)S(1)}, bf16[288,128]{1,0:T(8,128)(2,1)S(1)}, u32[]{:S(2)}, u32[]{:S(2)}) collective-permute-start(bf16[288,128]{1,0:T(8,128)(2,1)S(1)} %get-tuple-element.169), channel_id=1, source_target_pairs={{0,16},{4,20},{8,24},{12,28},{16,0},{20,4},{24,8},{28,12},{1,17},{... | collective-permute-start | bytes 221192 | tf_op jit(solution)/shard_map/ppermute | solution.py:464
  579.6 8.9 %collective-permute-start.60 = (bf16[288,128]{1,0:T(8,128)(2,1)S(1)}, bf16[288,128]{1,0:T(8,128)(2,1)S(1)}, u32[]{:S(2)}, u32[]{:S(2)}) collective-permute-start(bf16[288,128]{1,0:T(8,128)(2,1)S(1)} %get-tuple-element.167), channel_id=1, source_target_pairs={{0,8},{4,12},{8,0},{12,4},{16,24},{20,28},{24,16},{28,20},{1,9},{5... | collective-permute-start | bytes 221192 | tf_op jit(solution)/shard_map/ppermute | solution.py:464
  582.6 10.0 %collective-permute-start.50 = (bf16[288,128]{1,0:T(8,128)(2,1)S(1)}, bf16[288,128]{1,0:T(8,128)(2,1)S(1)}, u32[]{:S(2)}, u32[]{:S(2)}) collective-permute-start(bf16[288,128]{1,0:T(8,128)(2,1)S(1)} %get-tuple-element.163), channel_id=1, source_target_pairs={{0,24},{4,28},{8,16},{12,20},{16,8},{20,12},{24,0},{28,4},{1,25},{... | collective-permute-start | bytes 221192 | tf_op jit(solution)/shard_map/ppermute | solution.py:464
  584.2 12.0 %collective-permute-start.49 = (bf16[288,128]{1,0:T(8,128)(2,1)S(1)}, bf16[288,128]{1,0:T(8,128)(2,1)S(1)}, u32[]{:S(2)}, u32[]{:S(2)}) collective-permute-start(bf16[288,128]{1,0:T(8,128)(2,1)S(1)} %get-tuple-element.164), channel_id=1, source_target_pairs={{0,16},{4,20},{8,24},{12,28},{16,0},{20,4},{24,8},{28,12},{1,17},{... | collective-permute-start | bytes 221192 | tf_op jit(solution)/shard_map/ppermute | solution.py:464
  584.4 11.8 %collective-permute-start.48 = (bf16[288,128]{1,0:T(8,128)(2,1)S(1)}, bf16[288,128]{1,0:T(8,128)(2,1)S(1)}, u32[]{:S(2)}, u32[]{:S(2)}) collective-permute-start(bf16[288,128]{1,0:T(8,128)(2,1)S(1)} %get-tuple-element.162), channel_id=1, source_target_pairs={{0,8},{4,12},{8,0},{12,4},{16,24},{20,28},{24,16},{28,20},{1,9},{5... | collective-permute-start | bytes 221192 | tf_op jit(solution)/shard_map/ppermute | solution.py:464
  588.5 8.6 %collective-permute-start.63 = (bf16[288,128]{1,0:T(8,128)(2,1)S(1)}, bf16[288,128]{1,0:T(8,128)(2,1)S(1)}, u32[]{:S(2)}, u32[]{:S(2)}) collective-permute-start(bf16[288,128]{1,0:T(8,128)(2,1)S(1)} %fusion.167), channel_id=1, source_target_pairs={{0,24},{4,28},{8,16},{12,20},{16,8},{20,12},{24,0},{28,4},{1,25},{... | collective-permute-start | bytes 221192 | tf_op jit(solution)/shard_map/ppermute | solution.py:464
  592.6 8.3 %collective-permute-start.64 = (bf16[288,128]{1,0:T(8,128)(2,1)S(1)}, bf16[288,128]{1,0:T(8,128)(2,1)S(1)}, u32[]{:S(2)}, u32[]{:S(2)}) collective-permute-start(bf16[288,128]{1,0:T(8,128)(2,1)S(1)} %fusion.167), channel_id=1, source_target_pairs={{0,16},{4,20},{8,24},{12,28},{16,0},{20,4},{24,8},{28,12},{1,17},{... | collective-permute-start | bytes 221192 | tf_op jit(solution)/shard_map/ppermute | solution.py:464
  592.6 8.3 %collective-permute-start.65 = (bf16[288,128]{1,0:T(8,128)(2,1)S(1)}, bf16[288,128]{1,0:T(8,128)(2,1)S(1)}, u32[]{:S(2)}, u32[]{:S(2)}) collective-permute-start(bf16[288,128]{1,0:T(8,128)(2,1)S(1)} %fusion.167), channel_id=1, source_target_pairs={{0,8},{4,12},{8,0},{12,4},{16,24},{20,28},{24,16},{28,20},{1,9},{5... | collective-permute-start | bytes 221192 | tf_op jit(solution)/shard_map/ppermute | solution.py:464
  597.1 7.9 %collective-permute-start.52 = (bf16[288,128]{1,0:T(8,128)(2,1)S(1)}, bf16[288,128]{1,0:T(8,128)(2,1)S(1)}, u32[]{:S(2)}, u32[]{:S(2)}) collective-permute-start(bf16[288,128]{1,0:T(8,128)(2,1)S(1)} %fusion.170), channel_id=1, source_target_pairs={{0,16},{4,20},{8,24},{12,28},{16,0},{20,4},{24,8},{28,12},{1,17},{... | collective-permute-start | bytes 221192 | tf_op jit(solution)/shard_map/ppermute | solution.py:464
  597.1 7.9 %collective-permute-start.53 = (bf16[288,128]{1,0:T(8,128)(2,1)S(1)}, bf16[288,128]{1,0:T(8,128)(2,1)S(1)}, u32[]{:S(2)}, u32[]{:S(2)}) collective-permute-start(bf16[288,128]{1,0:T(8,128)(2,1)S(1)} %fusion.170), channel_id=1, source_target_pairs={{0,8},{4,12},{8,0},{12,4},{16,24},{20,28},{24,16},{28,20},{1,9},{5... | collective-permute-start | bytes 221192 | tf_op jit(solution)/shard_map/ppermute | solution.py:464
  601.0 7.0 %collective-permute-start.66 = (bf16[4,288,128]{2,1,0:T(8,128)(2,1)S(1)}, bf16[4,288,128]{2,1,0:T(8,128)(2,1)S(1)}, u32[]{:S(2)}, u32[]{:S(2)}) collective-permute-start(bf16[4,288,128]{2,1,0:T(8,128)(2,1)S(1)} %pad_maximum_fusion.26), channel_id=1, source_target_pairs={{0,2},{1,3},{2,0},{3,1},{4,6},{5,7},{6,4},{7,5},{8,10},{9,11},{10,... | collective-permute-start | bytes 884744 | tf_op jit(solution)/shard_map/ppermute | solution.py:464
  605.1 9.9 %collective-permute-start.54 = (bf16[4,288,128]{2,1,0:T(8,128)(2,1)S(1)}, bf16[4,288,128]{2,1,0:T(8,128)(2,1)S(1)}, u32[]{:S(2)}, u32[]{:S(2)}) collective-permute-start(bf16[4,288,128]{2,1,0:T(8,128)(2,1)S(1)} %pad_maximum_fusion.25), channel_id=1, source_target_pairs={{0,4},{4,0},{8,12},{12,8},{16,20},{20,16},{24,28},{28,24},{1,5},{5... | collective-permute-start | bytes 884744 | tf_op jit(solution)/shard_map/ppermute | solution.py:464
  608.1 18.1 %collective-permute-start.67 = (bf16[2,4,288,128]{3,2,1,0:T(8,128)(2,1)S(1)}, bf16[2,4,288,128]{3,2,1,0:T(8,128)(2,1)S(1)}, u32[]{:S(2)}, u32[]{:S(2)}) collective-permute-start(bf16[2,4,288,128]{3,2,1,0:T(8,128)(2,1)S(1)} %pad_maximum_fusion.20), channel_id=1, source_target_pairs={{0,4},{4,0},{8,12},{12,8},{16,20},{20,16},{24,28},{28,24},{1,5},{5... | collective-permute-start | bytes 1769480 | tf_op jit(solution)/shard_map/ppermute | solution.py:464
  615.2 12.4 %collective-permute-start.55 = (bf16[2,4,288,128]{3,2,1,0:T(8,128)(2,1)S(1)}, bf16[2,4,288,128]{3,2,1,0:T(8,128)(2,1)S(1)}, u32[]{:S(2)}, u32[]{:S(2)}) collective-permute-start(bf16[2,4,288,128]{3,2,1,0:T(8,128)(2,1)S(1)} %pad_maximum_fusion.19), channel_id=1, source_target_pairs={{0,2},{1,3},{2,0},{3,1},{4,6},{5,7},{6,4},{7,5},{8,10},{9,11},{10,... | collective-permute-start | bytes 1769480 | tf_op jit(solution)/shard_map/ppermute | solution.py:464
  (134 other events, 870.5 us)
Sparse Core Ops, SparseCore 0:
  10.8 54.5 all-gather.5
  66.9 32.9 all-gather.3

commit v3 on v2

--- a/solution.py
+++ b/solution.py
@@ -1,4 +1,5 @@
 import math
+from functools import partial
 
 import jax
 import jax.numpy as jnp
@@ -474,12 +475,12 @@
     return lax.dynamic_index_in_dim(value, index, position, keepdims=False)
 
 
-def scattered_sum(parts, layout, order, wire=jnp.bfloat16):
+def scattered_sum(parts, layout, order, wire=jnp.bfloat16, lead=0):
     sizes = tuple(2 ** len(bits) for _, bits in layout)
-    held = parts.reshape(sizes + parts.shape[1:])
+    held = parts.reshape(parts.shape[:lead] + sizes + parts.shape[lead + 1 :])
     left = list(layout)
     for group in order:
-        position, place = (left.index(group), place_in(group))
+        position, place = (lead + left.index(group), place_in(group))
         total = picked(held, place, position).astype(jnp.float32)
         for offset in range(1, 2 ** len(group[1])):
             gone = picked(held, place ^ offset, position).astype(wire)
@@ -541,18 +542,27 @@
     return rounds
 
 
+def looked_up(entries, index):
+    found = jnp.uint32(0)
+    for bit in range(max(max(entries), 1).bit_length()):
+        word = sum(((entry >> bit) & 1) << i for i, entry in enumerate(entries))
+        one = lax.shift_right_logical(jnp.uint32(word), index.astype(jnp.uint32)) & jnp.uint32(1)
+        found = found | lax.shift_left(one, jnp.uint32(bit))
+    return found.astype(jnp.int32)
+
+
 def routed(granules, targets, axes, me):
     slots, count = (len(targets[0]), len(targets))
     pieces = []
     for chosen in matchings(targets, slots, count):
-        sent = jnp.asarray([chosen[src][1] for src in range(count)], jnp.int32)
+        sent = [chosen[src][1] for src in range(count)]
         landing = [0] * count
         for src, (dst, i) in chosen.items():
             landing[dst] = targets[src][i][1]
         piece = lax.ppermute(
-            picked(granules, sent[me]), axes, [(src, chosen[src][0]) for src in range(count)]
+            picked(granules, looked_up(sent, me)), axes, [(src, chosen[src][0]) for src in range(count)]
         )
-        pieces.append((piece, jnp.asarray(landing, jnp.int32)[me]))
+        pieces.append((piece, looked_up(landing, me)))
     return [
         sum(
             jnp.where(place == slot, piece.astype(jnp.float32), 0.0)
@@ -576,7 +586,7 @@
     cols = lax.broadcasted_iota(jnp.int32, (size, size), 1)
     exact = lambda a, b: jnp.einsum("nij,njk->nik", a, b, precision=PRECISE)
     eye = (rows == cols).astype(jnp.float32)[None]
-    base = -jnp.where((rows // 8 == cols // 8)[None], strict, 0.0)
+    base = -jnp.where(((rows ^ cols) < 8)[None], strict, 0.0)
     second = exact(base, base)
     fourth = exact(second, second)
     inverse = eye + base
@@ -584,7 +594,7 @@
     inverse = inverse + exact(inverse, fourth)
     width = 8
     while width < size:
-        joint = (rows // (2 * width) == cols // (2 * width)) & (rows // width != cols // width)
+        joint = ((rows ^ cols) < 2 * width) & ((rows ^ cols) >= width)
         inverse = inverse - exact(exact(inverse, jnp.where(joint[None], strict, 0.0)), inverse)
         width *= 2
     return inverse
@@ -683,90 +693,86 @@
 PACK = SIDE * (SIDE + 1) // 2
 
 
-def gram_kernel(rows_ref, blocks_ref):
-    count = 0
-    for i in range(SIDE):
-        left = rows_ref[0, :, i * BLOCK : (i + 1) * BLOCK]
-        panel = contract_first(left, rows_ref[0, :, i * BLOCK :])
-        for j in range(SIDE - i):
-            blocks_ref[count] = panel[:, j * BLOCK : (j + 1) * BLOCK].astype(jnp.bfloat16)
-            count += 1
-
-
-def gram_blocks(rows):
-    count, height, width = rows.shape
+def gram_kernel(clip_ref, *refs):
+    count, total = (0, (len(refs) - 1) // 3)
+    for one in range(total):
+        momentum, grad, renewed = (refs[2 * one], refs[2 * one + 1], refs[2 * total + one])
+        rows = MOMENTUM * momentum[...] + (1.0 - MOMENTUM) * clip_ref[0] * grad[...]
+        renewed[...] = rows
+        narrow = rows.astype(jnp.bfloat16)
+        for i in range(SIDE):
+            left = narrow[:, i * BLOCK : (i + 1) * BLOCK]
+            panel = contract_first(left, narrow[:, i * BLOCK :])
+            for j in range(SIDE - i):
+                refs[-1][count] = panel[:, j * BLOCK : (j + 1) * BLOCK].astype(jnp.bfloat16)
+                count += 1
+
+
+def gram_blocks(clipping, momenta, grads):
+    whole = pl.BlockSpec(memory_space=pltpu.VMEM)
     return pl.pallas_call(
         gram_kernel,
-        grid=(count,),
-        in_specs=[pl.BlockSpec((1, height, width), lambda m: (m, 0, 0))],
-        out_specs=pl.BlockSpec((PACK, BLOCK, BLOCK), lambda m: (m, 0, 0)),
-        out_shape=jax.ShapeDtypeStruct((count * PACK, BLOCK, BLOCK), jnp.bfloat16),
+        in_specs=[pl.BlockSpec(memory_space=pltpu.SMEM)] + [whole] * (2 * len(grads)),
+        out_specs=[whole] * (len(grads) + 1),
+        out_shape=[jax.ShapeDtypeStruct(grad.shape, jnp.float32) for grad in grads]
+        + [jax.ShapeDtypeStruct((len(grads) * PACK, BLOCK, BLOCK), jnp.bfloat16)],
         name="gram_blocks",
-    )(rows)
-
-
-def muon_kernel(rates_ref, rows_ref, blocks_ref, out_ref, gram_ref):
-    count = 0
-    trace = jnp.zeros((BLOCK, BLOCK), jnp.float32)
+    )(clipping.reshape(1), *[array for pair in zip(momenta, grads) for array in pair])
+
+
+def muon_kernel(rates, blocks_ref, *refs):
+    gram_ref = refs[-1]
     line = lax.broadcasted_iota(jnp.int32, (BLOCK, BLOCK), 0)
     column = lax.broadcasted_iota(jnp.int32, (BLOCK, BLOCK), 1)
-    for i in range(SIDE):
-        for j in range(i, SIDE):
-            block = blocks_ref[count]
-            gram_ref[i * BLOCK : (i + 1) * BLOCK, j * BLOCK : (j + 1) * BLOCK] = block
-            if i == j:
-                trace = trace + jnp.where(line == column, block.astype(jnp.float32), 0.0)
-            else:
-                turned = block.astype(jnp.float32).T.astype(jnp.bfloat16)
-                gram_ref[j * BLOCK : (j + 1) * BLOCK, i * BLOCK : (i + 1) * BLOCK] = turned
-            count += 1
-    total = jnp.sum(jnp.sum(trace, axis=1, keepdims=True), axis=0, keepdims=True)
-    inverse_norm = 1.0 / (jnp.sqrt(total) + 1e-07)
-    squared = inverse_norm * inverse_norm
-
-    def times(rows):
-        narrow = rows.astype(jnp.bfloat16)
-        return jnp.dot(narrow, gram_ref[...], preferred_element_type=jnp.float32) * squared
-
-    def through(rows):
-        once = times(rows)
-        return NS_A * rows + NS_B * once + NS_C * times(once)
-
-    def advanced(rows):
-        return through(through(times(rows)))
-
-    first = through(rows_ref[0] * inverse_norm)
-    once = advanced(first)
-    ortho = NS_A * first + NS_B * once + NS_C * advanced(once)
-    out_ref[0] = ortho * rates_ref[pl.program_id(0)]
+    count = 0
+    for one, rate in enumerate(rates):
+        rows_ref, out_ref = (refs[one], refs[len(rates) + one])
+        trace = jnp.zeros((BLOCK, BLOCK), jnp.float32)
+        for i in range(SIDE):
+            for j in range(i, SIDE):
+                block = blocks_ref[count]
+                gram_ref[i * BLOCK : (i + 1) * BLOCK, j * BLOCK : (j + 1) * BLOCK] = block
+                if i == j:
+                    trace = trace + jnp.where(line == column, block.astype(jnp.float32), 0.0)
+                else:
+                    turned = block.astype(jnp.float32).T.astype(jnp.bfloat16)
+                    gram_ref[j * BLOCK : (j + 1) * BLOCK, i * BLOCK : (i + 1) * BLOCK] = turned
+                count += 1
+        total = jnp.sum(jnp.sum(trace, axis=1, keepdims=True), axis=0, keepdims=True)
+        inverse_norm = 1.0 / (jnp.sqrt(total) + 1e-07)
+        squared = inverse_norm * inverse_norm
+
+        def times(rows):
+            narrow = rows.astype(jnp.bfloat16)
+            return jnp.dot(narrow, gram_ref[...], preferred_element_type=jnp.float32) * squared
+
+        def through(rows):
+            once = times(rows)
+            return NS_A * rows + NS_B * once + NS_C * times(once)
+
+        def advanced(rows):
+            return through(through(times(rows)))
+
+        first = through(rows_ref[...] * inverse_norm)
+        once = advanced(first)
+        out_ref[...] = rate * (NS_A * first + NS_B * once + NS_C * advanced(once))
 
 
 def muon_rows(rows, blocks, rates):
-    count, height, width = rows.shape
+    whole = pl.BlockSpec(memory_space=pltpu.VMEM)
     return pl.pallas_call(
-        muon_kernel,
-        grid_spec=pltpu.PrefetchScalarGridSpec(
-            num_scalar_prefetch=1,
-            grid=(count,),
-            in_specs=[
-                pl.BlockSpec((1, height, width), lambda m, _: (m, 0, 0)),
-                pl.BlockSpec((PACK, BLOCK, BLOCK), lambda m, _: (m, 0, 0)),
-            ],
-            out_specs=pl.BlockSpec((1, height, width), lambda m, _: (m, 0, 0)),
-            scratch_shapes=[pltpu.VMEM((D, D), jnp.bfloat16)],
-        ),
-        out_shape=jax.ShapeDtypeStruct(rows.shape, jnp.float32),
+        partial(muon_kernel, rates),
+        in_specs=[whole] * (1 + len(rows)),
+        out_specs=[whole] * len(rows),
+        out_shape=[jax.ShapeDtypeStruct(one.shape, jnp.float32) for one in rows],
+        scratch_shapes=[pltpu.VMEM((D, D), jnp.bfloat16)],
         name="muon_rows",
-    )(rates, rows, blocks)
-
-
-def blocks_everywhere(blocks):
-    whole = blocks.reshape(2, 32, -1, BLOCK)
-    halves = []
-    for half, order in ((0, (CORES, Y_PAIR, X_PAIR, Z_LINE)), (1, (CORES, X_PAIR, Y_PAIR, Z_LINE))):
-        own = scattered_sum(whole[half], order, order).astype(jnp.bfloat16)
-        halves.append(gathered(own, order, order[::-1]))
-    return jnp.stack(halves).reshape(blocks.shape)
+    )(blocks, *rows)
+
+
+def blocks_everywhere(blocks, order):
+    own = scattered_sum(blocks.reshape(32, -1, BLOCK), order, order).astype(jnp.bfloat16)
+    return gathered(own, order, order[::-1]).reshape(blocks.shape)
 
 
 def head_tables(fsdp):
@@ -859,10 +865,10 @@
     packed = lax.all_gather(jnp.concatenate([tokens[0], row_ids]), "seq")
 
     give, find = head_tables(fsdp)
-    give_table = jnp.asarray(give, jnp.int32)
-    find_table = jnp.asarray(find, jnp.int32)
     slices = [
-        lax.dynamic_slice_in_dim(weight_in, give_table[head, group, j] * DKH, DKH, 0)
+        lax.dynamic_slice_in_dim(
+            weight_in, looked_up([one[j] for row in give for one in row], me) * DKH, DKH, 0
+        )
         for j in range(2)
     ]
     given = gathered(jnp.stack(slices).astype(heads_low), FSDP_LAYOUT, outward)
@@ -878,22 +884,22 @@
         ],
         axis=1,
     )
-    rate, bias = (decay_log[head], decay_bias[head])
+    this = lax.broadcasted_iota(jnp.int32, (H,), 0) == head
+    rate, bias = [jnp.sum(jnp.where(this, one, 0.0)) for one in (decay_log, decay_bias)]
 
     full_out = lax.all_gather(weight_out.astype(heads_low), "fsdp", axis=0, tiled=True)
     cot_group = gathered(cotangent[0], FSDP_LAYOUT, outward).reshape(fsdp * own, D)
     half_up = weight_up.shape[0] // 2
+    up_halves, given = lax.optimization_barrier(
+        (weight_up.astype(heads_low).reshape(2, half_up, D), given)
+    )
     up_gate, up_value = [
         part.astype(heads_low)
-        for part in routed(
-            weight_up.astype(heads_low).reshape(2, half_up, D), up_shuffle_targets(fsdp), "fsdp", group
-        )
+        for part in routed(up_halves, up_shuffle_targets(fsdp), "fsdp", group)
     ]
-    packed, up_gate, up_value, given = lax.optimization_barrier((packed, up_gate, up_value, given))
-    low_up = jnp.concatenate([up_gate, up_value])
     token_seq = packed[:, :own].reshape(length, D)
     ids = packed[:, own, :own].reshape(length).astype(jnp.float32)
-    head_rows = jnp.concatenate([picked(given, find_table[head, j]) for j in range(6)])
+    head_rows = jnp.concatenate([picked(given, looked_up([row[j] for row in find], head)) for j in range(6)])
     low_down = weight_down.astype(heads_low)
 
     token_rows = token_seq.astype(jnp.float32)
@@ -927,7 +933,10 @@
         return rms_scale(recurrent_values, head_gain) * jax.nn.silu(gate_values)
 
     gated, gate_back = jax.vjp(gate_pair, recurrent, gate_in, gain_head)
-    gated_low, cot_group = lax.optimization_barrier((gated.astype(heads_low), cot_group))
+    gated_low, cot_group, up_gate, up_value = lax.optimization_barrier(
+        (gated.astype(heads_low), cot_group, up_gate, up_value)
+    )
+    low_up = jnp.concatenate([up_gate, up_value])
     gated_own = lax.all_to_all(gated_low.reshape(seq, own, DVH), "seq", 0, 0)
     gated_own = jnp.transpose(gated_own, (1, 0, 2)).reshape(own, H * DVH)
 
@@ -952,6 +961,15 @@
     (grad_gate_up,) = swiglu_back(grad_hidden)
     grad_gate_up_low = grad_gate_up.astype(heads_low)
     two_parts = jnp.dot(grad_gate_up_low, low_up, preferred_element_type=jnp.float32)
+
+    over_seq = lambda parts, lead=0: scattered_sum(
+        parts, SEQ_LAYOUT, (X_PAIR, Z_LINE), lead=lead
+    ).astype(heads_low)
+    piece = FF // (seq * fsdp)
+    grad_up_part = contract_first(grad_gate_up_low, two_group).astype(heads_low)
+    up_own = over_seq(grad_up_part.reshape(2, seq, piece, D), 1)
+    grad_down_part = contract_first(hidden_low, cot_group).astype(heads_low)
+    down_own = over_seq(grad_down_part.reshape(seq, piece, D))
     grad_normed_two = scattered_sum(two_parts.reshape(fsdp, own, D), FSDP_LAYOUT, inward)
     grad_resid_part, grad_gain_two = norm_two_back(grad_normed_two)
     grad_residual = cotangent[0].astype(jnp.float32) + grad_resid_part
@@ -960,33 +978,16 @@
     grad_gated_own = jnp.transpose(grad_gated_own.reshape(own, seq, DVH), (1, 0, 2))
     grad_gated = lax.all_to_all(grad_gated_own, "seq", 0, 0).reshape(length, DVH)
 
-    grad_gated, grad_gate_up_late = lax.optimization_barrier((grad_gated, grad_gate_up_low))
-    grad_down_part = contract_first(hidden_low, cot_group)
-    grad_up_part = contract_first(grad_gate_up_late, two_group)
     gated_group = lax.all_to_all(gated_own.reshape(own, fsdp, -1), "fsdp", 1, 0)
     attn_group = gathered(grad_attn_low, FSDP_LAYOUT, outward).reshape(fsdp * own, D)
     grad_out_part = contract_first(gated_group.reshape(fsdp * own, -1), attn_group)
-    piece, out_piece = (FF // (seq * fsdp), H * DVH // (seq * fsdp))
-    late_parts = jnp.concatenate(
-        [
-            grad_down_part.astype(heads_low).reshape(seq, piece, D),
-            grad_out_part.astype(heads_low).reshape(seq, out_piece, D),
-            grad_up_part[: half_up].astype(heads_low).reshape(seq, piece, D),
-            grad_up_part[half_up :].astype(heads_low).reshape(seq, piece, D),
-        ],
-        axis=1,
-    )
-    late_left = scattered_sum(late_parts[..., : D // 2], SEQ_LAYOUT, (X_PAIR, Z_LINE))
-    late_right = scattered_sum(late_parts[..., D // 2 :], SEQ_LAYOUT, (Z_LINE, X_PAIR))
-    late_own = jnp.concatenate([late_left, late_right], axis=-1).astype(heads_low)
+    out_own = over_seq(grad_out_part.astype(heads_low).reshape(seq, -1, D))
     both = ("seq", "fsdp")
     (reduced_block,) = routed(
-        late_own[None, : piece + out_piece], block_targets(seq, fsdp), both, me
+        jnp.concatenate([down_own, out_own])[None], block_targets(seq, fsdp), both, me
     )
     reduced_down, reduced_out = (reduced_block[:piece], reduced_block[piece:])
-    reduced_up = jnp.concatenate(
-        routed(late_own[piece + out_piece :].reshape(2, piece, D), up_targets(seq, fsdp), both, me)
-    )
+    reduced_up = jnp.concatenate(routed(up_own, up_targets(seq, fsdp), both, me))
 
     grad_gated = grad_gated.astype(jnp.float32)
     grad_recurrent, grad_gate_in, grad_gain_head = gate_back(grad_gated)
@@ -1006,7 +1007,7 @@
     normed_parts = normed_parts + jnp.dot(grad_small, small_rows, precision=PRECISE)
     normed_low_parts = normed_parts.astype(heads_low).reshape(seq, own, D)
     normed_left = scattered_sum(normed_low_parts[..., : D // 2], SEQ_LAYOUT, (X_PAIR, Z_LINE))
-    normed_right = scattered_sum(normed_low_parts[..., D // 2 :], SEQ_LAYOUT, (Z_LINE, X_PAIR))
+    normed_right = scattered_sum(normed_low_parts[..., D // 2 :], SEQ_LAYOUT, (X_PAIR, Z_LINE))
     grad_normed = jnp.concatenate([normed_left, normed_right], axis=-1)
     _, norm_back = jax.vjp(rms_scale, own_rows, gain_one)
     grad_token_part, _ = norm_back(grad_normed)
@@ -1032,7 +1033,7 @@
             grad_gain_head,
             grad_rate.reshape(1),
             grad_bias.reshape(1),
-            (square(in_own) + square(late_own)).reshape(1),
+            (square(in_own) + square(up_own) + square(down_own) + square(out_own)).reshape(1),
         ]
     )
     fill = -compact.shape[0] % 1024
@@ -1064,16 +1065,16 @@
     clipping = jnp.minimum(1.0, CLIP_NORM / (grad_norm + 1e-06))
     reduced = (reduced_in, reduced_out, reduced_up, reduced_down)
     momenta = (momentum_in, momentum_out, momentum_up, momentum_down)
-    renewed = [MOMENTUM * m + (1.0 - MOMENTUM) * clipping * g for m, g in zip(momenta, reduced)]
-    height = max(one.shape[0] for one in renewed)
-    stacked = jnp.stack([jnp.pad(one, ((0, height - one.shape[0]), (0, 0))) for one in renewed])
-    blocks = blocks_everywhere(gram_blocks(stacked.astype(heads_low)))
-    rates = jnp.asarray(
-        [-LEARN_RATE * 0.2 * math.sqrt(max(one.shape[0] * seq * fsdp, D)) for one in renewed],
-        jnp.float32,
-    )
-    stacked = muon_rows(stacked, blocks, rates)
-    updates = [stacked[i, : one.shape[0]] for i, one in enumerate(renewed)]
+    renewed, updates = ([], [])
+    for first, order in ((0, (CORES, Y_PAIR, X_PAIR, Z_LINE)), (2, (CORES, X_PAIR, Y_PAIR, Z_LINE))):
+        *rows, blocks = gram_blocks(
+            clipping, momenta[first : first + 2], reduced[first : first + 2]
+        )
+        rates = [
+            -LEARN_RATE * 0.2 * math.sqrt(max(one.shape[0] * seq * fsdp, D)) for one in rows
+        ]
+        renewed += rows
+        updates += muon_rows(rows, blocks_everywhere(blocks, order), rates)
     clipped = clipping * grad_vector
     first_next = ADAM_ONE * first_moment + (1.0 - ADAM_ONE) * clipped
     second_next = ADAM_TWO * second_moment + (1.0 - ADAM_TWO) * clipped * clipped

time: 687 us -> 533 us (0.78)
  waiting for transfers between devices: 194 us -> 138 us
  between operations: 60.4 us -> 23.3 us
  local copies, waits for them, and re-layouts: 78.6 us -> 45.6 us
  other arithmetic: 102 us -> 89 us
  blocking collectives: 21 us -> 13.4 us
    ppermute x61 -> x65, waiting for transfers between devices: 186 us -> 101 us  [exchanged(): lax.ppermute(value, axis, [(i, i ^ mask) for i in range(lax.axis_size(axi...]
    ppermute x8, waiting for transfers between devices: 0.02 us -> 29.8 us  [routed(): lax.ppermute(picked(granules, looked_up(sent, me)), axes, [(src, chosen[s...]
    dynamic_slice x18 -> x0, local copies, waits for them, and re-layouts: 21.7 us -> none  [the longest x7 8.71 us: routed(): sent[me]]
    ppermute x8, starting transfers between devices: 32.1 us -> 15.2 us  [routed(): lax.ppermute(picked(granules, looked_up(sent, me)), axes, [(src, chosen[s...]
    ppermute x61 -> x65, starting transfers between devices: 72.8 us -> 87.7 us  [exchanged(): lax.ppermute(value, axis, [(i, i ^ mask) for i in range(lax.axis_size(axi...]
    all_to_all x1, blocking collectives: 21 us -> 13.4 us  [pair_shards(): gated_own = lax.all_to_all(gated_low.reshape(seq, own, DVH), 'seq', 0, 0)]
    squeeze x4 -> x0, local copies, waits for them, and re-layouts: 7.54 us -> none  [pair_shards(): updates = [stacked[i, :one.shape[0]] for i, one in enumerate(renewed)]]
    all_to_all x1, waiting for transfers between devices: 7.43 us -> 0.01 us  [pair_shards(): lax.all_to_all(grad_gated_own, 'seq', 0, 0).reshape(length, DVH)]
  transfers between devices with their start and end apart: 73 -> 77, of which waited for: 32 -> 26; matrix products, arithmetic and copies ran while one was open for 25% -> 34% of each run, Pallas kernels for 1% -> 4%
where the time goes in v3:
time: 533 us; the launch traced here: 525 us
  waiting for transfers between devices  138 us (26%)
  starting transfers between devices  111 us (21%)
  other arithmetic  89 us (17%)
  matrix products  71.1 us (13%)
  local copies, waits for them, and re-layouts  45.6 us (9%)
  Pallas kernels  33 us (6%)
  between operations  23.3 us (4%)
  blocking collectives  13.4 us (3%)
    ppermute x65, waiting for transfers between devices, exchanged(): lax.ppermute(value, axis, [(i, i ^ mask) for i in range(lax.axis_size(axi...  101 us
    ppermute x65, starting transfers between devices, exchanged(): lax.ppermute(value, axis, [(i, i ^ mask) for i in range(lax.axis_size(axi...  87.7 us
    ppermute x8, waiting for transfers between devices, routed(): lax.ppermute(picked(granules, looked_up(sent, me)), axes, [(src, chosen[s...  29.8 us
    pallas_call x2, Pallas kernels, muon_rows(): pl.pallas_call(partial(muon_kernel, rates), in_specs=[whole] * (1 + len(r...  25.2 us
    dot_general x17, matrix products, product(): jnp.einsum(spec, left, right, precision=MIX, preferred_element_type=jnp.f...  18.1 us
    ppermute x8, starting transfers between devices, routed(): lax.ppermute(picked(granules, looked_up(sent, me)), axes, [(src, chosen[s...  15.2 us
    another operation x37, other arithmetic, gathered(): held = jnp.stack(rows, axis=spot)  15.2 us
    all_to_all x1, blocking collectives, pair_shards(): gated_own = lax.all_to_all(gated_low.reshape(seq, own, DVH), 'seq', 0, 0)  13.4 us
  transfers between devices with their start and end apart: 77, of which 26 were waited for; matrix products, arithmetic and copies ran while one was open for 34% of the time, Pallas kernels for 4%

profile of v3, /device:TPU:0, one launch (start us, length us, event | category | flops | bytes accessed | tf_op | source)
XLA Modules:
  0.0 524.8 jit_solution(17384664991801259283)
XLA Ops:
  11.2 3.1 collective-permute-start
  19.5 7.6 %collective-permute-done = bf16[2,128,1024]{2,1,0:T(8,128)(2,1)} collective-permute-done((bf16[2,128,1024]{2,1,0:T(8,128)(2,1)S(1)}, bf16[2,128,1024]{2,1,0:T(8,128)(2,1)}, u32[]{:S(2)}, u32[]{:S(2)}) %collective-permute-start) | collective-permute-done | bytes 524320 | tf_op jit(solution)/shard_map/ppermute | solution.py:465
  32.8 3.1 convert_element_type.683
  42.6 16.7 %collective-permute-done.4 = bf16[704,1024]{1,0:T(8,128)(2,1)S(1)} collective-permute-done((bf16[704,1024]{1,0:T(8,128)(2,1)S(1)}, bf16[704,1024]{1,0:T(8,128)(2,1)S(1)}, u32[]{:S(2)}, u32[]{:S(2)}) %collective-permute-start.4) | collective-permute-done | bytes 1441824 | tf_op jit(solution)/shard_map/ppermute | solution.py:562
  59.3 2.5 fusion.3
  61.8 3.5 all-gather.6.cloned.1.call-done
  65.3 2.1 multiply_reduce_fusion.1
  69.0 2.1 multiply_convert_fusion.1
  74.2 3.3 fusion.7
  103.4 2.3 multiply_convert_fusion.3
  107.0 13.4 %all_to_all.25 = bf16[8,128,256]{1,2,0:T(8,128)(2,1)} all-to-all(bf16[8,128,256]{1,2,0:T(8,128)(2,1)S(1)} %copy.115), channel_id=1, replica_groups=mesh['seq'=8,'fsdp'=4] {'seq'}, dimensions={0} | all-to-all | bytes 1048576 | tf_op jit(solution)/shard_map/all_to_all | solution.py:940
  120.5 3.2 multiply_reduce_fusion.18
  125.0 15.7 %collective-permute-start.6 = (bf16[128,1024]{1,0:T(8,128)(2,1)}, bf16[128,1024]{1,0:T(8,128)(2,1)}, u32[]{:S(2)}, u32[]{:S(2)}) collective-permute-start(bf16[128,1024]{1,0:T(8,128)(2,1)} %multiply_convert_fusion.4), channel_id=1, source_target_pairs={{0,2},{1,3},{2,0},{3,1},{4,6},{5,7},{6,4},{7,5},{8,10},{9,11},{10,... | collective-permute-start | bytes 786440 | tf_op jit(solution)/shard_map/ppermute | solution.py:465
  140.7 6.3 %collective-permute-done.6 = bf16[128,1024]{1,0:T(8,128)(2,1)} collective-permute-done((bf16[128,1024]{1,0:T(8,128)(2,1)}, bf16[128,1024]{1,0:T(8,128)(2,1)}, u32[]{:S(2)}, u32[]{:S(2)}) %collective-permute-start.6) | collective-permute-done | bytes 262176 | tf_op jit(solution)/shard_map/ppermute | solution.py:465
  150.9 4.4 all-to-all-start.2
  155.3 2.8 constant_dynamic-update-slice_fusion
  159.9 4.2 all-to-all-done.2
  164.1 2.1 copy.135
  186.6 10.0 %collective-permute-done.25 = bf16[4,88,1024]{2,1,0:T(8,128)(2,1)S(1)} collective-permute-done((bf16[4,88,1024]{2,1,0:T(8,128)(2,1)S(1)}, bf16[4,88,1024]{2,1,0:T(8,128)(2,1)S(1)}, u32[]{:S(2)}, u32[]{:S(2)}) %collective-permute-start.25) | collective-permute-done | bytes 720928 | tf_op jit(solution)/shard_map/ppermute | solution.py:465
  200.3 1.9 collective-permute-start.26
  203.0 2.2 fusion.263
  205.6 2.5 convolution_convert_fusion.1
  209.0 4.0 all-to-all-start.1
  214.3 4.8 collective-permute-done.27
  219.1 2.6 multiply_reduce_fusion.21
  221.7 9.7 %collective-permute-done.36 = bf16[2,4,88,1024]{3,2,0,1:T(8,128)(2,1)} collective-permute-done((bf16[2,4,88,1024]{3,2,0,1:T(8,128)(2,1)}, bf16[2,4,88,1024]{3,2,0,1:T(8,128)(2,1)}, u32[]{:S(2)}, u32[]{:S(2)}) %collective-permute-start.36) | collective-permute-done | bytes 1441824 | tf_op jit(solution)/shard_map/ppermute | solution.py:465
  231.5 1.9 convert_add_fusion
  243.4 2.8 multiply_reduce_fusion.7
  246.2 2.1 add_add_fusion
  249.7 1.9 fusion.167
  268.9 2.5 multiply_reduce_fusion.4
  273.8 3.8 fusion.31
  281.1 2.5 convolution_bitcast_fusion
  283.7 6.2 %multiply_reduce_fusion = (f32[1024]{0:T(1024)S(1)}, bf16[1024,1024]{1,0:T(8,128)(2,1)S(1)}) fusion(f32[1024]{0:T(1024)S(1)} %copy-done.68, bf16[8,144,1024]{2,1,0:T(8,128)(2,1)S(1)} %bitcast.756, f32[1024,1024]{1,0:T(8,128)} %fusion.31, f32[1,1024]{1,0:T(1,128)S(1)} %copy-done.66, f32[1,1024]{1,0:T(1,128)S(1)} %copy-done.64, ...), kind=kOutput, calls=%fused_computation.1 | convolution fusion | flops 31460352 | bytes 8413184 | tf_op jit(solution)/shard_map/dot_general | solution.py:1007
  295.6 5.5 %fusion.274 = f32[2,2,192,1024]{3,2,1,0:T(8,128)} fusion(bf16[2,2,192,1024]{3,2,1,0:T(8,128)(2,1)} %bitcast.797, bf16[1024,1024,1,1]{1,0,3,2:T(8,128)(2,1)} %bitcast.794), kind=kOutput, calls=%fused_computation.649 | convolution fusion | flops 1610612736 | bytes 6815744 | tf_op jit(solution)/shard_map/dot_general | solution.py:108
  302.5 2.3 multiply_reduce_fusion.10
  309.2 13.0 %collective-permute-done.40 = bf16[88,1024]{1,0:T(8,128)(2,1)S(1)} collective-permute-done((bf16[88,1024]{1,0:T(8,128)(2,1)}, bf16[88,1024]{1,0:T(8,128)(2,1)S(1)}, u32[]{:S(2)}, u32[]{:S(2)}) %collective-permute-start.40) | collective-permute-done | bytes 180256 | tf_op jit(solution)/shard_map/ppermute | solution.py:562
  327.1 3.0 collective-permute-start.32
  334.2 8.3 %collective-permute-done.33 = bf16[64,1024]{1,0:T(8,128)(2,1)S(1)} collective-permute-done((bf16[64,1024]{1,0:T(8,128)(2,1)S(1)}, bf16[64,1024]{1,0:T(8,128)(2,1)S(1)}, u32[]{:S(2)}, u32[]{:S(2)}) %collective-permute-start.33) | collective-permute-done | bytes 131104 | tf_op jit(solution)/shard_map/ppermute | solution.py:465
  343.9 3.8 collective-permute-start.35
  353.7 2.2 convert_add_fusion.6
  363.0 2.4 collective-permute-start.47
  370.5 7.9 %collective-permute-start.24 = (bf16[64,1024]{1,0:T(8,128)(2,1)S(1)}, bf16[64,1024]{1,0:T(8,128)(2,1)S(1)}, u32[]{:S(2)}, u32[]{:S(2)}) collective-permute-start(bf16[64,1024]{1,0:T(8,128)(2,1)S(1)} %get-tuple-element.195), channel_id=1, source_target_pairs={{0,5},{1,11},{2,21},{3,22},{4,0},{5,6},{6,12},{7,23},{8,1},{9,13},... | collective-permute-start | bytes 393224 | tf_op jit(solution)/shard_map/ppermute | solution.py:562
  381.5 3.8 gram_blocks.3
  385.3 2.5 dynamic-slice_bitcast_fusion.2
  389.6 3.7 collective-permute-start.61
  394.3 3.9 gram_blocks.2
  401.7 2.6 collective-permute-start.13
  405.2 3.0 collective-permute-done.15
  408.2 5.8 %collective-permute-done.14 = bf16[128,512]{1,0:T(8,128)(2,1)S(1)} collective-permute-done((bf16[128,512]{1,0:T(8,128)(2,1)S(1)}, bf16[128,512]{1,0:T(8,128)(2,1)S(1)}, u32[]{:S(2)}, u32[]{:S(2)}) %collective-permute-start.14) | collective-permute-done | bytes 131104 | tf_op jit(solution)/shard_map/ppermute | solution.py:465
  416.8 2.4 collective-permute-start.50
  419.3 11.7 %collective-permute-done.62 = bf16[2,4,288,128]{3,2,1,0:T(8,128)(2,1)S(1)} collective-permute-done((bf16[2,4,288,128]{3,2,1,0:T(8,128)(2,1)S(1)}, bf16[2,4,288,128]{3,2,1,0:T(8,128)(2,1)S(1)}, u32[]{:S(2)}, u32[]{:S(2)}) %collective-permute-start.62) | collective-permute-done | bytes 589856 | tf_op jit(solution)/shard_map/ppermute | solution.py:465
  434.1 4.8 collective-permute-done.63
  440.6 2.9 collective-permute-start.64
  445.5 2.5 collective-permute-start.52
  451.2 3.3 collective-permute-start.69
  454.6 3.8 collective-permute-done.53
  458.9 4.0 collective-permute-start.57
  462.9 2.1 collective-permute-start.70
  466.6 3.1 collective-permute-done.70
  470.0 5.8 %collective-permute-done.58 = bf16[4,288,128]{2,1,0:T(8,128)(2,1)S(1)} collective-permute-done((bf16[4,288,128]{2,1,0:T(8,128)(2,1)S(1)}, bf16[4,288,128]{2,1,0:T(8,128)(2,1)S(1)}, u32[]{:S(2)}, u32[]{:S(2)}) %collective-permute-start.58) | collective-permute-done | bytes 294944 | tf_op jit(solution)/shard_map/ppermute | solution.py:465
  477.9 5.9 %collective-permute-done.71 = bf16[2,4,288,128]{3,2,1,0:T(8,128)(2,1)S(1)} collective-permute-done((bf16[2,4,288,128]{3,2,1,0:T(8,128)(2,1)S(1)}, bf16[2,4,288,128]{3,2,1,0:T(8,128)(2,1)S(1)}, u32[]{:S(2)}, u32[]{:S(2)}) %collective-permute-start.71) | collective-permute-done | bytes 589856 | tf_op jit(solution)/shard_map/ppermute | solution.py:465
  489.7 12.4 %muon_rows.3 = (f32[176,1024]{1,0:T(8,128)}, f32[88,1024]{1,0:T(8,128)}) custom-call(bf16[72,128,128]{2,1,0:T(8,128)(2,1)} %bitcast.767, f32[176,1024]{1,0:T(8,128)} %get-tuple-element.36.refs_0_, f32[88,1024]{1,0:T(8,128)} %get-tuple-element.37.refs_1_), custom_call_target="tpu_custom_call" | custom-call | tf_op jit(solution)/shard_map/muon_rows/pallas_call | solution.py:763
  503.8 12.8 %muon_rows.2 = (f32[192,1024]{1,0:T(8,128)}, f32[64,1024]{1,0:T(8,128)}) custom-call(bf16[72,128,128]{2,1,0:T(8,128)(2,1)} %bitcast.768, f32[192,1024]{1,0:T(8,128)} %get-tuple-element.34.refs_0_, f32[64,1024]{1,0:T(8,128)} %get-tuple-element.35.refs_1_), custom_call_target="tpu_custom_call" | custom-call | tf_op jit(solution)/shard_map/muon_rows/pallas_call | solution.py:763
  (586 shorter events, 190.6 us)
Async XLA Ops:
  7.2 58.1 %all-gather.6.cloned.1.call-start = ((), (), s32[]{:S(2)}) async-start(), calls=%async_computation.4 | async-start | bytes 2654208 | tf_op jit(solution)/shard_map/all_gather | solution.py:865
  9.8 110.7 %all-gather.4.cloned.1.call-start = ((), (), s32[]{:S(2)}) async-start(), calls=%async_computation.3 | async-start | bytes 5242880 | tf_op jit(solution)/shard_map/all_gather | solution.py:890
  11.2 15.9 %collective-permute-start = (bf16[2,128,1024]{2,1,0:T(8,128)(2,1)S(1)}, bf16[2,128,1024]{2,1,0:T(8,128)(2,1)}, u32[]{:S(2)}, u32[]{:S(2)}) collective-permute-start(bf16[2,128,1024]{2,1,0:T(8,128)(2,1)S(1)} %pad_maximum_fusion.17), channel_id=1, source_target_pairs={{0,2},{1,3},{2,0},{3,1},{4,6},{5,7},{6,4},{7,5},{8,10},{9,11},{10,... | collective-permute-start | bytes 1572872 | tf_op jit(solution)/shard_map/ppermute | solution.py:465
  14.2 22.5 %collective-permute-start.2 = (bf16[128,1024]{1,0:T(8,128)(2,1)}, bf16[128,1024]{1,0:T(8,128)(2,1)}, u32[]{:S(2)}, u32[]{:S(2)}) collective-permute-start(bf16[128,1024]{1,0:T(8,128)(2,1)} %bitcast.59), channel_id=1, source_target_pairs={{0,2},{1,3},{2,0},{3,1},{4,6},{5,7},{6,4},{7,5},{8,10},{9,11},{10,... | collective-permute-start | bytes 786440 | tf_op jit(solution)/shard_map/ppermute | solution.py:465
  30.1 8.3 %collective-permute-start.1 = (bf16[2,2,128,1024]{3,2,1,0:T(8,128)(2,1)}, bf16[2,2,128,1024]{3,2,1,0:T(8,128)(2,1)}, u32[]{:S(2)}, u32[]{:S(2)}) collective-permute-start(bf16[2,2,128,1024]{3,2,1,0:T(8,128)(2,1)} %pad_maximum_fusion.8), channel_id=1, source_target_pairs={{0,1},{1,0},{2,3},{3,2},{4,5},{5,4},{6,7},{7,6},{8,9},{9,8},{10,11... | collective-permute-start | bytes 3145736 | tf_op jit(solution)/shard_map/ppermute | solution.py:465
  40.3 19.0 %collective-permute-start.4 = (bf16[704,1024]{1,0:T(8,128)(2,1)S(1)}, bf16[704,1024]{1,0:T(8,128)(2,1)S(1)}, u32[]{:S(2)}, u32[]{:S(2)}) collective-permute-start(bf16[704,1024]{1,0:T(8,128)(2,1)S(1)} %get-tuple-element.128), channel_id=1, source_target_pairs={{0,1},{1,3},{2,0},{3,2},{4,5},{5,7},{6,4},{7,6},{8,9},{9,11},{10,8... | collective-permute-start | bytes 4325384 | tf_op jit(solution)/shard_map/ppermute | solution.py:562
  40.3 19.0 %collective-permute-start.5 = (bf16[704,1024]{1,0:T(8,128)(2,1)S(1)}, bf16[704,1024]{1,0:T(8,128)(2,1)S(1)}, u32[]{:S(2)}, u32[]{:S(2)}) collective-permute-start(bf16[704,1024]{1,0:T(8,128)(2,1)S(1)} %get-tuple-element.127), channel_id=1, source_target_pairs={{0,0},{1,2},{2,1},{3,3},{4,4},{5,6},{6,5},{7,7},{8,8},{9,10},{10,9... | collective-permute-start | bytes 4325384 | tf_op jit(solution)/shard_map/ppermute | solution.py:562
  125.0 22.0 %collective-permute-start.6 = (bf16[128,1024]{1,0:T(8,128)(2,1)}, bf16[128,1024]{1,0:T(8,128)(2,1)}, u32[]{:S(2)}, u32[]{:S(2)}) collective-permute-start(bf16[128,1024]{1,0:T(8,128)(2,1)} %multiply_convert_fusion.4), channel_id=1, source_target_pairs={{0,2},{1,3},{2,0},{3,1},{4,6},{5,7},{6,4},{7,5},{8,10},{9,11},{10,... | collective-permute-start | bytes 786440 | tf_op jit(solution)/shard_map/ppermute | solution.py:465
  149.7 16.5 %collective-permute-start.7 = (bf16[2,128,1024]{2,1,0:T(8,128)(2,1)}, bf16[2,128,1024]{2,1,0:T(8,128)(2,1)}, u32[]{:S(2)}, u32[]{:S(2)}) collective-permute-start(bf16[2,128,1024]{2,1,0:T(8,128)(2,1)} %pad_maximum_fusion.19), channel_id=1, source_target_pairs={{0,1},{1,0},{2,3},{3,2},{4,5},{5,4},{6,7},{7,6},{8,9},{9,8},{10,11... | collective-permute-start | bytes 1572872 | tf_op jit(solution)/shard_map/ppermute | solution.py:465
  150.9 13.2 %all-to-all-start.2 = ((bf16[1,128,4,512]{1,3,0,2:T(8,128)(2,1)}), bf16[1,128,4,512]{1,3,0,2:T(8,128)(2,1)}, u32[]{:S(2)}, u32[]{:S(2)}) async-start(bf16[1,128,4,512]{1,3,0,2:T(8,128)(2,1)} %bitcast.781), calls=%async_computation.2 | async-start | bytes 1048576 | tf_op jit(solution)/shard_map/all_to_all | solution.py:981
  176.7 7.3 %collective-permute-start.10 = (bf16[2,128,1024]{2,1,0:T(8,128)(2,1)S(1)}, bf16[2,128,1024]{2,1,0:T(8,128)(2,1)S(1)}, u32[]{:S(2)}, u32[]{:S(2)}) collective-permute-start(bf16[2,128,1024]{2,1,0:T(8,128)(2,1)S(1)} %fusion.51), channel_id=1, source_target_pairs={{0,1},{1,0},{2,3},{3,2},{4,5},{5,4},{6,7},{7,6},{8,9},{9,8},{10,11... | collective-permute-start | bytes 1572872 | tf_op jit(solution)/shard_map/ppermute | solution.py:465
  176.8 7.9 %collective-permute-start.8 = (bf16[2,128,1024]{2,1,0:T(8,128)(2,1)S(1)}, bf16[2,128,1024]{2,1,0:T(8,128)(2,1)S(1)}, u32[]{:S(2)}, u32[]{:S(2)}) collective-permute-start(bf16[2,128,1024]{2,1,0:T(8,128)(2,1)S(1)} %fusion.52), channel_id=1, source_target_pairs={{0,1},{1,0},{2,3},{3,2},{4,5},{5,4},{6,7},{7,6},{8,9},{9,8},{10,11... | collective-permute-start | bytes 1572872 | tf_op jit(solution)/shard_map/ppermute | solution.py:465
  177.4 19.1 %collective-permute-start.25 = (bf16[4,88,1024]{2,1,0:T(8,128)(2,1)S(1)}, bf16[4,88,1024]{2,1,0:T(8,128)(2,1)S(1)}, u32[]{:S(2)}, u32[]{:S(2)}) collective-permute-start(bf16[4,88,1024]{2,1,0:T(8,128)(2,1)S(1)} %dynamic-slice_bitcast_fusion.4), channel_id=1, source_target_pairs={{0,4},{4,0},{8,12},{12,8},{16,20},{20,16},{24,28},{28,24},{1,5},{5... | collective-permute-start | bytes 2162696 | tf_op jit(solution)/shard_map/ppermute | solution.py:465
  183.4 48.1 %collective-permute-start.36 = (bf16[2,4,88,1024]{3,2,0,1:T(8,128)(2,1)}, bf16[2,4,88,1024]{3,2,0,1:T(8,128)(2,1)}, u32[]{:S(2)}, u32[]{:S(2)}) collective-permute-start(bf16[2,4,88,1024]{3,2,0,1:T(8,128)(2,1)} %bitcast.737), channel_id=1, source_target_pairs={{0,4},{4,0},{8,12},{12,8},{16,20},{20,16},{24,28},{28,24},{1,5},{5... | collective-permute-start | bytes 4325384 | tf_op jit(solution)/shard_map/ppermute | solution.py:465
  184.2 16.1 %collective-permute-start.11 = (bf16[128,1024]{1,0:T(8,128)(2,1)S(1)}, bf16[128,1024]{1,0:T(8,128)(2,1)S(1)}, u32[]{:S(2)}, u32[]{:S(2)}) collective-permute-start(bf16[128,1024]{1,0:T(8,128)(2,1)S(1)} %fusion.107), channel_id=1, source_target_pairs={{0,2},{1,3},{2,0},{3,1},{4,6},{5,7},{6,4},{7,5},{8,10},{9,11},{10,... | collective-permute-start | bytes 786440 | tf_op jit(solution)/shard_map/ppermute | solution.py:465
  184.9 18.1 %collective-permute-start.9 = (bf16[128,1024]{1,0:T(8,128)(2,1)S(1)}, bf16[128,1024]{1,0:T(8,128)(2,1)S(1)}, u32[]{:S(2)}, u32[]{:S(2)}) collective-permute-start(bf16[128,1024]{1,0:T(8,128)(2,1)S(1)} %fusion.106), channel_id=1, source_target_pairs={{0,2},{1,3},{2,0},{3,1},{4,6},{5,7},{6,4},{7,5},{8,10},{9,11},{10,... | collective-permute-start | bytes 786440 | tf_op jit(solution)/shard_map/ppermute | solution.py:465
  197.8 16.5 %collective-permute-start.28 = (bf16[88,1024]{1,0:T(8,128)(2,1)}, bf16[88,1024]{1,0:T(8,128)(2,1)}, u32[]{:S(2)}, u32[]{:S(2)}) collective-permute-start(bf16[88,1024]{1,0:T(8,128)(2,1)} %get-tuple-element.146), channel_id=1, source_target_pairs={{0,24},{4,28},{8,16},{12,20},{16,8},{20,12},{24,0},{28,4},{1,25},{... | collective-permute-start | bytes 540680 | tf_op jit(solution)/shard_map/ppermute | solution.py:465
  199.0 20.1 %collective-permute-start.27 = (bf16[88,1024]{1,0:T(8,128)(2,1)}, bf16[88,1024]{1,0:T(8,128)(2,1)}, u32[]{:S(2)}, u32[]{:S(2)}) collective-permute-start(bf16[88,1024]{1,0:T(8,128)(2,1)} %get-tuple-element.147), channel_id=1, source_target_pairs={{0,16},{4,20},{8,24},{12,28},{16,0},{20,4},{24,8},{28,12},{1,17},{... | collective-permute-start | bytes 540680 | tf_op jit(solution)/shard_map/ppermute | solution.py:465
  200.3 18.8 %collective-permute-start.26 = (bf16[88,1024]{1,0:T(8,128)(2,1)}, bf16[88,1024]{1,0:T(8,128)(2,1)}, u32[]{:S(2)}, u32[]{:S(2)}) collective-permute-start(bf16[88,1024]{1,0:T(8,128)(2,1)} %get-tuple-element.145), channel_id=1, source_target_pairs={{0,8},{4,12},{8,0},{12,4},{16,24},{20,28},{24,16},{28,20},{1,9},{5... | collective-permute-start | bytes 540680 | tf_op jit(solution)/shard_map/ppermute | solution.py:465
  205.2 7.8 %collective-permute-start.29 = (bf16[128,1024]{1,0:T(8,128)(2,1)}, bf16[128,1024]{1,0:T(8,128)(2,1)}, u32[]{:S(2)}, u32[]{:S(2)}) collective-permute-start(bf16[128,1024]{1,0:T(8,128)(2,1)} %get-tuple-element.103), channel_id=1, source_target_pairs={{0,2},{1,3},{2,0},{3,1},{4,6},{5,7},{6,4},{7,5},{8,10},{9,11},{10,... | collective-permute-start | bytes 786440 | tf_op jit(solution)/shard_map/ppermute | solution.py:465
  209.0 34.4 %all-to-all-start.1 = ((bf16[8,128,256]{2,1,0:T(8,128)(2,1)}), bf16[8,128,256]{2,1,0:T(8,128)(2,1)S(1)}, u32[]{:S(2)}, u32[]{:S(2)}) async-start(bf16[8,128,256]{2,1,0:T(8,128)(2,1)} %bitcast.795), calls=%async_computation.1 | async-start | bytes 1048576 | tf_op jit(solution)/shard_map/all_to_all | solution.py:979
  214.2 24.7 %collective-permute-start.30 = (bf16[2,128,1024]{2,1,0:T(8,128)(2,1)S(1)}, bf16[2,128,1024]{2,1,0:T(8,128)(2,1)S(1)}, u32[]{:S(2)}, u32[]{:S(2)}) collective-permute-start(bf16[2,128,1024]{2,1,0:T(8,128)(2,1)S(1)} %pad_maximum_fusion.20), channel_id=1, source_target_pairs={{0,1},{1,0},{2,3},{3,2},{4,5},{5,4},{6,7},{7,6},{8,9},{9,8},{10,11... | collective-permute-start | bytes 1572872 | tf_op jit(solution)/shard_map/ppermute | solution.py:465
  234.6 66.5 %collective-permute-start.39 = (bf16[2,88,1024]{2,1,0:T(8,128)(2,1)}, bf16[2,88,1024]{2,1,0:T(8,128)(2,1)}, u32[]{:S(2)}, u32[]{:S(2)}) collective-permute-start(bf16[2,88,1024]{2,1,0:T(8,128)(2,1)} %get-tuple-element.120), channel_id=1, source_target_pairs={{0,24},{4,28},{8,16},{12,20},{16,8},{20,12},{24,0},{28,4},{1,25},{... | collective-permute-start | bytes 1081352 | tf_op jit(solution)/shard_map/ppermute | solution.py:465
  235.8 66.7 %collective-permute-start.38 = (bf16[2,88,1024]{2,1,0:T(8,128)(2,1)}, bf16[2,88,1024]{2,1,0:T(8,128)(2,1)}, u32[]{:S(2)}, u32[]{:S(2)}) collective-permute-start(bf16[2,88,1024]{2,1,0:T(8,128)(2,1)} %get-tuple-element.121), channel_id=1, source_target_pairs={{0,16},{4,20},{8,24},{12,28},{16,0},{20,4},{24,8},{28,12},{1,17},{... | collective-permute-start | bytes 1081352 | tf_op jit(solution)/shard_map/ppermute | solution.py:465
  237.1 65.4 %collective-permute-start.37 = (bf16[2,88,1024]{2,1,0:T(8,128)(2,1)}, bf16[2,88,1024]{2,1,0:T(8,128)(2,1)}, u32[]{:S(2)}, u32[]{:S(2)}) collective-permute-start(bf16[2,88,1024]{2,1,0:T(8,128)(2,1)} %get-tuple-element.119), channel_id=1, source_target_pairs={{0,8},{4,12},{8,0},{12,4},{16,24},{20,28},{24,16},{28,20},{1,9},{5... | collective-permute-start | bytes 1081352 | tf_op jit(solution)/shard_map/ppermute | solution.py:465
  242.0 82.2 %collective-permute-start.31 = (bf16[4,64,1024]{2,1,0:T(8,128)(2,1)}, bf16[4,64,1024]{2,1,0:T(8,128)(2,1)}, u32[]{:S(2)}, u32[]{:S(2)}) collective-permute-start(bf16[4,64,1024]{2,1,0:T(8,128)(2,1)} %dynamic-slice_bitcast_fusion.5), channel_id=1, source_target_pairs={{0,4},{4,0},{8,12},{12,8},{16,20},{20,16},{24,28},{28,24},{1,5},{5... | collective-permute-start | bytes 1572872 | tf_op jit(solution)/shard_map/ppermute | solution.py:465
  291.9 35.2 %collective-permute-start.16 = (bf16[4,128,512]{2,1,0:T(8,128)(2,1)}, bf16[4,128,512]{2,1,0:T(8,128)(2,1)}, u32[]{:S(2)}, u32[]{:S(2)}) collective-permute-start(bf16[4,128,512]{2,1,0:T(8,128)(2,1)} %dynamic-slice_bitcast_fusion.6), channel_id=1, source_target_pairs={{0,4},{4,0},{8,12},{12,8},{16,20},{20,16},{24,28},{28,24},{1,5},{5... | collective-permute-start | bytes 1572872 | tf_op jit(solution)/shard_map/ppermute | solution.py:465
  301.1 51.1 %collective-permute-start.12 = (bf16[4,128,512]{2,1,0:T(8,128)(2,1)}, bf16[4,128,512]{2,1,0:T(8,128)(2,1)}, u32[]{:S(2)}, u32[]{:S(2)}) collective-permute-start(bf16[4,128,512]{2,1,0:T(8,128)(2,1)} %dynamic-slice_bitcast_fusion.7), channel_id=1, source_target_pairs={{0,4},{4,0},{8,12},{12,8},{16,20},{20,16},{24,28},{28,24},{1,5},{5... | collective-permute-start | bytes 1572872 | tf_op jit(solution)/shard_map/ppermute | solution.py:465
  305.5 16.7 %collective-permute-start.40 = (bf16[88,1024]{1,0:T(8,128)(2,1)}, bf16[88,1024]{1,0:T(8,128)(2,1)S(1)}, u32[]{:S(2)}, u32[]{:S(2)}) collective-permute-start(bf16[88,1024]{1,0:T(8,128)(2,1)} %get-tuple-element.201), channel_id=1, source_target_pairs={{0,16},{1,20},{2,24},{3,28},{4,0},{5,4},{6,8},{7,12},{8,17},{9,21}... | collective-permute-start | bytes 540680 | tf_op jit(solution)/shard_map/ppermute | solution.py:562
  305.5 16.7 %collective-permute-start.41 = (bf16[88,1024]{1,0:T(8,128)(2,1)S(1)}, bf16[88,1024]{1,0:T(8,128)(2,1)}, u32[]{:S(2)}, u32[]{:S(2)}) collective-permute-start(bf16[88,1024]{1,0:T(8,128)(2,1)S(1)} %get-tuple-element.200), channel_id=1, source_target_pairs={{0,0},{1,4},{2,8},{3,12},{4,16},{5,20},{6,24},{7,28},{8,1},{9,5},{... | collective-permute-start | bytes 540680 | tf_op jit(solution)/shard_map/ppermute | solution.py:562
  322.2 9.1 %collective-permute-start.20 = (bf16[2,192,1024]{2,1,0:T(8,128)(2,1)S(1)}, bf16[2,192,1024]{2,1,0:T(8,128)(2,1)S(1)}, u32[]{:S(2)}, u32[]{:S(2)}) collective-permute-start(bf16[2,192,1024]{2,1,0:T(8,128)(2,1)S(1)} %fusion.33), channel_id=1, source_target_pairs={{0,1},{1,0},{2,3},{3,2},{4,5},{5,4},{6,7},{7,6},{8,9},{9,8},{10,11... | collective-permute-start | bytes 2359304 | tf_op jit(solution)/shard_map/ppermute | solution.py:465
  325.6 8.4 %collective-permute-start.34 = (bf16[64,1024]{1,0:T(8,128)(2,1)S(1)}, bf16[64,1024]{1,0:T(8,128)(2,1)S(1)}, u32[]{:S(2)}, u32[]{:S(2)}) collective-permute-start(bf16[64,1024]{1,0:T(8,128)(2,1)S(1)} %get-tuple-element.155), channel_id=1, source_target_pairs={{0,24},{4,28},{8,16},{12,20},{16,8},{20,12},{24,0},{28,4},{1,25},{... | collective-permute-start | bytes 393224 | tf_op jit(solution)/shard_map/ppermute | solution.py:465
  325.7 16.8 %collective-permute-start.33 = (bf16[64,1024]{1,0:T(8,128)(2,1)S(1)}, bf16[64,1024]{1,0:T(8,128)(2,1)S(1)}, u32[]{:S(2)}, u32[]{:S(2)}) collective-permute-start(bf16[64,1024]{1,0:T(8,128)(2,1)S(1)} %get-tuple-element.156), channel_id=1, source_target_pairs={{0,16},{4,20},{8,24},{12,28},{16,0},{20,4},{24,8},{28,12},{1,17},{... | collective-permute-start | bytes 393224 | tf_op jit(solution)/shard_map/ppermute | solution.py:465
  327.1 15.4 %collective-permute-start.32 = (bf16[64,1024]{1,0:T(8,128)(2,1)S(1)}, bf16[64,1024]{1,0:T(8,128)(2,1)S(1)}, u32[]{:S(2)}, u32[]{:S(2)}) collective-permute-start(bf16[64,1024]{1,0:T(8,128)(2,1)S(1)} %get-tuple-element.154), channel_id=1, source_target_pairs={{0,8},{4,12},{8,0},{12,4},{16,24},{20,28},{24,16},{28,20},{1,9},{5... | collective-permute-start | bytes 393224 | tf_op jit(solution)/shard_map/ppermute | solution.py:465
  331.7 16.0 %collective-permute-start.21 = (bf16[192,1024]{1,0:T(8,128)(2,1)S(1)}, bf16[192,1024]{1,0:T(8,128)(2,1)S(1)}, u32[]{:S(2)}, u32[]{:S(2)}) collective-permute-start(bf16[192,1024]{1,0:T(8,128)(2,1)S(1)} %fusion.73), channel_id=1, source_target_pairs={{0,2},{1,3},{2,0},{3,1},{4,6},{5,7},{6,4},{7,5},{8,10},{9,11},{10,... | collective-permute-start | bytes 1179656 | tf_op jit(solution)/shard_map/ppermute | solution.py:465
  334.0 65.8 %collective-permute-start.19 = (bf16[128,512]{1,0:T(8,128)(2,1)}, bf16[128,512]{1,0:T(8,128)(2,1)}, u32[]{:S(2)}, u32[]{:S(2)}) collective-permute-start(bf16[128,512]{1,0:T(8,128)(2,1)} %get-tuple-element.163), channel_id=1, source_target_pairs={{0,24},{4,28},{8,16},{12,20},{16,8},{20,12},{24,0},{28,4},{1,25},{... | collective-permute-start | bytes 393224 | tf_op jit(solution)/shard_map/ppermute | solution.py:465
  343.9 13.4 %collective-permute-start.35 = (bf16[152,1024]{1,0:T(8,128)(2,1)}, bf16[152,1024]{1,0:T(8,128)(2,1)}, u32[]{:S(2)}, u32[]{:S(2)}) collective-permute-start(bf16[152,1024]{1,0:T(8,128)(2,1)} %pad_maximum_fusion.21), channel_id=1, source_target_pairs={{0,0},{1,8},{2,16},{3,24},{4,1},{5,9},{6,17},{7,25},{8,2},{9,10},{... | collective-permute-start | bytes 933896 | tf_op jit(solution)/shard_map/ppermute | solution.py:562
  355.9 45.1 %collective-permute-start.18 = (bf16[128,512]{1,0:T(8,128)(2,1)}, bf16[128,512]{1,0:T(8,128)(2,1)S(1)}, u32[]{:S(2)}, u32[]{:S(2)}) collective-permute-start(bf16[128,512]{1,0:T(8,128)(2,1)} %get-tuple-element.164), channel_id=1, source_target_pairs={{0,16},{4,20},{8,24},{12,28},{16,0},{20,4},{24,8},{28,12},{1,17},{... | collective-permute-start | bytes 393224 | tf_op jit(solution)/shard_map/ppermute | solution.py:465
  367.8 20.0 %collective-permute-start.22 = (bf16[64,1024]{1,0:T(8,128)(2,1)S(1)}, bf16[64,1024]{1,0:T(8,128)(2,1)S(1)}, u32[]{:S(2)}, u32[]{:S(2)}) collective-permute-start(bf16[64,1024]{1,0:T(8,128)(2,1)S(1)} %get-tuple-element.197), channel_id=1, source_target_pairs={{0,0},{1,5},{2,11},{3,21},{4,1},{5,12},{6,22},{7,23},{8,6},{9,13},... | collective-permute-start | bytes 393224 | tf_op jit(solution)/shard_map/ppermute | solution.py:562
  369.9 19.7 %collective-permute-start.23 = (bf16[64,1024]{1,0:T(8,128)(2,1)S(1)}, bf16[64,1024]{1,0:T(8,128)(2,1)S(1)}, u32[]{:S(2)}, u32[]{:S(2)}) collective-permute-start(bf16[64,1024]{1,0:T(8,128)(2,1)S(1)} %get-tuple-element.196), channel_id=1, source_target_pairs={{0,0},{1,10},{2,11},{3,22},{4,6},{5,12},{6,13},{7,23},{8,1},{9,7},... | collective-permute-start | bytes 393224 | tf_op jit(solution)/shard_map/ppermute | solution.py:562
  370.5 22.7 %collective-permute-start.24 = (bf16[64,1024]{1,0:T(8,128)(2,1)S(1)}, bf16[64,1024]{1,0:T(8,128)(2,1)S(1)}, u32[]{:S(2)}, u32[]{:S(2)}) collective-permute-start(bf16[64,1024]{1,0:T(8,128)(2,1)S(1)} %get-tuple-element.195), channel_id=1, source_target_pairs={{0,5},{1,11},{2,21},{3,22},{4,0},{5,6},{6,12},{7,23},{8,1},{9,13},... | collective-permute-start | bytes 393224 | tf_op jit(solution)/shard_map/ppermute | solution.py:562
  387.8 13.9 %collective-permute-start.17 = (bf16[128,512]{1,0:T(8,128)(2,1)S(1)}, bf16[128,512]{1,0:T(8,128)(2,1)S(1)}, u32[]{:S(2)}, u32[]{:S(2)}) collective-permute-start(bf16[128,512]{1,0:T(8,128)(2,1)S(1)} %copy-done.58), channel_id=1, source_target_pairs={{0,8},{4,12},{8,0},{12,4},{16,24},{20,28},{24,16},{28,20},{1,9},{5... | collective-permute-start | bytes 393224 | tf_op jit(solution)/shard_map/ppermute | solution.py:465
  389.6 24.7 %collective-permute-start.61 = (bf16[2,2,4,288,128]{4,3,2,1,0:T(8,128)(2,1)}, bf16[2,2,4,288,128]{4,3,2,1,0:T(8,128)(2,1)}, u32[]{:S(2)}, u32[]{:S(2)}) collective-permute-start(bf16[2,2,4,288,128]{4,3,2,1,0:T(8,128)(2,1)} %dynamic-slice_bitcast_fusion.2), channel_id=1, source_target_pairs={{0,1},{1,0},{2,3},{3,2},{4,5},{5,4},{6,7},{7,6},{8,9},{9,8},{10,11... | collective-permute-start | bytes 3538952 | tf_op jit(solution)/shard_map/ppermute | solution.py:465
  399.6 16.8 %collective-permute-start.49 = (bf16[2,2,4,288,128]{4,3,2,1,0:T(8,128)(2,1)S(1)}, bf16[2,2,4,288,128]{4,3,2,1,0:T(8,128)(2,1)S(1)}, u32[]{:S(2)}, u32[]{:S(2)}) collective-permute-start(bf16[2,2,4,288,128]{4,3,2,1,0:T(8,128)(2,1)S(1)} %dynamic-slice_bitcast_fusion.3), channel_id=1, source_target_pairs={{0,1},{1,0},{2,3},{3,2},{4,5},{5,4},{6,7},{7,6},{8,9},{9,8},{10,11... | collective-permute-start | bytes 3538952 | tf_op jit(solution)/shard_map/ppermute | solution.py:465
  399.8 8.4 %collective-permute-start.15 = (bf16[128,512]{1,0:T(8,128)(2,1)S(1)}, bf16[128,512]{1,0:T(8,128)(2,1)S(1)}, u32[]{:S(2)}, u32[]{:S(2)}) collective-permute-start(bf16[128,512]{1,0:T(8,128)(2,1)S(1)} %get-tuple-element.160), channel_id=1, source_target_pairs={{0,24},{4,28},{8,16},{12,20},{16,8},{20,12},{24,0},{28,4},{1,25},{... | collective-permute-start | bytes 393224 | tf_op jit(solution)/shard_map/ppermute | solution.py:465
  401.0 13.0 %collective-permute-start.14 = (bf16[128,512]{1,0:T(8,128)(2,1)S(1)}, bf16[128,512]{1,0:T(8,128)(2,1)S(1)}, u32[]{:S(2)}, u32[]{:S(2)}) collective-permute-start(bf16[128,512]{1,0:T(8,128)(2,1)S(1)} %get-tuple-element.161), channel_id=1, source_target_pairs={{0,16},{4,20},{8,24},{12,28},{16,0},{20,4},{24,8},{28,12},{1,17},{... | collective-permute-start | bytes 393224 | tf_op jit(solution)/shard_map/ppermute | solution.py:465
  401.7 12.3 %collective-permute-start.13 = (bf16[128,512]{1,0:T(8,128)(2,1)S(1)}, bf16[128,512]{1,0:T(8,128)(2,1)S(1)}, u32[]{:S(2)}, u32[]{:S(2)}) collective-permute-start(bf16[128,512]{1,0:T(8,128)(2,1)S(1)} %get-tuple-element.159), channel_id=1, source_target_pairs={{0,8},{4,12},{8,0},{12,4},{16,24},{20,28},{24,16},{28,20},{1,9},{5... | collective-permute-start | bytes 393224 | tf_op jit(solution)/shard_map/ppermute | solution.py:465
  416.1 14.9 %collective-permute-start.62 = (bf16[2,4,288,128]{3,2,1,0:T(8,128)(2,1)S(1)}, bf16[2,4,288,128]{3,2,1,0:T(8,128)(2,1)S(1)}, u32[]{:S(2)}, u32[]{:S(2)}) collective-permute-start(bf16[2,4,288,128]{3,2,1,0:T(8,128)(2,1)S(1)} %fusion.44), channel_id=1, source_target_pairs={{0,4},{4,0},{8,12},{12,8},{16,20},{20,16},{24,28},{28,24},{1,5},{5... | collective-permute-start | bytes 1769480 | tf_op jit(solution)/shard_map/ppermute | solution.py:465
  416.8 15.3 %collective-permute-start.50 = (bf16[2,4,288,128]{3,2,1,0:T(8,128)(2,1)S(1)}, bf16[2,4,288,128]{3,2,1,0:T(8,128)(2,1)S(1)}, u32[]{:S(2)}, u32[]{:S(2)}) collective-permute-start(bf16[2,4,288,128]{3,2,1,0:T(8,128)(2,1)S(1)} %fusion.43), channel_id=1, source_target_pairs={{0,2},{1,3},{2,0},{3,1},{4,6},{5,7},{6,4},{7,5},{8,10},{9,11},{10,... | collective-permute-start | bytes 1769480 | tf_op jit(solution)/shard_map/ppermute | solution.py:465
  431.2 7.7 %collective-permute-start.63 = (bf16[4,288,128]{2,1,0:T(8,128)(2,1)S(1)}, bf16[4,288,128]{2,1,0:T(8,128)(2,1)S(1)}, u32[]{:S(2)}, u32[]{:S(2)}) collective-permute-start(bf16[4,288,128]{2,1,0:T(8,128)(2,1)S(1)} %fusion.97), channel_id=1, source_target_pairs={{0,2},{1,3},{2,0},{3,1},{4,6},{5,7},{6,4},{7,5},{8,10},{9,11},{10,... | collective-permute-start | bytes 884744 | tf_op jit(solution)/shard_map/ppermute | solution.py:465
  432.3 11.1 %collective-permute-start.51 = (bf16[4,288,128]{2,1,0:T(8,128)(2,1)S(1)}, bf16[4,288,128]{2,1,0:T(8,128)(2,1)S(1)}, u32[]{:S(2)}, u32[]{:S(2)}) collective-permute-start(bf16[4,288,128]{2,1,0:T(8,128)(2,1)S(1)} %fusion.96), channel_id=1, source_target_pairs={{0,4},{4,0},{8,12},{12,8},{16,20},{20,16},{24,28},{28,24},{1,5},{5... | collective-permute-start | bytes 884744 | tf_op jit(solution)/shard_map/ppermute | solution.py:465
  440.6 8.9 %collective-permute-start.65 = (bf16[288,128]{1,0:T(8,128)(2,1)S(1)}, bf16[288,128]{1,0:T(8,128)(2,1)S(1)}, u32[]{:S(2)}, u32[]{:S(2)}) collective-permute-start(bf16[288,128]{1,0:T(8,128)(2,1)S(1)} %get-tuple-element.175), channel_id=1, source_target_pairs={{0,16},{4,20},{8,24},{12,28},{16,0},{20,4},{24,8},{28,12},{1,17},{... | collective-permute-start | bytes 221192 | tf_op jit(solution)/shard_map/ppermute | solution.py:465
  440.6 8.9 %collective-permute-start.64 = (bf16[288,128]{1,0:T(8,128)(2,1)S(1)}, bf16[288,128]{1,0:T(8,128)(2,1)S(1)}, u32[]{:S(2)}, u32[]{:S(2)}) collective-permute-start(bf16[288,128]{1,0:T(8,128)(2,1)S(1)} %get-tuple-element.173), channel_id=1, source_target_pairs={{0,8},{4,12},{8,0},{12,4},{16,24},{20,28},{24,16},{28,20},{1,9},{5... | collective-permute-start | bytes 221192 | tf_op jit(solution)/shard_map/ppermute | solution.py:465
  443.6 7.7 %collective-permute-start.54 = (bf16[288,128]{1,0:T(8,128)(2,1)S(1)}, bf16[288,128]{1,0:T(8,128)(2,1)S(1)}, u32[]{:S(2)}, u32[]{:S(2)}) collective-permute-start(bf16[288,128]{1,0:T(8,128)(2,1)S(1)} %get-tuple-element.179), channel_id=1, source_target_pairs={{0,24},{4,28},{8,16},{12,20},{16,8},{20,12},{24,0},{28,4},{1,25},{... | collective-permute-start | bytes 221192 | tf_op jit(solution)/shard_map/ppermute | solution.py:465
  445.1 13.2 %collective-permute-start.53 = (bf16[288,128]{1,0:T(8,128)(2,1)S(1)}, bf16[288,128]{1,0:T(8,128)(2,1)S(1)}, u32[]{:S(2)}, u32[]{:S(2)}) collective-permute-start(bf16[288,128]{1,0:T(8,128)(2,1)S(1)} %get-tuple-element.180), channel_id=1, source_target_pairs={{0,16},{4,20},{8,24},{12,28},{16,0},{20,4},{24,8},{28,12},{1,17},{... | collective-permute-start | bytes 221192 | tf_op jit(solution)/shard_map/ppermute | solution.py:465
  445.5 12.9 %collective-permute-start.52 = (bf16[288,128]{1,0:T(8,128)(2,1)S(1)}, bf16[288,128]{1,0:T(8,128)(2,1)S(1)}, u32[]{:S(2)}, u32[]{:S(2)}) collective-permute-start(bf16[288,128]{1,0:T(8,128)(2,1)S(1)} %get-tuple-element.178), channel_id=1, source_target_pairs={{0,8},{4,12},{8,0},{12,4},{16,24},{20,28},{24,16},{28,20},{1,9},{5... | collective-permute-start | bytes 221192 | tf_op jit(solution)/shard_map/ppermute | solution.py:465
  449.5 9.3 %collective-permute-start.67 = (bf16[288,128]{1,0:T(8,128)(2,1)S(1)}, bf16[288,128]{1,0:T(8,128)(2,1)S(1)}, u32[]{:S(2)}, u32[]{:S(2)}) collective-permute-start(bf16[288,128]{1,0:T(8,128)(2,1)S(1)} %fusion.170), channel_id=1, source_target_pairs={{0,24},{4,28},{8,16},{12,20},{16,8},{20,12},{24,0},{28,4},{1,25},{... | collective-permute-start | bytes 221192 | tf_op jit(solution)/shard_map/ppermute | solution.py:465
  451.2 11.6 %collective-permute-start.68 = (bf16[288,128]{1,0:T(8,128)(2,1)S(1)}, bf16[288,128]{1,0:T(8,128)(2,1)S(1)}, u32[]{:S(2)}, u32[]{:S(2)}) collective-permute-start(bf16[288,128]{1,0:T(8,128)(2,1)S(1)} %fusion.170), channel_id=1, source_target_pairs={{0,16},{4,20},{8,24},{12,28},{16,0},{20,4},{24,8},{28,12},{1,17},{... | collective-permute-start | bytes 221192 | tf_op jit(solution)/shard_map/ppermute | solution.py:465
  451.2 11.6 %collective-permute-start.69 = (bf16[288,128]{1,0:T(8,128)(2,1)S(1)}, bf16[288,128]{1,0:T(8,128)(2,1)S(1)}, u32[]{:S(2)}, u32[]{:S(2)}) collective-permute-start(bf16[288,128]{1,0:T(8,128)(2,1)S(1)} %fusion.170), channel_id=1, source_target_pairs={{0,8},{4,12},{8,0},{12,4},{16,24},{20,28},{24,16},{28,20},{1,9},{5... | collective-permute-start | bytes 221192 | tf_op jit(solution)/shard_map/ppermute | solution.py:465
  458.9 6.8 %collective-permute-start.56 = (bf16[288,128]{1,0:T(8,128)(2,1)S(1)}, bf16[288,128]{1,0:T(8,128)(2,1)S(1)}, u32[]{:S(2)}, u32[]{:S(2)}) collective-permute-start(bf16[288,128]{1,0:T(8,128)(2,1)S(1)} %fusion.173), channel_id=1, source_target_pairs={{0,16},{4,20},{8,24},{12,28},{16,0},{20,4},{24,8},{28,12},{1,17},{... | collective-permute-start | bytes 221192 | tf_op jit(solution)/shard_map/ppermute | solution.py:465
  465.8 9.9 %collective-permute-start.58 = (bf16[4,288,128]{2,1,0:T(8,128)(2,1)S(1)}, bf16[4,288,128]{2,1,0:T(8,128)(2,1)S(1)}, u32[]{:S(2)}, u32[]{:S(2)}) collective-permute-start(bf16[4,288,128]{2,1,0:T(8,128)(2,1)S(1)} %pad_maximum_fusion.22), channel_id=1, source_target_pairs={{0,4},{4,0},{8,12},{12,8},{16,20},{20,16},{24,28},{28,24},{1,5},{5... | collective-permute-start | bytes 884744 | tf_op jit(solution)/shard_map/ppermute | solution.py:465
  469.9 13.9 %collective-permute-start.71 = (bf16[2,4,288,128]{3,2,1,0:T(8,128)(2,1)S(1)}, bf16[2,4,288,128]{3,2,1,0:T(8,128)(2,1)S(1)}, u32[]{:S(2)}, u32[]{:S(2)}) collective-permute-start(bf16[2,4,288,128]{3,2,1,0:T(8,128)(2,1)S(1)} %pad_maximum_fusion.16), channel_id=1, source_target_pairs={{0,4},{4,0},{8,12},{12,8},{16,20},{20,16},{24,28},{28,24},{1,5},{5... | collective-permute-start | bytes 1769480 | tf_op jit(solution)/shard_map/ppermute | solution.py:465
  475.9 9.9 %collective-permute-start.59 = (bf16[2,4,288,128]{3,2,1,0:T(8,128)(2,1)S(1)}, bf16[2,4,288,128]{3,2,1,0:T(8,128)(2,1)S(1)}, u32[]{:S(2)}, u32[]{:S(2)}) collective-permute-start(bf16[2,4,288,128]{3,2,1,0:T(8,128)(2,1)S(1)} %pad_maximum_fusion.15), channel_id=1, source_target_pairs={{0,2},{1,3},{2,0},{3,1},{4,6},{5,7},{6,4},{7,5},{8,10},{9,11},{10,... | collective-permute-start | bytes 1769480 | tf_op jit(solution)/shard_map/ppermute | solution.py:465
  487.1 15.0 %collective-permute-start.60 = (bf16[2,2,4,288,128]{4,3,2,1,0:T(8,128)(2,1)}, bf16[2,2,4,288,128]{4,3,2,1,0:T(8,128)(2,1)S(1)}, u32[]{:S(2)}, u32[]{:S(2)}) collective-permute-start(bf16[2,2,4,288,128]{4,3,2,1,0:T(8,128)(2,1)} %pad_maximum_fusion.6), channel_id=1, source_target_pairs={{0,1},{1,0},{2,3},{3,2},{4,5},{5,4},{6,7},{7,6},{8,9},{9,8},{10,11... | collective-permute-start | bytes 3538952 | tf_op jit(solution)/shard_map/ppermute | solution.py:465
  (118 other events, 880.3 us)
Sparse Core Ops, SparseCore 0:
  10.8 54.5 all-gather.5
  66.9 32.9 all-gather.3
